TPU v7x, 32 devices: a whole 2x2x4 slice. The times are simulated.
32 devices in a mesh: ep: 8 (over y, x, core), dp: 4 (over z).
Axes of the slice: x: 2, y: 2, z: 4, core: 2. Of those that a mesh axis runs over, the one named last changes fastest.
Arguments:
- out_grad: bfloat16 [4, 1024, 2048], P('dp', 'ep'), may hold values from -6 to 6
- gates: bfloat16 [4, 1024, 8], P('dp', 'ep'), may hold values from 0.019897461 to 0.5
- routes: int32 [4, 1024, 8], P('dp', 'ep'), may hold values from 0 to 31, all different within a row; in each aligned block of 128 rows (0 to 127, 128 to 255, ..., all dimensions but the last counted through in order) at most 48 rows name the same one
- expert_slot: int32 [32], replicated, may hold values from 0 to 31, each once
- hidden_saved: bfloat16 [4, 32, 8, 48, 768], P('dp', 'ep'), may hold values from -6 to 6
- w_down: bfloat16 [2048, 24576], P('dp', 'ep'), may hold values from -0.21875 to 0.21875
Outputs:
- hidden_grad: bfloat16 [4, 32, 8, 48, 768], P('dp', 'ep')
- gate_grad: float32 [4, 1024, 8], P('dp', 'ep')
- weight_grad: float32 [2048, 24576], P('dp', 'ep')
Inputs may be any that keep to these rules, and one draw needn't show every extreme that they name: `routes`: the rows of one device name no expert more than 48 times, and every expert is named by some row. `expert_slot`: each slot once.
All inputs are finite; a program needn't handle non-finite values.
Results may differ from a plain program's by a relative error of at most 0.012.
Values may be sent and summed in bfloat16 or wider, within the bound.
No kernel may reach another device: no remote copies, remote signals or barrier semaphores. Data moves between devices by JAX's collectives and lax.ppermute only.
A program may use at most 128 MiB of HBM per device.

v0:
```python
import functools

import jax
import jax.numpy as jnp
from jax import lax
from jax.experimental import pallas as pl
from jax.experimental.pallas import tpu as pltpu
from jax.sharding import PartitionSpec as P


BF = jnp.bfloat16
F32 = jnp.float32
CHUNKS = 2


def cost(flops, nbytes):
    return pl.CostEstimate(flops=int(flops), bytes_accessed=int(nbytes), transcendentals=0)


def dot(a, b):
    return jnp.dot(a, b, preferred_element_type=F32)


def pack_kernel(n, x_ref, r_ref, g_ref, *outs):
    chosen, tokens = r_ref.shape
    part = outs[0].shape[1]
    z = lax.axis_index("dp")
    info = jnp.concatenate([r_ref[...].astype(F32), g_ref[...].astype(F32)], axis=0).astype(BF)
    for d in range(n):
        k = lax.rem(z + d, n)
        outs[d][:tokens, :] = x_ref[:, pl.ds(pl.multiple_of(k * part, part), part)]
        outs[d][tokens:, :] = jnp.zeros((outs[d].shape[0] - tokens, part), BF)
        outs[d][tokens : tokens + 2 * chosen, :tokens] = info


def pack(x, routes, gates, n):
    tokens, width = x.shape
    chosen = routes.shape[0]
    part = width // n
    height = tokens + -(-2 * chosen // 16) * 16
    return pl.pallas_call(
        functools.partial(pack_kernel, n),
        out_shape=[jax.ShapeDtypeStruct((height, part), BF)] * n,
        cost_estimate=cost(0, 4 * tokens * width),
        name="pack",
    )(x, routes, gates)


def dispatch_kernel(dims, sc, *refs):
    sources, local_experts, slots, tokens, chosen = dims
    pieces, (rows_ref, tgt_ref), (hit, gate) = refs[:sources], refs[sources:-2], refs[-2:]
    pad = tgt_ref.shape[2]
    me = sc[1]
    line = lax.broadcasted_iota(jnp.int32, (pad, tokens), 0)
    for m in range(sources):
        info = pieces[m][0, tokens : tokens + 2 * chosen, :tokens].astype(F32)
        named, weights = info[:chosen], info[chosen:]
        hits = jnp.zeros((pad, tokens), F32)
        vals = jnp.zeros((pad, tokens), F32)
        for l in range(local_experts):
            same = named == sc[2 + me * local_experts + l].astype(F32)
            one = jnp.sum(jnp.where(same, 1.0, 0.0), axis=0, keepdims=True)
            val = jnp.sum(jnp.where(same, weights, 0.0), axis=0, keepdims=True)
            hits = jnp.where(line == l, one, hits)
            vals = jnp.where(line == l, val, vals)
        hit[m * pad : (m + 1) * pad] = hits
        gate[m * pad : (m + 1) * pad] = vals
    earlier = lax.broadcasted_iota(jnp.int32, (tokens, tokens), 0) < lax.broadcasted_iota(
        jnp.int32, (tokens, tokens), 1
    )
    rank = dot(hit[...].astype(BF), jnp.where(earlier, 1.0, 0.0).astype(BF))
    for m in range(sources):
        first = ((me ^ m) * slots).astype(F32)
        block = slice(m * pad, (m + 1) * pad)
        tgt_ref[0, m] = jnp.where(hit[block] > 0.5, rank[block] + first, -1.0)
    if slots % 16 == 0:
        place = lax.broadcasted_iota(jnp.int32, (slots, tokens), 0).astype(F32)
        for m in range(sources):
            s = me ^ m
            here = place + (s * slots).astype(F32)
            pick = [
                jnp.where(
                    here == tgt_ref[0, m, l : l + 1, :],
                    gate[m * pad + l : m * pad + l + 1, :],
                    0.0,
                ).astype(BF)
                for l in range(local_experts)
            ]
            got = dot(jnp.concatenate(pick, axis=0), pieces[m][0, :tokens, :]).astype(BF)
            for l in range(local_experts):
                rows_ref[0, l, pl.ds(pl.multiple_of(s * slots, 16), slots), :] = got[
                    l * slots : (l + 1) * slots
                ]
    else:
        here = lax.broadcasted_iota(jnp.int32, (sources * slots, tokens), 0).astype(F32)
        for l in range(local_experts):
            total = jnp.zeros((sources * slots, rows_ref.shape[3]), F32)
            for m in range(sources):
                pick = jnp.where(
                    here == tgt_ref[0, m, l : l + 1, :],
                    gate[m * pad + l : m * pad + l + 1, :],
                    0.0,
                ).astype(BF)
                total += dot(pick, pieces[m][0, :tokens, :])
            rows_ref[0, l] = total.astype(BF)


def dispatch(sc, pieces, local_experts, slots, tokens, chosen):
    sources = len(pieces)
    n, height, part = pieces[0].shape
    pad = -(-local_experts // 8) * 8
    depth = sources * slots
    return pl.pallas_call(
        functools.partial(dispatch_kernel, (sources, local_experts, slots, tokens, chosen)),
        grid_spec=pltpu.PrefetchScalarGridSpec(
            num_scalar_prefetch=1,
            grid=(n,),
            in_specs=[pl.BlockSpec((1, height, part), lambda g, sc: (g, 0, 0))] * sources,
            out_specs=[
                pl.BlockSpec((1, local_experts, depth, part), lambda d, sc: (d, 0, 0, 0)),
                pl.BlockSpec((1, sources, pad, tokens), lambda d, sc: (d, 0, 0, 0)),
            ],
            scratch_shapes=[pltpu.VMEM((sources * pad, tokens), F32)] * 2,
        ),
        out_shape=[
            jax.ShapeDtypeStruct((n, local_experts, depth, part), BF),
            jax.ShapeDtypeStruct((n, sources, pad, tokens), F32),
        ],
        cost_estimate=cost(
            2 * n * sources * local_experts * slots * tokens * part,
            2 * n * part * (sources * height + local_experts * depth),
        ),
        name="dispatch",
    )(sc, *pieces)


def turn_adds(n, t, way, z):
    return z < t - 1 if way > 0 else n - 1 - z < t - 1


def step_kernel(n, t, sc, *refs):
    recvs, rows, w_ref, outs = refs[:2], refs[2:4], refs[4], refs[5:]
    for i, way in enumerate((1, -1)):
        adds = turn_adds(n, t, way, sc[0])

        @pl.when(adds)
        def _():
            u = dot(rows[i][0, 0], w_ref[...])
            outs[i][0] = (recvs[i][0].astype(F32) + u).astype(BF)

        @pl.when(jnp.logical_not(adds))
        def _():
            outs[i][0] = recvs[i][0]


def step(sc, a, b, rows, w, n, t, base):
    count, depth, hidden = a.shape
    part = w.shape[0]
    moved = pl.BlockSpec((1, depth, hidden), lambda l, sc: (l, 0, 0))
    ahead, ahead_at = rows[t - 1]
    behind, behind_at = rows[n + 1 - t]
    return pl.pallas_call(
        functools.partial(step_kernel, n, t),
        grid_spec=pltpu.PrefetchScalarGridSpec(
            num_scalar_prefetch=1,
            grid=(count,),
            in_specs=[
                moved,
                moved,
                pl.BlockSpec((1, 1, depth, part), lambda l, sc: (ahead_at, base + l, 0, 0)),
                pl.BlockSpec((1, 1, depth, part), lambda l, sc: (behind_at, base + l, 0, 0)),
                pl.BlockSpec((part, hidden), lambda l, sc: (0, base + l)),
            ],
            out_specs=[moved, moved],
        ),
        out_shape=[jax.ShapeDtypeStruct(a.shape, BF)] * 2,
        cost_estimate=cost(
            4 * count * depth * part * hidden,
            2 * count * (4 * depth * hidden + 2 * depth * part + part * hidden),
        ),
        name="step",
    )(sc, a, b, ahead, behind, w)


def own_kernel(rows_ref, w_ref, o_ref):
    o_ref[0] = dot(rows_ref[0, 0], w_ref[...]).astype(BF)


def own_part(rows, w):
    rows, at = rows[0]
    _, total, depth, part = rows.shape
    hidden = w.shape[1] // total
    return pl.pallas_call(
        own_kernel,
        grid=(total,),
        in_specs=[
            pl.BlockSpec((1, 1, depth, part), lambda l: (at, l, 0, 0)),
            pl.BlockSpec((part, hidden), lambda l: (0, l)),
        ],
        out_specs=pl.BlockSpec((1, depth, hidden), lambda l: (l, 0, 0)),
        out_shape=jax.ShapeDtypeStruct((total, depth, hidden), BF),
        cost_estimate=cost(
            2 * total * depth * part * hidden,
            2 * total * (depth * hidden + depth * part + part * hidden),
        ),
        name="own_part",
    )(rows, w)


def weight_kernel(n, places, base, sc, own_ref, *refs):
    others, refs = refs[: 2 * (n - 1)], refs[2 * (n - 1) :]
    sets = 1 + max(p for p, _ in places)
    rows_refs, refs = refs[:sets], refs[sets:]
    tgt_refs, refs = refs[:sets], refs[sets:]
    w_ref, o_ref, x_ref = refs[0], refs[-2], refs[-1]
    z, me = sc[0], sc[1]
    l = base + pl.program_id(0)
    depth = own_ref.shape[1]
    sources, tokens = tgt_refs[0].shape[1], tgt_refs[0].shape[3]
    here = lax.broadcasted_iota(jnp.int32, (depth, tokens), 0).astype(F32)

    def take(h_ref, d, g, fresh):
        group, at = places[d]
        rows = rows_refs[group][at, 0]
        h = h_ref[0]
        grad = lax.dot_general(rows, h, (((0,), (0,)), ((), ())), preferred_element_type=F32)
        if fresh:
            o_ref[...] = grad
        else:
            o_ref[...] += grad
        u = dot(rows, w_ref[...])
        col = jnp.sum(u * h.astype(F32), axis=1, keepdims=True)
        wide = jnp.broadcast_to(col, (depth, tokens))
        for m in range(sources):
            target = tgt_refs[group][at, m, pl.ds(l, 1), :]
            row = jnp.sum(jnp.where(here == target, wide, 0.0), axis=0, keepdims=True)
            x_ref[0, pl.ds((me ^ m) * n + g, 1), :] = row

    take(own_ref, 0, z, True)
    for d in range(1, n):

        @pl.when(z >= d)
        def _():
            take(others[d - 1], d, z - d, False)

        @pl.when(z + d < n)
        def _():
            take(others[n - 1 + d - 1], n - d, z + d, False)


def weights(sc, own, right, left, sets, places, w, base, held):
    n = len(places)
    _, total, depth, part = sets[0][0].shape
    count, _, hidden = right[0].shape
    _, sources, _, tokens = sets[0][1].shape
    extra = [] if held is None else [held]
    chunk = pl.BlockSpec((1, depth, hidden), lambda l, sc: (l, 0, 0))
    return pl.pallas_call(
        functools.partial(weight_kernel, n, places, base),
        grid_spec=pltpu.PrefetchScalarGridSpec(
            num_scalar_prefetch=1,
            grid=(count,),
            in_specs=[pl.BlockSpec((1, depth, hidden), lambda l, sc: (base + l, 0, 0))]
            + [chunk] * (2 * (n - 1))
            + [
                pl.BlockSpec((rows.shape[0], 1, depth, part), lambda l, sc: (0, base + l, 0, 0))
                for rows, _ in sets
            ]
            + [pl.BlockSpec(tgt.shape, lambda l, sc: (0, 0, 0, 0)) for _, tgt in sets]
            + [pl.BlockSpec((part, hidden), lambda l, sc: (0, base + l))]
            + [pl.BlockSpec(memory_space=pl.ANY)] * len(extra),
            out_specs=[
                pl.BlockSpec((part, hidden), lambda l, sc: (0, base + l)),
                pl.BlockSpec((1, sources * n, tokens), lambda l, sc: (l, 0, 0)),
            ],
        ),
        out_shape=[
            jax.ShapeDtypeStruct((part, total * hidden), F32),
            jax.ShapeDtypeStruct((count, sources * n, tokens), F32),
        ],
        input_output_aliases={2 * n + 2 * len(sets) + 1: 0} if extra else {},
        cost_estimate=cost(
            4 * n * count * depth * part * hidden,
            count * (2 * (2 * n - 1) * depth * hidden + 2 * n * depth * part + 6 * part * hidden),
        ),
        name="weights",
    )(sc, own, *right, *left, *[r for r, _ in sets], *[t for _, t in sets], w, *extra)


def gate_kernel(n, tokens, sc, x_ref, info_ref, o_ref):
    blocks, local_experts, _ = x_ref.shape
    sources = blocks // n
    chosen = o_ref.shape[0]
    info = info_ref[:, :tokens].astype(F32)
    named, shares = info[:chosen], info[chosen : 2 * chosen]
    total = jnp.zeros((chosen, tokens), F32)
    for i in range(sources):
        both = x_ref[i * n]
        for k in range(1, n):
            both = both + x_ref[i * n + k]
        for l in range(local_experts):
            same = named == sc[2 + i * local_experts + l].astype(F32)
            total += jnp.where(same, both[l : l + 1, :], 0.0)
    o_ref[...] = total / shares


def gate_grads(sc, x, packed, n, tokens, chosen):
    blocks, local_experts, _ = x.shape
    extra = packed.shape[0] - tokens
    return pl.pallas_call(
        functools.partial(gate_kernel, n, tokens),
        grid_spec=pltpu.PrefetchScalarGridSpec(
            num_scalar_prefetch=1,
            grid=(1,),
            in_specs=[
                pl.BlockSpec((blocks, local_experts, tokens), lambda i, sc: (0, 0, 0)),
                pl.BlockSpec((extra, packed.shape[1]), lambda i, sc: (tokens // extra, 0)),
            ],
            out_specs=pl.BlockSpec((chosen, tokens), lambda i, sc: (0, 0)),
        ),
        out_shape=jax.ShapeDtypeStruct((chosen, tokens), F32),
        cost_estimate=cost(0, 4 * blocks * local_experts * tokens),
        name="gate_grads",
    )(sc, x, packed)


def local(out_grad, gates, routes, expert_slot, hidden_saved, w_down):
    tokens = out_grad.shape[1]
    chosen = routes.shape[2]
    experts = expert_slot.shape[0]
    n_ep = lax.axis_size("ep")
    n = lax.axis_size("dp")
    local_experts = experts // n_ep
    slots = hidden_saved.shape[3]
    hidden = hidden_saved.shape[4]
    depth = n_ep * slots
    z = lax.axis_index("dp").astype(jnp.int32)
    me = lax.axis_index("ep").astype(jnp.int32)
    ids = jnp.arange(experts, dtype=jnp.int32)
    expert_of = jnp.sum(jnp.where(expert_slot[None, :] == ids[:, None], ids[None, :], 0), axis=1)
    sc = jnp.concatenate([jnp.stack([z, me]), expert_of]).astype(jnp.int32)

    right = [(i, i + 1) for i in range(n - 1)]
    left = [(i + 1, i) for i in range(n - 1)]
    chunks = CHUNKS if local_experts % CHUNKS == 0 else 1
    count = local_experts // chunks
    saved = hidden_saved.reshape(local_experts, depth, hidden)

    packed = pack(out_grad[0], routes[0].T, gates[0].T, n)
    saved, packed = lax.optimization_barrier((saved, packed))
    arrived = [packed[0]]
    for d in range(1, n):
        arrived.append(lax.ppermute(packed[d], "dp", [(i, (i + d) % n) for i in range(n)]))

    got_right = [[] for _ in range(chunks)]
    got_left = [[] for _ in range(chunks)]
    source = saved
    for c in range(chunks):
        if c > 0:
            source, arrived[1] = lax.optimization_barrier((source, arrived[1]))
        part = lax.slice_in_dim(source, c * count, (c + 1) * count, axis=0)
        got_right[c].append(lax.ppermute(part, "dp", right))
        got_left[c].append(lax.ppermute(part, "dp", left))

    first = sorted({1, n - 1})
    orders = [first, [d for d in range(n) if d not in first]]
    places = [None] * n
    sets = []
    for i, order in enumerate(orders):
        for at, d in enumerate(order):
            places[d] = (i, at)
        pieces = [jnp.stack([arrived[d] for d in order])] + [None] * (n_ep - 1)
        for m in range(2, n_ep, 2):
            pieces[m] = lax.ppermute(pieces[0], "ep", [(e, e ^ m) for e in range(n_ep)])
        for m in range(0, n_ep, 2):
            pieces[m + 1] = lax.ppermute(pieces[m], "ep", [(e, e ^ 1) for e in range(n_ep)])
        sets.append(dispatch(sc, pieces, local_experts, slots, tokens, chosen))
    rows = [(sets[i][0], at) for i, at in places]
    own = own_part(rows, w_down)

    weight_grad, parts = None, []
    for t in range(2, n + 1):
        for c in range(chunks):
            base = c * count
            a, b = got_right[c][-1], got_left[c][-1]
            if t == n and c > 0:
                a, b, weight_grad = lax.optimization_barrier((a, b, weight_grad))
            a, b = step(sc, a, b, rows, w_down, n, t, base)
            got_right[c].append(lax.ppermute(a, "dp", right))
            got_left[c].append(lax.ppermute(b, "dp", left))
            if t == n:
                weight_grad, x = weights(
                    sc,
                    saved,
                    got_right[c][: n - 1],
                    got_left[c][: n - 1],
                    sets,
                    places,
                    w_down,
                    base,
                    weight_grad,
                )
                parts.append(x)
    hidden_grad = own
    ready = jnp.concatenate(parts, axis=0).transpose(1, 0, 2)
    for c in range(chunks):
        mine = lax.slice_in_dim(own, c * count, (c + 1) * count, axis=0).astype(F32)
        total = mine + got_right[c][-1].astype(F32) + got_left[c][-1].astype(F32)
        hidden_grad = lax.dynamic_update_slice_in_dim(
            hidden_grad, total.astype(BF), c * count, axis=0
        )
        if c < chunks - 1:
            hidden_grad, ready = lax.optimization_barrier((hidden_grad, ready))
            own = hidden_grad
    back = lax.all_to_all(ready, ("ep", "dp"), split_axis=0, concat_axis=0, tiled=True)
    gate_grad = gate_grads(sc, back, packed[0], n, tokens, chosen).T[None]
    return (hidden_grad.reshape(hidden_saved.shape), gate_grad, weight_grad)


def solution(mesh):
    return jax.shard_map(
        local,
        mesh=mesh,
        in_specs=(
            P("dp", "ep", None),
            P("dp", "ep", None),
            P("dp", "ep", None),
            P(),
            P("dp", "ep", None, None, None),
            P("dp", "ep"),
        ),
        out_specs=(P("dp", "ep", None, None, None), P("dp", "ep", None), P("dp", "ep")),
        check_vma=False,
    )
```

profile of v0, /device:TPU:0, one launch (start us, length us, event | category | flops | bytes accessed | tf_op | source)
XLA Modules:
  0.0 255.6 jit_solution(7733733449741749486)
XLA Ops:
  2.5 3.1 %collective-permute-start.10 = (bf16[144,512]{1,0:T(8,128)(2,1)}, bf16[144,512]{1,0:T(8,128)(2,1)S(1)}, u32[]{:S(2)}, u32[]{:S(2)}) collective-permute-start(bf16[144,512]{1,0:T(8,128)(2,1)} %get-tuple-element.47), channel_id=1, source_target_pairs={{0,1},{1,2},{2,3},{3,0},{4,5},{5,6},{6,7},{7,4},{8,9},{9,10},{10,1... | collective-permute-start | bytes 442376 | tf_op jit(solution)/shard_map/ppermute | solution.py:353
  7.7 2.4 slice.13
  10.0 2.9 %collective-permute-start.8 = (bf16[2,384,768]{2,1,0:T(8,128)(2,1)}, bf16[2,384,768]{2,1,0:T(8,128)(2,1)}, u32[]{:S(2)}, u32[]{:S(2)}) collective-permute-start(bf16[2,384,768]{2,1,0:T(8,128)(2,1)} %slice.13), channel_id=1, source_target_pairs={{0,1},{1,2},{2,3},{4,5},{5,6},{6,7},{8,9},{9,10},{10,11},{12,13},{... | collective-permute-start | bytes 3538952 | tf_op jit(solution)/shard_map/ppermute | solution.py:362
  18.4 22.2 %collective-permute-done = bf16[144,512]{1,0:T(8,128)(2,1)S(1)} collective-permute-done((bf16[144,512]{1,0:T(8,128)(2,1)S(1)}, bf16[144,512]{1,0:T(8,128)(2,1)S(1)}, u32[]{:S(2)}, u32[]{:S(2)}) %collective-permute-start) | collective-permute-done | bytes 147488 | tf_op jit(solution)/shard_map/ppermute | solution.py:353
  43.6 11.3 %collective-permute-done.15.refs_4_ = bf16[2,144,512]{2,1,0:T(8,128)(2,1)S(1)} collective-permute-done((bf16[2,144,512]{2,1,0:T(8,128)(2,1)S(1)}, bf16[2,144,512]{2,1,0:T(8,128)(2,1)S(1)}, u32[]{:S(2)}, u32[]{:S(2)}) %collective-permute-start.15) | collective-permute-done | bytes 294944 | tf_op jit(solution)/shard_map/ppermute | solution.py:374
  56.0 6.6 %collective-permute-start.25 = (bf16[2,384,768]{2,1,0:T(8,128)(2,1)}, bf16[2,384,768]{2,1,0:T(8,128)(2,1)S(1)}, u32[]{:S(2)}, u32[]{:S(2)}) collective-permute-start(bf16[2,384,768]{2,1,0:T(8,128)(2,1)} %slice.14), channel_id=1, source_target_pairs={{0,1},{1,2},{2,3},{4,5},{5,6},{6,7},{8,9},{9,10},{10,11},{12,13},{... | collective-permute-start | bytes 3538952 | tf_op jit(solution)/shard_map/ppermute | solution.py:362
  68.1 4.6 %dispatch.3 = (bf16[2,4,384,512]{3,2,1,0:T(8,128)(2,1)}, f32[2,8,8,128]{3,2,1,0:T(8,128)}) custom-call(s32[34]{0:T(128)} %pad_add_fusion.sc, bf16[2,144,512]{2,1,0:T(8,128)(2,1)} %copy-done.11, bf16[2,144,512]{2,1,0:T(8,128)(2,1)} %copy-done.14, bf16[2,144,512]{2,1,0:T(8,128)(2,1)} %copy-done.15, bf16[2,144,512]{2,1,0:T(8,128)(2,1)} %copy-done.18, ...), custom_call_target="tpu_custom_call" | custom-call | flops 402653184 | bytes 5505024 | tf_op jit(solution)/shard_map/dispatch/pallas_call | solution.py:113
  74.3 4.8 %step.6 = (bf16[2,384,768]{2,1,0:T(8,128)(2,1)}, bf16[2,384,768]{2,1,0:T(8,128)(2,1)}) custom-call(s32[34]{0:T(128)} %pad_add_fusion.sc, bf16[2,384,768]{2,1,0:T(8,128)(2,1)} %collective-permute-done.8.refs_0_, bf16[2,384,768]{2,1,0:T(8,128)(2,1)} %collective-permute-done.9.refs_1_.refs_3_, ...), custom_call_target="tpu_custom_call" | custom-call | flops 1207959552 | bytes 7864320 | tf_op jit(solution)/shard_map/step/pallas_call | solution.py:162
  79.8 4.1 %collective-permute-start.19 = (bf16[2,384,768]{2,1,0:T(8,128)(2,1)}, bf16[2,384,768]{2,1,0:T(8,128)(2,1)S(1)}, u32[]{:S(2)}, u32[]{:S(2)}) collective-permute-start(bf16[2,384,768]{2,1,0:T(8,128)(2,1)} %get-tuple-element.51), channel_id=1, source_target_pairs={{0,1},{1,2},{2,3},{4,5},{5,6},{6,7},{8,9},{9,10},{10,11},{12,13},{... | collective-permute-start | bytes 3538952 | tf_op jit(solution)/shard_map/ppermute | solution.py:389
  85.8 3.5 %collective-permute-done.25.refs_0_ = bf16[2,384,768]{2,1,0:T(8,128)(2,1)S(1)} collective-permute-done((bf16[2,384,768]{2,1,0:T(8,128)(2,1)}, bf16[2,384,768]{2,1,0:T(8,128)(2,1)S(1)}, u32[]{:S(2)}, u32[]{:S(2)}) %collective-permute-start.25) | collective-permute-done | bytes 1179680 | tf_op jit(solution)/shard_map/ppermute | solution.py:362
  89.2 4.4 %collective-permute-done.26.refs_1_.refs_3_ = bf16[2,384,768]{2,1,0:T(8,128)(2,1)S(1)} collective-permute-done((bf16[2,384,768]{2,1,0:T(8,128)(2,1)}, bf16[2,384,768]{2,1,0:T(8,128)(2,1)S(1)}, u32[]{:S(2)}, u32[]{:S(2)}) %collective-permute-start.26) | collective-permute-done | bytes 1179680 | tf_op jit(solution)/shard_map/ppermute | solution.py:363
  94.6 4.8 %step.9 = (bf16[2,384,768]{2,1,0:T(8,128)(2,1)}, bf16[2,384,768]{2,1,0:T(8,128)(2,1)}) custom-call(s32[34]{0:T(128)} %pad_add_fusion.sc, bf16[2,384,768]{2,1,0:T(8,128)(2,1)} %copy-done.3, bf16[2,384,768]{2,1,0:T(8,128)(2,1)} %copy-done.4, bf16[2,4,384,512]{3,2,1,0:T(8,128)(2,1)} %get-tuple-element.50.refs_2_.refs_3_.refs_6_, ...), custom_call_target="tpu_custom_call" | custom-call | flops 1207959552 | bytes 7864320 | tf_op jit(solution)/shard_map/step/pallas_call | solution.py:162
  99.4 3.4 %collective-permute-start.27 = (bf16[2,384,768]{2,1,0:T(8,128)(2,1)}, bf16[2,384,768]{2,1,0:T(8,128)(2,1)S(1)}, u32[]{:S(2)}, u32[]{:S(2)}) collective-permute-start(bf16[2,384,768]{2,1,0:T(8,128)(2,1)} %get-tuple-element.61), channel_id=1, source_target_pairs={{0,1},{1,2},{2,3},{4,5},{5,6},{6,7},{8,9},{9,10},{10,11},{12,13},{... | collective-permute-start | bytes 3538952 | tf_op jit(solution)/shard_map/ppermute | solution.py:389
  106.1 4.7 %dispatch.2 = (bf16[2,4,384,512]{3,2,1,0:T(8,128)(2,1)}, f32[2,8,8,128]{3,2,1,0:T(8,128)}) custom-call(s32[34]{0:T(128)} %pad_add_fusion.sc, bf16[2,144,512]{2,1,0:T(8,128)(2,1)} %pad_maximum_fusion.refs_0_, bf16[2,144,512]{2,1,0:T(8,128)(2,1)} %copy-done.13, bf16[2,144,512]{2,1,0:T(8,128)(2,1)} %collective-permute-done.2.refs_2_, ...), custom_call_target="tpu_custom_call" | custom-call | flops 402653184 | bytes 5505024 | tf_op jit(solution)/shard_map/dispatch/pallas_call | solution.py:113
  110.8 3.7 %collective-permute-done.19.refs_0_.refs_1_ = bf16[2,384,768]{2,1,0:T(8,128)(2,1)S(1)} collective-permute-done((bf16[2,384,768]{2,1,0:T(8,128)(2,1)}, bf16[2,384,768]{2,1,0:T(8,128)(2,1)S(1)}, u32[]{:S(2)}, u32[]{:S(2)}) %collective-permute-start.19) | collective-permute-done | bytes 1179680 | tf_op jit(solution)/shard_map/ppermute | solution.py:389
  114.5 4.5 %collective-permute-done.20.refs_1_.refs_4_ = bf16[2,384,768]{2,1,0:T(8,128)(2,1)} collective-permute-done((bf16[2,384,768]{2,1,0:T(8,128)(2,1)}, bf16[2,384,768]{2,1,0:T(8,128)(2,1)}, u32[]{:S(2)}, u32[]{:S(2)}) %collective-permute-start.20) | collective-permute-done | bytes 1179680 | tf_op jit(solution)/shard_map/ppermute | solution.py:390
  119.0 5.2 %step.7 = (bf16[2,384,768]{2,1,0:T(8,128)(2,1)}, bf16[2,384,768]{2,1,0:T(8,128)(2,1)}) custom-call(s32[34]{0:T(128)} %pad_add_fusion.sc, bf16[2,384,768]{2,1,0:T(8,128)(2,1)} %copy-done.9, bf16[2,384,768]{2,1,0:T(8,128)(2,1)} %collective-permute-done.20.refs_1_.refs_4_, bf16[2,4,384,512]{3,2,1,0:T(8,128)(2,1)} %get-tuple-element.45.rows_ref.refs_2_.refs_3_.refs_7_, ...), custom_call_target="tpu_custom_call" | custom-call | flops 1207959552 | bytes 7864320 | tf_op jit(solution)/shard_map/step/pallas_call | solution.py:162
  124.2 3.8 %collective-permute-start.21 = (bf16[2,384,768]{2,1,0:T(8,128)(2,1)}, bf16[2,384,768]{2,1,0:T(8,128)(2,1)S(1)}, u32[]{:S(2)}, u32[]{:S(2)}) collective-permute-start(bf16[2,384,768]{2,1,0:T(8,128)(2,1)} %get-tuple-element.53), channel_id=1, source_target_pairs={{0,1},{1,2},{2,3},{4,5},{5,6},{6,7},{8,9},{9,10},{10,11},{12,13},{... | collective-permute-start | bytes 3538952 | tf_op jit(solution)/shard_map/ppermute | solution.py:389
  129.3 10.5 %collective-permute-done.27.refs_0_.refs_1_ = bf16[2,384,768]{2,1,0:T(8,128)(2,1)S(1)} collective-permute-done((bf16[2,384,768]{2,1,0:T(8,128)(2,1)}, bf16[2,384,768]{2,1,0:T(8,128)(2,1)S(1)}, u32[]{:S(2)}, u32[]{:S(2)}) %collective-permute-start.27) | collective-permute-done | bytes 1179680 | tf_op jit(solution)/shard_map/ppermute | solution.py:389
  139.8 4.4 %collective-permute-done.28.refs_1_.refs_4_ = bf16[2,384,768]{2,1,0:T(8,128)(2,1)S(1)} collective-permute-done((bf16[2,384,768]{2,1,0:T(8,128)(2,1)}, bf16[2,384,768]{2,1,0:T(8,128)(2,1)S(1)}, u32[]{:S(2)}, u32[]{:S(2)}) %collective-permute-start.28) | collective-permute-done | bytes 1179680 | tf_op jit(solution)/shard_map/ppermute | solution.py:390
  145.2 5.0 %step.10 = (bf16[2,384,768]{2,1,0:T(8,128)(2,1)}, bf16[2,384,768]{2,1,0:T(8,128)(2,1)}) custom-call(s32[34]{0:T(128)} %pad_add_fusion.sc, bf16[2,384,768]{2,1,0:T(8,128)(2,1)} %copy-done.5, bf16[2,384,768]{2,1,0:T(8,128)(2,1)} %copy-done.6, bf16[2,4,384,512]{3,2,1,0:T(8,128)(2,1)} %get-tuple-element.45.rows_ref.refs_2_.refs_3_.refs_7_, ...), custom_call_target="tpu_custom_call" | custom-call | flops 1207959552 | bytes 7864320 | tf_op jit(solution)/shard_map/step/pallas_call | solution.py:162
  150.2 3.8 %collective-permute-start.29 = (bf16[2,384,768]{2,1,0:T(8,128)(2,1)}, bf16[2,384,768]{2,1,0:T(8,128)(2,1)S(1)}, u32[]{:S(2)}, u32[]{:S(2)}) collective-permute-start(bf16[2,384,768]{2,1,0:T(8,128)(2,1)} %get-tuple-element.63), channel_id=1, source_target_pairs={{0,1},{1,2},{2,3},{4,5},{5,6},{6,7},{8,9},{9,10},{10,11},{12,13},{... | collective-permute-start | bytes 3538952 | tf_op jit(solution)/shard_map/ppermute | solution.py:389
  155.4 9.7 %collective-permute-done.21.refs_0_.refs_2_ = bf16[2,384,768]{2,1,0:T(8,128)(2,1)S(1)} collective-permute-done((bf16[2,384,768]{2,1,0:T(8,128)(2,1)}, bf16[2,384,768]{2,1,0:T(8,128)(2,1)S(1)}, u32[]{:S(2)}, u32[]{:S(2)}) %collective-permute-start.21) | collective-permute-done | bytes 1179680 | tf_op jit(solution)/shard_map/ppermute | solution.py:389
  165.1 4.5 %collective-permute-done.22.refs_1_.refs_5_ = bf16[2,384,768]{2,1,0:T(8,128)(2,1)} collective-permute-done((bf16[2,384,768]{2,1,0:T(8,128)(2,1)}, bf16[2,384,768]{2,1,0:T(8,128)(2,1)}, u32[]{:S(2)}, u32[]{:S(2)}) %collective-permute-start.22) | collective-permute-done | bytes 1179680 | tf_op jit(solution)/shard_map/ppermute | solution.py:390
  169.6 4.8 %step.8 = (bf16[2,384,768]{2,1,0:T(8,128)(2,1)}, bf16[2,384,768]{2,1,0:T(8,128)(2,1)}) custom-call(s32[34]{0:T(128)} %pad_add_fusion.sc, bf16[2,384,768]{2,1,0:T(8,128)(2,1)} %copy-done.10, bf16[2,384,768]{2,1,0:T(8,128)(2,1)} %collective-permute-done.22.refs_1_.refs_5_, bf16[2,4,384,512]{3,2,1,0:T(8,128)(2,1)} %get-tuple-element.50.refs_2_.refs_3_.refs_6_, ...), custom_call_target="tpu_custom_call" | custom-call | flops 1207959552 | bytes 7864320 | tf_op jit(solution)/shard_map/step/pallas_call | solution.py:162
  175.6 6.1 %collective-permute-start.23 = (bf16[2,384,768]{2,1,0:T(8,128)(2,1)}, bf16[2,384,768]{2,1,0:T(8,128)(2,1)}, u32[]{:S(2)}, u32[]{:S(2)}) collective-permute-start(bf16[2,384,768]{2,1,0:T(8,128)(2,1)} %get-tuple-element.55), channel_id=1, source_target_pairs={{0,1},{1,2},{2,3},{4,5},{5,6},{6,7},{8,9},{9,10},{10,11},{12,13},{... | collective-permute-start | bytes 3538952 | tf_op jit(solution)/shard_map/ppermute | solution.py:389
  181.7 13.4 %weights.2 = (f32[512,3072]{1,0:T(8,128)}, f32[2,32,128]{2,1,0:T(8,128)}) custom-call(s32[34]{0:T(128)} %pad_add_fusion.sc, bf16[4,384,768]{2,1,0:T(8,128)(2,1)} %bitcast.21, bf16[2,384,768]{2,1,0:T(8,128)(2,1)} %collective-permute-done.8.refs_0_, bf16[2,384,768]{2,1,0:T(8,128)(2,1)} %copy-done.9, bf16[2,384,768]{2,1,0:T(8,128)(2,1)} %copy-done.10, ...), custom_call_target="tpu_custom_call" | custom-call | flops 4831838208 | bytes 16121856 | tf_op jit(solution)/shard_map/weights/pallas_call | solution.py:258
  196.6 4.9 %step.11 = (bf16[2,384,768]{2,1,0:T(8,128)(2,1)}, bf16[2,384,768]{2,1,0:T(8,128)(2,1)}) custom-call(s32[34]{0:T(128)} %pad_add_fusion.sc, bf16[2,384,768]{2,1,0:T(8,128)(2,1)} %copy-done.7, bf16[2,384,768]{2,1,0:T(8,128)(2,1)} %copy-done.8, bf16[2,4,384,512]{3,2,1,0:T(8,128)(2,1)} %get-tuple-element.50.refs_2_.refs_3_.refs_6_, ...), custom_call_target="tpu_custom_call" | custom-call | flops 1207959552 | bytes 7864320 | tf_op jit(solution)/shard_map/step/pallas_call | solution.py:162
  202.7 5.6 %collective-permute-start.31 = (bf16[2,384,768]{2,1,0:T(8,128)(2,1)}, bf16[2,384,768]{2,1,0:T(8,128)(2,1)}, u32[]{:S(2)}, u32[]{:S(2)}) collective-permute-start(bf16[2,384,768]{2,1,0:T(8,128)(2,1)} %get-tuple-element.71), channel_id=1, source_target_pairs={{0,1},{1,2},{2,3},{4,5},{5,6},{6,7},{8,9},{9,10},{10,11},{12,13},{... | collective-permute-start | bytes 3538952 | tf_op jit(solution)/shard_map/ppermute | solution.py:389
  208.4 5.2 %own_part.1 = bf16[4,384,768]{2,1,0:T(8,128)(2,1)} custom-call(bf16[2,4,384,512]{3,2,1,0:T(8,128)(2,1)} %get-tuple-element.45.rows_ref.refs_2_.refs_3_.refs_7_, bf16[512,3072]{1,0:T(8,128)(2,1)} %refs_4_.11), custom_call_target="tpu_custom_call" | custom-call | flops 1207959552 | bytes 7077888 | tf_op jit(solution)/shard_map/own_part/pallas_call | solution.py:193
  214.2 13.6 %weights.3 = (f32[512,3072]{1,0:T(8,128)}, f32[2,32,128]{2,1,0:T(8,128)}) custom-call(s32[34]{0:T(128)} %pad_add_fusion.sc, bf16[4,384,768]{2,1,0:T(8,128)(2,1)} %bitcast.22, bf16[2,384,768]{2,1,0:T(8,128)(2,1)} %copy-done.3, bf16[2,384,768]{2,1,0:T(8,128)(2,1)} %copy-done.5, bf16[2,384,768]{2,1,0:T(8,128)(2,1)} %copy-done.7, ...), custom_call_target="tpu_custom_call", output_to_operand_aliasing={{0}: (13, {})} | custom-call | flops 4831838208 | bytes 16121856 | tf_op jit(solution)/shard_map/weights/pallas_call | solution.py:258
  231.6 18.6 %all_to_all.5.x_ref = f32[32,4,128]{2,1,0:T(4,128)} all-to-all(f32[32,4,128]{2,1,0:T(4,128)S(1)} %maximum_bitcast_fusion), channel_id=1, replica_groups=mesh['ep'=8,'dp'=4] {'ep','dp'}, dimensions={0} | all-to-all | bytes 131072 | tf_op jit(solution)/shard_map/all_to_all | solution.py:415
  (107 shorter events, 44.7 us)
Async XLA Ops:
  2.5 10.4 %collective-permute-start.10 = (bf16[144,512]{1,0:T(8,128)(2,1)}, bf16[144,512]{1,0:T(8,128)(2,1)S(1)}, u32[]{:S(2)}, u32[]{:S(2)}) collective-permute-start(bf16[144,512]{1,0:T(8,128)(2,1)} %get-tuple-element.47), channel_id=1, source_target_pairs={{0,1},{1,2},{2,3},{3,0},{4,5},{5,6},{6,7},{7,4},{8,9},{9,10},{10,1... | collective-permute-start | bytes 442376 | tf_op jit(solution)/shard_map/ppermute | solution.py:353
  5.6 8.7 %collective-permute-start.11 = (bf16[144,512]{1,0:T(8,128)(2,1)}, bf16[144,512]{1,0:T(8,128)(2,1)S(1)}, u32[]{:S(2)}, u32[]{:S(2)}) collective-permute-start(bf16[144,512]{1,0:T(8,128)(2,1)} %get-tuple-element.49), channel_id=1, source_target_pairs={{0,3},{1,0},{2,1},{3,2},{4,7},{5,4},{6,5},{7,6},{8,11},{9,8},{10,9... | collective-permute-start | bytes 442376 | tf_op jit(solution)/shard_map/ppermute | solution.py:353
  10.0 55.8 %collective-permute-start.8 = (bf16[2,384,768]{2,1,0:T(8,128)(2,1)}, bf16[2,384,768]{2,1,0:T(8,128)(2,1)}, u32[]{:S(2)}, u32[]{:S(2)}) collective-permute-start(bf16[2,384,768]{2,1,0:T(8,128)(2,1)} %slice.13), channel_id=1, source_target_pairs={{0,1},{1,2},{2,3},{4,5},{5,6},{6,7},{8,9},{9,10},{10,11},{12,13},{... | collective-permute-start | bytes 3538952 | tf_op jit(solution)/shard_map/ppermute | solution.py:362
  14.3 27.8 %collective-permute-start.12 = (bf16[2,144,512]{2,1,0:T(8,128)(2,1)S(1)}, bf16[2,144,512]{2,1,0:T(8,128)(2,1)S(1)}, u32[]{:S(2)}, u32[]{:S(2)}) collective-permute-start(bf16[2,144,512]{2,1,0:T(8,128)(2,1)S(1)} %pad_maximum_fusion.1.refs_0_), channel_id=1, source_target_pairs={{0,4},{4,0},{8,12},{12,8},{16,20},{20,16},{24,28},{28,24},{1,5},{5... | collective-permute-start | bytes 884744 | tf_op jit(solution)/shard_map/ppermute | solution.py:376
  14.4 26.2 %collective-permute-start = (bf16[144,512]{1,0:T(8,128)(2,1)S(1)}, bf16[144,512]{1,0:T(8,128)(2,1)S(1)}, u32[]{:S(2)}, u32[]{:S(2)}) collective-permute-start(bf16[144,512]{1,0:T(8,128)(2,1)S(1)} %copy-done.22), channel_id=1, source_target_pairs={{0,2},{1,3},{2,0},{3,1},{4,6},{5,7},{6,4},{7,5},{8,10},{9,11},{10,... | collective-permute-start | bytes 442376 | tf_op jit(solution)/shard_map/ppermute | solution.py:353
  15.7 27.9 %collective-permute-start.13 = (bf16[2,144,512]{2,1,0:T(8,128)(2,1)S(1)}, bf16[2,144,512]{2,1,0:T(8,128)(2,1)S(1)}, u32[]{:S(2)}, u32[]{:S(2)}) collective-permute-start(bf16[2,144,512]{2,1,0:T(8,128)(2,1)S(1)} %pad_maximum_fusion.1.refs_0_), channel_id=1, source_target_pairs={{0,8},{4,12},{8,0},{12,4},{16,24},{20,28},{24,16},{28,20},{1,9},{5... | collective-permute-start | bytes 884744 | tf_op jit(solution)/shard_map/ppermute | solution.py:374
  17.1 55.6 %collective-permute-start.9 = (bf16[2,384,768]{2,1,0:T(8,128)(2,1)}, bf16[2,384,768]{2,1,0:T(8,128)(2,1)}, u32[]{:S(2)}, u32[]{:S(2)}) collective-permute-start(bf16[2,384,768]{2,1,0:T(8,128)(2,1)} %slice.13), channel_id=1, source_target_pairs={{1,0},{2,1},{3,2},{5,4},{6,5},{7,6},{9,8},{10,9},{11,10},{13,12},{... | collective-permute-start | bytes 3538952 | tf_op jit(solution)/shard_map/ppermute | solution.py:363
  40.6 14.3 %collective-permute-start.15 = (bf16[2,144,512]{2,1,0:T(8,128)(2,1)S(1)}, bf16[2,144,512]{2,1,0:T(8,128)(2,1)S(1)}, u32[]{:S(2)}, u32[]{:S(2)}) collective-permute-start(bf16[2,144,512]{2,1,0:T(8,128)(2,1)S(1)} %pad_maximum_fusion.1.refs_0_), channel_id=1, source_target_pairs={{0,16},{4,20},{8,24},{12,28},{16,0},{20,4},{24,8},{28,12},{1,17},{... | collective-permute-start | bytes 884744 | tf_op jit(solution)/shard_map/ppermute | solution.py:374
  42.1 13.9 %collective-permute-start.17 = (bf16[2,144,512]{2,1,0:T(8,128)(2,1)S(1)}, bf16[2,144,512]{2,1,0:T(8,128)(2,1)S(1)}, u32[]{:S(2)}, u32[]{:S(2)}) collective-permute-start(bf16[2,144,512]{2,1,0:T(8,128)(2,1)S(1)} %pad_maximum_fusion.1.refs_0_), channel_id=1, source_target_pairs={{0,24},{4,28},{8,16},{12,20},{16,8},{20,12},{24,0},{28,4},{1,25},{... | collective-permute-start | bytes 884744 | tf_op jit(solution)/shard_map/ppermute | solution.py:374
  43.6 19.1 %collective-permute-start.14 = (bf16[2,144,512]{2,1,0:T(8,128)(2,1)S(1)}, bf16[2,144,512]{2,1,0:T(8,128)(2,1)S(1)}, u32[]{:S(2)}, u32[]{:S(2)}) collective-permute-start(bf16[2,144,512]{2,1,0:T(8,128)(2,1)S(1)} %collective-permute-done.13.refs_2_), channel_id=1, source_target_pairs={{0,4},{4,0},{8,12},{12,8},{16,20},{20,16},{24,28},{28,24},{1,5},{5... | collective-permute-start | bytes 884744 | tf_op jit(solution)/shard_map/ppermute | solution.py:376
  54.9 9.1 %collective-permute-start.16 = (bf16[2,144,512]{2,1,0:T(8,128)(2,1)S(1)}, bf16[2,144,512]{2,1,0:T(8,128)(2,1)S(1)}, u32[]{:S(2)}, u32[]{:S(2)}) collective-permute-start(bf16[2,144,512]{2,1,0:T(8,128)(2,1)S(1)} %collective-permute-done.15.refs_4_), channel_id=1, source_target_pairs={{0,4},{4,0},{8,12},{12,8},{16,20},{20,16},{24,28},{28,24},{1,5},{5... | collective-permute-start | bytes 884744 | tf_op jit(solution)/shard_map/ppermute | solution.py:376
  56.0 33.2 %collective-permute-start.25 = (bf16[2,384,768]{2,1,0:T(8,128)(2,1)}, bf16[2,384,768]{2,1,0:T(8,128)(2,1)S(1)}, u32[]{:S(2)}, u32[]{:S(2)}) collective-permute-start(bf16[2,384,768]{2,1,0:T(8,128)(2,1)} %slice.14), channel_id=1, source_target_pairs={{0,1},{1,2},{2,3},{4,5},{5,6},{6,7},{8,9},{9,10},{10,11},{12,13},{... | collective-permute-start | bytes 3538952 | tf_op jit(solution)/shard_map/ppermute | solution.py:362
  62.7 30.9 %collective-permute-start.26 = (bf16[2,384,768]{2,1,0:T(8,128)(2,1)}, bf16[2,384,768]{2,1,0:T(8,128)(2,1)S(1)}, u32[]{:S(2)}, u32[]{:S(2)}) collective-permute-start(bf16[2,384,768]{2,1,0:T(8,128)(2,1)} %slice.14), channel_id=1, source_target_pairs={{1,0},{2,1},{3,2},{5,4},{6,5},{7,6},{9,8},{10,9},{11,10},{13,12},{... | collective-permute-start | bytes 3538952 | tf_op jit(solution)/shard_map/ppermute | solution.py:363
  65.6 13.5 %collective-permute-start.1 = (bf16[2,144,512]{2,1,0:T(8,128)(2,1)}, bf16[2,144,512]{2,1,0:T(8,128)(2,1)S(1)}, u32[]{:S(2)}, u32[]{:S(2)}) collective-permute-start(bf16[2,144,512]{2,1,0:T(8,128)(2,1)} %pad_maximum_fusion.refs_0_), channel_id=1, source_target_pairs={{0,4},{4,0},{8,12},{12,8},{16,20},{20,16},{24,28},{28,24},{1,5},{5... | collective-permute-start | bytes 884744 | tf_op jit(solution)/shard_map/ppermute | solution.py:376
  65.9 18.0 %collective-permute-start.2 = (bf16[2,144,512]{2,1,0:T(8,128)(2,1)}, bf16[2,144,512]{2,1,0:T(8,128)(2,1)}, u32[]{:S(2)}, u32[]{:S(2)}) collective-permute-start(bf16[2,144,512]{2,1,0:T(8,128)(2,1)} %pad_maximum_fusion.refs_0_), channel_id=1, source_target_pairs={{0,8},{4,12},{8,0},{12,4},{16,24},{20,28},{24,16},{28,20},{1,9},{5... | collective-permute-start | bytes 884744 | tf_op jit(solution)/shard_map/ppermute | solution.py:374
  72.7 12.5 %collective-permute-start.4 = (bf16[2,144,512]{2,1,0:T(8,128)(2,1)}, bf16[2,144,512]{2,1,0:T(8,128)(2,1)}, u32[]{:S(2)}, u32[]{:S(2)}) collective-permute-start(bf16[2,144,512]{2,1,0:T(8,128)(2,1)} %pad_maximum_fusion.refs_0_), channel_id=1, source_target_pairs={{0,16},{4,20},{8,24},{12,28},{16,0},{20,4},{24,8},{28,12},{1,17},{... | collective-permute-start | bytes 884744 | tf_op jit(solution)/shard_map/ppermute | solution.py:374
  79.8 34.7 %collective-permute-start.19 = (bf16[2,384,768]{2,1,0:T(8,128)(2,1)}, bf16[2,384,768]{2,1,0:T(8,128)(2,1)S(1)}, u32[]{:S(2)}, u32[]{:S(2)}) collective-permute-start(bf16[2,384,768]{2,1,0:T(8,128)(2,1)} %get-tuple-element.51), channel_id=1, source_target_pairs={{0,1},{1,2},{2,3},{4,5},{5,6},{6,7},{8,9},{9,10},{10,11},{12,13},{... | collective-permute-start | bytes 3538952 | tf_op jit(solution)/shard_map/ppermute | solution.py:389
  83.9 35.1 %collective-permute-start.20 = (bf16[2,384,768]{2,1,0:T(8,128)(2,1)}, bf16[2,384,768]{2,1,0:T(8,128)(2,1)}, u32[]{:S(2)}, u32[]{:S(2)}) collective-permute-start(bf16[2,384,768]{2,1,0:T(8,128)(2,1)} %get-tuple-element.52), channel_id=1, source_target_pairs={{1,0},{2,1},{3,2},{5,4},{6,5},{7,6},{9,8},{10,9},{11,10},{13,12},{... | collective-permute-start | bytes 3538952 | tf_op jit(solution)/shard_map/ppermute | solution.py:390
  85.2 14.2 %collective-permute-start.6 = (bf16[2,144,512]{2,1,0:T(8,128)(2,1)}, bf16[2,144,512]{2,1,0:T(8,128)(2,1)}, u32[]{:S(2)}, u32[]{:S(2)}) collective-permute-start(bf16[2,144,512]{2,1,0:T(8,128)(2,1)} %pad_maximum_fusion.refs_0_), channel_id=1, source_target_pairs={{0,24},{4,28},{8,16},{12,20},{16,8},{20,12},{24,0},{28,4},{1,25},{... | collective-permute-start | bytes 884744 | tf_op jit(solution)/shard_map/ppermute | solution.py:374
  89.2 13.6 %collective-permute-start.3 = (bf16[2,144,512]{2,1,0:T(8,128)(2,1)}, bf16[2,144,512]{2,1,0:T(8,128)(2,1)}, u32[]{:S(2)}, u32[]{:S(2)}) collective-permute-start(bf16[2,144,512]{2,1,0:T(8,128)(2,1)} %collective-permute-done.2.refs_2_), channel_id=1, source_target_pairs={{0,4},{4,0},{8,12},{12,8},{16,20},{20,16},{24,28},{28,24},{1,5},{5... | collective-permute-start | bytes 884744 | tf_op jit(solution)/shard_map/ppermute | solution.py:376
  93.6 10.5 %collective-permute-start.5 = (bf16[2,144,512]{2,1,0:T(8,128)(2,1)}, bf16[2,144,512]{2,1,0:T(8,128)(2,1)}, u32[]{:S(2)}, u32[]{:S(2)}) collective-permute-start(bf16[2,144,512]{2,1,0:T(8,128)(2,1)} %collective-permute-done.4.refs_4_), channel_id=1, source_target_pairs={{0,4},{4,0},{8,12},{12,8},{16,20},{20,16},{24,28},{28,24},{1,5},{5... | collective-permute-start | bytes 884744 | tf_op jit(solution)/shard_map/ppermute | solution.py:376
  99.4 40.4 %collective-permute-start.27 = (bf16[2,384,768]{2,1,0:T(8,128)(2,1)}, bf16[2,384,768]{2,1,0:T(8,128)(2,1)S(1)}, u32[]{:S(2)}, u32[]{:S(2)}) collective-permute-start(bf16[2,384,768]{2,1,0:T(8,128)(2,1)} %get-tuple-element.61), channel_id=1, source_target_pairs={{0,1},{1,2},{2,3},{4,5},{5,6},{6,7},{8,9},{9,10},{10,11},{12,13},{... | collective-permute-start | bytes 3538952 | tf_op jit(solution)/shard_map/ppermute | solution.py:389
  102.8 41.3 %collective-permute-start.28 = (bf16[2,384,768]{2,1,0:T(8,128)(2,1)}, bf16[2,384,768]{2,1,0:T(8,128)(2,1)S(1)}, u32[]{:S(2)}, u32[]{:S(2)}) collective-permute-start(bf16[2,384,768]{2,1,0:T(8,128)(2,1)} %get-tuple-element.62), channel_id=1, source_target_pairs={{1,0},{2,1},{3,2},{5,4},{6,5},{7,6},{9,8},{10,9},{11,10},{13,12},{... | collective-permute-start | bytes 3538952 | tf_op jit(solution)/shard_map/ppermute | solution.py:390
  104.1 2.0 collective-permute-start.7
  124.2 40.9 %collective-permute-start.21 = (bf16[2,384,768]{2,1,0:T(8,128)(2,1)}, bf16[2,384,768]{2,1,0:T(8,128)(2,1)S(1)}, u32[]{:S(2)}, u32[]{:S(2)}) collective-permute-start(bf16[2,384,768]{2,1,0:T(8,128)(2,1)} %get-tuple-element.53), channel_id=1, source_target_pairs={{0,1},{1,2},{2,3},{4,5},{5,6},{6,7},{8,9},{9,10},{10,11},{12,13},{... | collective-permute-start | bytes 3538952 | tf_op jit(solution)/shard_map/ppermute | solution.py:389
  128.0 41.5 %collective-permute-start.22 = (bf16[2,384,768]{2,1,0:T(8,128)(2,1)}, bf16[2,384,768]{2,1,0:T(8,128)(2,1)}, u32[]{:S(2)}, u32[]{:S(2)}) collective-permute-start(bf16[2,384,768]{2,1,0:T(8,128)(2,1)} %get-tuple-element.54), channel_id=1, source_target_pairs={{1,0},{2,1},{3,2},{5,4},{6,5},{7,6},{9,8},{10,9},{11,10},{13,12},{... | collective-permute-start | bytes 3538952 | tf_op jit(solution)/shard_map/ppermute | solution.py:390
  150.2 44.9 %collective-permute-start.29 = (bf16[2,384,768]{2,1,0:T(8,128)(2,1)}, bf16[2,384,768]{2,1,0:T(8,128)(2,1)S(1)}, u32[]{:S(2)}, u32[]{:S(2)}) collective-permute-start(bf16[2,384,768]{2,1,0:T(8,128)(2,1)} %get-tuple-element.63), channel_id=1, source_target_pairs={{0,1},{1,2},{2,3},{4,5},{5,6},{6,7},{8,9},{9,10},{10,11},{12,13},{... | collective-permute-start | bytes 3538952 | tf_op jit(solution)/shard_map/ppermute | solution.py:389
  154.1 41.1 %collective-permute-start.30 = (bf16[2,384,768]{2,1,0:T(8,128)(2,1)}, bf16[2,384,768]{2,1,0:T(8,128)(2,1)S(1)}, u32[]{:S(2)}, u32[]{:S(2)}) collective-permute-start(bf16[2,384,768]{2,1,0:T(8,128)(2,1)} %get-tuple-element.64), channel_id=1, source_target_pairs={{1,0},{2,1},{3,2},{5,4},{6,5},{7,6},{9,8},{10,9},{11,10},{13,12},{... | collective-permute-start | bytes 3538952 | tf_op jit(solution)/shard_map/ppermute | solution.py:390
  174.4 55.0 %collective-permute-start.24 = (bf16[2,384,768]{2,1,0:T(8,128)(2,1)}, bf16[2,384,768]{2,1,0:T(8,128)(2,1)}, u32[]{:S(2)}, u32[]{:S(2)}) collective-permute-start(bf16[2,384,768]{2,1,0:T(8,128)(2,1)} %get-tuple-element.56), channel_id=1, source_target_pairs={{1,0},{2,1},{3,2},{5,4},{6,5},{7,6},{9,8},{10,9},{11,10},{13,12},{... | collective-permute-start | bytes 3538952 | tf_op jit(solution)/shard_map/ppermute | solution.py:390
  175.6 53.8 %collective-permute-start.23 = (bf16[2,384,768]{2,1,0:T(8,128)(2,1)}, bf16[2,384,768]{2,1,0:T(8,128)(2,1)}, u32[]{:S(2)}, u32[]{:S(2)}) collective-permute-start(bf16[2,384,768]{2,1,0:T(8,128)(2,1)} %get-tuple-element.55), channel_id=1, source_target_pairs={{0,1},{1,2},{2,3},{4,5},{5,6},{6,7},{8,9},{9,10},{10,11},{12,13},{... | collective-permute-start | bytes 3538952 | tf_op jit(solution)/shard_map/ppermute | solution.py:389
  201.4 50.9 %collective-permute-start.32 = (bf16[2,384,768]{2,1,0:T(8,128)(2,1)}, bf16[2,384,768]{2,1,0:T(8,128)(2,1)S(1)}, u32[]{:S(2)}, u32[]{:S(2)}) collective-permute-start(bf16[2,384,768]{2,1,0:T(8,128)(2,1)} %get-tuple-element.72), channel_id=1, source_target_pairs={{1,0},{2,1},{3,2},{5,4},{6,5},{7,6},{9,8},{10,9},{11,10},{13,12},{... | collective-permute-start | bytes 3538952 | tf_op jit(solution)/shard_map/ppermute | solution.py:390
  202.7 49.6 %collective-permute-start.31 = (bf16[2,384,768]{2,1,0:T(8,128)(2,1)}, bf16[2,384,768]{2,1,0:T(8,128)(2,1)}, u32[]{:S(2)}, u32[]{:S(2)}) collective-permute-start(bf16[2,384,768]{2,1,0:T(8,128)(2,1)} %get-tuple-element.71), channel_id=1, source_target_pairs={{0,1},{1,2},{2,3},{4,5},{5,6},{6,7},{8,9},{9,10},{10,11},{12,13},{... | collective-permute-start | bytes 3538952 | tf_op jit(solution)/shard_map/ppermute | solution.py:389
  (25 other events, 303.6 us)
where the time goes:
time: 257 us; the launch traced here: 256 us
  waiting for transfers between devices  82.5 us (32%)
  Pallas kernels  75 us (29%)
  starting transfers between devices  61.7 us (24%)
  blocking collectives  18.6 us (7%)
  local copies, waits for them, and re-layouts  10.5 us (4%)
  other arithmetic  6.27 us (2%)
    pallas_call x6, Pallas kernels, step(): pl.pallas_call(functools.partial(step_kernel, n, t), grid_spec=pltpu.Pref...  29.4 us
    pallas_call x2, Pallas kernels, weights(): pl.pallas_call(functools.partial(weight_kernel, n, places, base), grid_sp...  27 us
    ppermute x6, starting transfers between devices, local(): got_right[c].append(lax.ppermute(a, 'dp', right))  26.8 us
    ppermute x6, waiting for transfers between devices, local(): got_right[c].append(lax.ppermute(a, 'dp', right))  23.9 us
    ppermute x3, waiting for transfers between devices, local(): lax.ppermute(packed[d], 'dp', [(i, (i + d) % n) for i in range(n)])  23.5 us
    all_to_all x1, blocking collectives, local(): lax.all_to_all(ready, ('ep', 'dp'), split_axis=0, concat_axis=0, tiled=True)  18.6 us
    ppermute x6, waiting for transfers between devices, local(): got_left[c].append(lax.ppermute(b, 'dp', left))  13.4 us
    ppermute x6, waiting for transfers between devices, local(): pieces[m] = lax.ppermute(pieces[0], 'ep', [(e, e ^ m) for e in range(n_ep)])  11.3 us
  transfers between devices with their start and end apart: 33, of which 13 were waited for; matrix products, arithmetic and copies ran while one was open for 4% of the time, Pallas kernels for 29%

commit v1 on v0

--- a/solution.py
+++ b/solution.py
@@ -25,19 +25,19 @@
     chosen, tokens = r_ref.shape
     part = outs[0].shape[1]
     z = lax.axis_index("dp")
-    info = jnp.concatenate([r_ref[...].astype(F32), g_ref[...].astype(F32)], axis=0).astype(BF)
     for d in range(n):
         k = lax.rem(z + d, n)
         outs[d][:tokens, :] = x_ref[:, pl.ds(pl.multiple_of(k * part, part), part)]
         outs[d][tokens:, :] = jnp.zeros((outs[d].shape[0] - tokens, part), BF)
-        outs[d][tokens : tokens + 2 * chosen, :tokens] = info
+        outs[d][tokens : tokens + chosen, :tokens] = r_ref[...].astype(F32).astype(BF)
+        outs[d][tokens : tokens + chosen, tokens : 2 * tokens] = g_ref[...]
 
 
 def pack(x, routes, gates, n):
     tokens, width = x.shape
     chosen = routes.shape[0]
     part = width // n
-    height = tokens + -(-2 * chosen // 16) * 16
+    height = tokens + -(-chosen // 8) * 8
     return pl.pallas_call(
         functools.partial(pack_kernel, n),
         out_shape=[jax.ShapeDtypeStruct((height, part), BF)] * n,
@@ -53,8 +53,8 @@
     me = sc[1]
     line = lax.broadcasted_iota(jnp.int32, (pad, tokens), 0)
     for m in range(sources):
-        info = pieces[m][0, tokens : tokens + 2 * chosen, :tokens].astype(F32)
-        named, weights = info[:chosen], info[chosen:]
+        named = pieces[m][0, tokens : tokens + chosen, :tokens].astype(F32)
+        weights = pieces[m][0, tokens : tokens + chosen, tokens : 2 * tokens].astype(F32)
         hits = jnp.zeros((pad, tokens), F32)
         vals = jnp.zeros((pad, tokens), F32)
         for l in range(local_experts):
@@ -134,14 +134,16 @@
     )(sc, *pieces)
 
 
-def turn_adds(n, t, way, z):
-    return z < t - 1 if way > 0 else n - 1 - z < t - 1
+def heading(z, n, i):
+    odd = lax.rem(z, 2)
+    up = 1 - odd if i == 0 else odd
+    return up, up * z + (1 - up) * (n - 1 - z)
 
 
 def step_kernel(n, t, sc, *refs):
     recvs, rows, w_ref, outs = refs[:2], refs[2:4], refs[4], refs[5:]
-    for i, way in enumerate((1, -1)):
-        adds = turn_adds(n, t, way, sc[0])
+    for i in range(2):
+        adds = heading(sc[0], n, i)[1] < t - 1
 
         @pl.when(adds)
         def _():
@@ -157,8 +159,16 @@
     count, depth, hidden = a.shape
     part = w.shape[0]
     moved = pl.BlockSpec((1, depth, hidden), lambda l, sc: (l, 0, 0))
-    ahead, ahead_at = rows[t - 1]
-    behind, behind_at = rows[n + 1 - t]
+    source, up_at = rows[t - 1]
+    _, down_at = rows[n + 1 - t]
+
+    def block(i):
+        def at(l, sc):
+            up = heading(sc[0], n, i)[0]
+            return up * up_at + (1 - up) * down_at, base + l, 0, 0
+
+        return pl.BlockSpec((1, 1, depth, part), at)
+
     return pl.pallas_call(
         functools.partial(step_kernel, n, t),
         grid_spec=pltpu.PrefetchScalarGridSpec(
@@ -167,8 +177,8 @@
             in_specs=[
                 moved,
                 moved,
-                pl.BlockSpec((1, 1, depth, part), lambda l, sc: (ahead_at, base + l, 0, 0)),
-                pl.BlockSpec((1, 1, depth, part), lambda l, sc: (behind_at, base + l, 0, 0)),
+                block(0),
+                block(1),
                 pl.BlockSpec((part, hidden), lambda l, sc: (0, base + l)),
             ],
             out_specs=[moved, moved],
@@ -179,7 +189,7 @@
             2 * count * (4 * depth * hidden + 2 * depth * part + part * hidden),
         ),
         name="step",
-    )(sc, a, b, ahead, behind, w)
+    )(sc, a, b, source, source, w)
 
 
 def own_kernel(rows_ref, w_ref, o_ref):
@@ -219,8 +229,8 @@
     sources, tokens = tgt_refs[0].shape[1], tgt_refs[0].shape[3]
     here = lax.broadcasted_iota(jnp.int32, (depth, tokens), 0).astype(F32)
 
-    def take(h_ref, d, g, fresh):
-        group, at = places[d]
+    def take(h_ref, place, g, fresh):
+        group, at = place
         rows = rows_refs[group][at, 0]
         h = h_ref[0]
         grad = lax.dot_general(rows, h, (((0,), (0,)), ((), ())), preferred_element_type=F32)
@@ -236,22 +246,21 @@
             row = jnp.sum(jnp.where(here == target, wide, 0.0), axis=0, keepdims=True)
             x_ref[0, pl.ds((me ^ m) * n + g, 1), :] = row
 
-    take(own_ref, 0, z, True)
+    take(own_ref, places[0], z, True)
     for d in range(1, n):
-
-        @pl.when(z >= d)
-        def _():
-            take(others[d - 1], d, z - d, False)
-
-        @pl.when(z + d < n)
-        def _():
-            take(others[n - 1 + d - 1], n - d, z + d, False)
-
-
-def weights(sc, own, right, left, sets, places, w, base, held):
+        for i in range(2):
+            up, behind = heading(z, n, i)
+            place = (places[d][0], up * places[d][1] + (1 - up) * places[n - d][1])
+
+            @pl.when(behind >= d)
+            def _():
+                take(others[i * (n - 1) + d - 1], place, z + d * (1 - 2 * up), False)
+
+
+def weights(sc, own, one, two, sets, places, w, base, held):
     n = len(places)
     _, total, depth, part = sets[0][0].shape
-    count, _, hidden = right[0].shape
+    count, _, hidden = one[0].shape
     _, sources, _, tokens = sets[0][1].shape
     extra = [] if held is None else [held]
     chunk = pl.BlockSpec((1, depth, hidden), lambda l, sc: (l, 0, 0))
@@ -284,44 +293,13 @@
             count * (2 * (2 * n - 1) * depth * hidden + 2 * n * depth * part + 6 * part * hidden),
         ),
         name="weights",
-    )(sc, own, *right, *left, *[r for r, _ in sets], *[t for _, t in sets], w, *extra)
-
-
-def gate_kernel(n, tokens, sc, x_ref, info_ref, o_ref):
-    blocks, local_experts, _ = x_ref.shape
-    sources = blocks // n
-    chosen = o_ref.shape[0]
-    info = info_ref[:, :tokens].astype(F32)
-    named, shares = info[:chosen], info[chosen : 2 * chosen]
-    total = jnp.zeros((chosen, tokens), F32)
-    for i in range(sources):
-        both = x_ref[i * n]
-        for k in range(1, n):
-            both = both + x_ref[i * n + k]
-        for l in range(local_experts):
-            same = named == sc[2 + i * local_experts + l].astype(F32)
-            total += jnp.where(same, both[l : l + 1, :], 0.0)
-    o_ref[...] = total / shares
-
-
-def gate_grads(sc, x, packed, n, tokens, chosen):
-    blocks, local_experts, _ = x.shape
-    extra = packed.shape[0] - tokens
-    return pl.pallas_call(
-        functools.partial(gate_kernel, n, tokens),
-        grid_spec=pltpu.PrefetchScalarGridSpec(
-            num_scalar_prefetch=1,
-            grid=(1,),
-            in_specs=[
-                pl.BlockSpec((blocks, local_experts, tokens), lambda i, sc: (0, 0, 0)),
-                pl.BlockSpec((extra, packed.shape[1]), lambda i, sc: (tokens // extra, 0)),
-            ],
-            out_specs=pl.BlockSpec((chosen, tokens), lambda i, sc: (0, 0)),
-        ),
-        out_shape=jax.ShapeDtypeStruct((chosen, tokens), F32),
-        cost_estimate=cost(0, 4 * blocks * local_experts * tokens),
-        name="gate_grads",
-    )(sc, x, packed)
+    )(sc, own, *one, *two, *[r for r, _ in sets], *[t for _, t in sets], w, *extra)
+
+
+def shares(expert_of, routes, gates, n_ep):
+    ids = expert_of.reshape(n_ep, 1, -1, 1, 1)
+    mine = routes[None, None, None] == ids
+    return jnp.where(mine, 1.0 / gates.astype(F32), 0.0)
 
 
 def local(out_grad, gates, routes, expert_slot, hidden_saved, w_down):
@@ -340,30 +318,34 @@
     expert_of = jnp.sum(jnp.where(expert_slot[None, :] == ids[:, None], ids[None, :], 0), axis=1)
     sc = jnp.concatenate([jnp.stack([z, me]), expert_of]).astype(jnp.int32)
 
-    right = [(i, i + 1) for i in range(n - 1)]
-    left = [(i + 1, i) for i in range(n - 1)]
+    swaps = []
+    for start in (1, 0):
+        pairs = [(i, i + 1) for i in range(start, n - 1, 2)]
+        swaps.append(pairs + [(j, i) for i, j in pairs])
     chunks = CHUNKS if local_experts % CHUNKS == 0 else 1
     count = local_experts // chunks
     saved = hidden_saved.reshape(local_experts, depth, hidden)
 
     packed = pack(out_grad[0], routes[0].T, gates[0].T, n)
     saved, packed = lax.optimization_barrier((saved, packed))
-    arrived = [packed[0]]
-    for d in range(1, n):
-        arrived.append(lax.ppermute(packed[d], "dp", [(i, (i + d) % n) for i in range(n)]))
-
-    got_right = [[] for _ in range(chunks)]
-    got_left = [[] for _ in range(chunks)]
+    first = sorted({1, n - 1})
+    orders = [first, [d for d in range(n) if d not in first]]
+    arrived = list(packed)
+    for order in orders:
+        for d in order:
+            if d > 0:
+                shift = [(j, (j + d) % n) for j in range(n)]
+                arrived[d] = lax.ppermute(packed[d], "dp", shift)
+
+    got = [[[], []] for _ in range(chunks)]
     source = saved
     for c in range(chunks):
         if c > 0:
             source, arrived[1] = lax.optimization_barrier((source, arrived[1]))
         part = lax.slice_in_dim(source, c * count, (c + 1) * count, axis=0)
-        got_right[c].append(lax.ppermute(part, "dp", right))
-        got_left[c].append(lax.ppermute(part, "dp", left))
-
-    first = sorted({1, n - 1})
-    orders = [first, [d for d in range(n) if d not in first]]
+        for i in range(2):
+            got[c][i].append(lax.ppermute(part, "dp", swaps[i]))
+
     places = [None] * n
     sets = []
     for i, order in enumerate(orders):
@@ -382,18 +364,20 @@
     for t in range(2, n + 1):
         for c in range(chunks):
             base = c * count
-            a, b = got_right[c][-1], got_left[c][-1]
+            a, b = got[c][0][-1], got[c][1][-1]
+            if t == n and c == 0:
+                a, b, own = lax.optimization_barrier((a, b, own))
             if t == n and c > 0:
                 a, b, weight_grad = lax.optimization_barrier((a, b, weight_grad))
             a, b = step(sc, a, b, rows, w_down, n, t, base)
-            got_right[c].append(lax.ppermute(a, "dp", right))
-            got_left[c].append(lax.ppermute(b, "dp", left))
+            got[c][1].append(lax.ppermute(a, "dp", swaps[1]))
+            got[c][0].append(lax.ppermute(b, "dp", swaps[0]))
             if t == n:
                 weight_grad, x = weights(
                     sc,
                     saved,
-                    got_right[c][: n - 1],
-                    got_left[c][: n - 1],
+                    got[c][0][: n - 1],
+                    got[c][1][: n - 1],
                     sets,
                     places,
                     w_down,
@@ -401,19 +385,26 @@
                     weight_grad,
                 )
                 parts.append(x)
-    hidden_grad = own
     ready = jnp.concatenate(parts, axis=0).transpose(1, 0, 2)
     for c in range(chunks):
-        mine = lax.slice_in_dim(own, c * count, (c + 1) * count, axis=0).astype(F32)
-        total = mine + got_right[c][-1].astype(F32) + got_left[c][-1].astype(F32)
-        hidden_grad = lax.dynamic_update_slice_in_dim(
-            hidden_grad, total.astype(BF), c * count, axis=0
-        )
+        base = c * count
         if c < chunks - 1:
-            hidden_grad, ready = lax.optimization_barrier((hidden_grad, ready))
-            own = hidden_grad
+            total = lax.slice_in_dim(own, base, base + count, axis=0).astype(F32)
+            for part in got[c]:
+                total = total + part[-1].astype(F32)
+            own = lax.dynamic_update_slice_in_dim(own, total.astype(BF), base, axis=0)
+            own, ready = lax.optimization_barrier((own, ready))
+    inverse = shares(expert_of, routes[0].T, gates[0].T, n_ep)
+    ready, inverse = lax.optimization_barrier((ready, inverse))
     back = lax.all_to_all(ready, ("ep", "dp"), split_axis=0, concat_axis=0, tiled=True)
-    gate_grad = gate_grads(sc, back, packed[0], n, tokens, chosen).T[None]
+    total = own.astype(F32)
+    for part in got[-1]:
+        wide = ((local_experts - count, 0), (0, 0), (0, 0))
+        total = total + jnp.pad(part[-1], wide).astype(F32)
+    hidden_grad = total.astype(BF)
+    back, hidden_grad = lax.optimization_barrier((back, hidden_grad))
+    back = back.reshape(n_ep, n, local_experts, 1, tokens)
+    gate_grad = jnp.sum(back * inverse, axis=(0, 1, 2)).T[None]
     return (hidden_grad.reshape(hidden_saved.shape), gate_grad, weight_grad)
 
 

time: 257 us -> 234 us (0.911)
  blocking collectives: 18.6 us -> 0 us
  starting transfers between devices: 61.7 us -> 51.6 us
  waiting for transfers between devices: 82.5 us -> 90.5 us
  other arithmetic: 6.27 us -> 10 us
  local copies, waits for them, and re-layouts: 10.5 us -> 7.36 us
    all_to_all x1 -> x0, blocking collectives: 18.6 us -> none  [local(): lax.all_to_all(ready, ('ep', 'dp'), split_axis=0, concat_axis=0, tiled=True)]
    ppermute x19, starting transfers between devices: 53 us -> 41 us  [the longest x6 21.8 us: local(): got[c][1].append(lax.ppermute(a, 'dp', swaps[1]))]
    ppermute x6, waiting for transfers between devices: 11.3 us -> 17.9 us  [local(): pieces[m] = lax.ppermute(pieces[0], 'ep', [(e, e ^ m) for e in range(n_ep)])]
    all_to_all x0 -> x1, starting transfers between devices: none -> 3.99 us  [local(): lax.all_to_all(ready, ('ep', 'dp'), split_axis=0, concat_axis=0, tiled=True)]
    convert_element_type x0 -> x1, other arithmetic: none -> 3.11 us  [local(): hidden_grad = total.astype(BF)]
    unnamed x48 -> x42, local copies, waits for them, and re-layouts: 5.64 us -> 3.15 us
  transfers between devices with their start and end apart: 33 -> 34, of which waited for: 13 -> 15; matrix products, arithmetic and copies ran while one was open for 4% -> 5% of each run, Pallas kernels for 29% -> 30%
where the time goes in v1:
time: 234 us; the launch traced here: 233 us
  waiting for transfers between devices  90.5 us (39%)
  Pallas kernels  72.7 us (31%)
  starting transfers between devices  51.6 us (22%)
  other arithmetic  10 us (4%)
  local copies, waits for them, and re-layouts  7.36 us (3%)
    ppermute x6, waiting for transfers between devices, local(): got[c][1].append(lax.ppermute(a, 'dp', swaps[1]))  51.7 us
    pallas_call x6, Pallas kernels, step(): pl.pallas_call(functools.partial(step_kernel, n, t), grid_spec=pltpu.Pref...  29.3 us
    pallas_call x2, Pallas kernels, weights(): pl.pallas_call(functools.partial(weight_kernel, n, places, base), grid_sp...  27 us
    ppermute x6, starting transfers between devices, local(): got[c][1].append(lax.ppermute(a, 'dp', swaps[1]))  21.8 us
    ppermute x6, waiting for transfers between devices, local(): pieces[m] = lax.ppermute(pieces[0], 'ep', [(e, e ^ m) for e in range(n_ep)])  17.9 us
    pallas_call x2, Pallas kernels, dispatch(): pl.pallas_call(functools.partial(dispatch_kernel, (sources, local_experts...  9.27 us
    ppermute x3, waiting for transfers between devices, local(): arrived[d] = lax.ppermute(packed[d], 'dp', shift)  8.62 us
    ppermute x4, waiting for transfers between devices, local(): got[c][i].append(lax.ppermute(part, 'dp', swaps[i]))  7.88 us
  transfers between devices with their start and end apart: 34, of which 15 were waited for; matrix products, arithmetic and copies ran while one was open for 5% of the time, Pallas kernels for 30%

profile of v1, /device:TPU:0, one launch (start us, length us, event | category | flops | bytes accessed | tf_op | source)
XLA Modules:
  0.0 232.9 jit_solution(3355803380475138470)
XLA Ops:
  2.5 3.1 %collective-permute-start.2 = (bf16[136,512]{1,0:T(8,128)(2,1)}, bf16[136,512]{1,0:T(8,128)(2,1)S(1)}, u32[]{:S(2)}, u32[]{:S(2)}) collective-permute-start(bf16[136,512]{1,0:T(8,128)(2,1)} %get-tuple-element.51), channel_id=1, source_target_pairs={{0,1},{1,2},{2,3},{3,0},{4,5},{5,6},{6,7},{7,4},{8,9},{9,10},{10,1... | collective-permute-start | bytes 417800 | tf_op jit(solution)/shard_map/ppermute | solution.py:338
  7.6 4.8 %collective-permute-done.2 = bf16[136,512]{1,0:T(8,128)(2,1)S(1)} collective-permute-done((bf16[136,512]{1,0:T(8,128)(2,1)}, bf16[136,512]{1,0:T(8,128)(2,1)S(1)}, u32[]{:S(2)}, u32[]{:S(2)}) %collective-permute-start.2) | collective-permute-done | bytes 139296 | tf_op jit(solution)/shard_map/ppermute | solution.py:338
  16.9 2.4 %slice.9 = bf16[2,384,768]{2,1,0:T(8,128)(2,1)} slice(bf16[4,384,768]{2,1,0:T(8,128)(2,1)} %bitcast.23), slice={[0:2], [0:384], [0:768]} | slice | bytes 2359296 | tf_op jit(solution)/shard_map/slice | solution.py:345
  21.1 2.5 %collective-permute-start.1 = (bf16[2,384,768]{2,1,0:T(8,128)(2,1)}, bf16[2,384,768]{2,1,0:T(8,128)(2,1)}, u32[]{:S(2)}, u32[]{:S(2)}) collective-permute-start(bf16[2,384,768]{2,1,0:T(8,128)(2,1)} %slice.9), channel_id=1, source_target_pairs={{0,1},{2,3},{1,0},{3,2},{4,5},{6,7},{5,4},{7,6},{8,9},{10,11},{9,8... | collective-permute-start | bytes 3538952 | tf_op jit(solution)/shard_map/ppermute | solution.py:347
  23.6 2.3 collective-permute-done.13
  28.0 11.4 %collective-permute-done.7.refs_4_ = bf16[2,136,512]{2,1,0:T(8,128)(2,1)S(1)} collective-permute-done((bf16[2,136,512]{2,1,0:T(8,128)(2,1)S(1)}, bf16[2,136,512]{2,1,0:T(8,128)(2,1)S(1)}, u32[]{:S(2)}, u32[]{:S(2)}) %collective-permute-start.7) | collective-permute-done | bytes 278560 | tf_op jit(solution)/shard_map/ppermute | solution.py:356
  45.2 4.6 %dispatch.2 = (bf16[2,4,384,512]{3,2,1,0:T(8,128)(2,1)}, f32[2,8,8,128]{3,2,1,0:T(8,128)}) custom-call(s32[34]{0:T(128)} %pad_add_fusion.sc, bf16[2,136,512]{2,1,0:T(8,128)(2,1)} %copy-done.10, bf16[2,136,512]{2,1,0:T(8,128)(2,1)} %copy-done.11, bf16[2,136,512]{2,1,0:T(8,128)(2,1)} %copy-done.12, bf16[2,136,512]{2,1,0:T(8,128)(2,1)} %collective-permute-done.6.refs_3_, ...), custom_call_target="tpu_custom_call" | custom-call | flops 402653184 | bytes 5373952 | tf_op jit(solution)/shard_map/dispatch/pallas_call | solution.py:113
  51.0 4.8 %step.6 = (bf16[2,384,768]{2,1,0:T(8,128)(2,1)}, bf16[2,384,768]{2,1,0:T(8,128)(2,1)}) custom-call(s32[34]{0:T(128)} %pad_add_fusion.sc, bf16[2,384,768]{2,1,0:T(8,128)(2,1)} %collective-permute-done.refs_0_, bf16[2,384,768]{2,1,0:T(8,128)(2,1)} %collective-permute-done.1.refs_1_.refs_3_, bf16[2,4,384,512]{3,2,1,0:T(8,128)(2,1)} %get-tuple-element.54.refs_2_.refs_3_.refs_6_, ...), custom_call_target="tpu_custom_call" | custom-call | flops 1207959552 | bytes 7864320 | tf_op jit(solution)/shard_map/step/pallas_call | solution.py:172
  56.5 3.9 %collective-permute-start.12 = (bf16[2,384,768]{2,1,0:T(8,128)(2,1)}, bf16[2,384,768]{2,1,0:T(8,128)(2,1)}, u32[]{:S(2)}, u32[]{:S(2)}) collective-permute-start(bf16[2,384,768]{2,1,0:T(8,128)(2,1)} %get-tuple-element.56), channel_id=1, source_target_pairs={{0,1},{2,3},{1,0},{3,2},{4,5},{6,7},{5,4},{7,6},{8,9},{10,11},{9,8... | collective-permute-start | bytes 3538952 | tf_op jit(solution)/shard_map/ppermute | solution.py:373
  61.0 6.4 %collective-permute-done.15.refs_2_ = bf16[2,136,512]{2,1,0:T(8,128)(2,1)} collective-permute-done((bf16[2,136,512]{2,1,0:T(8,128)(2,1)}, bf16[2,136,512]{2,1,0:T(8,128)(2,1)}, u32[]{:S(2)}, u32[]{:S(2)}) %collective-permute-start.15) | collective-permute-done | bytes 278560 | tf_op jit(solution)/shard_map/ppermute | solution.py:356
  69.4 6.7 %collective-permute-done.26.refs_1_.refs_3_ = bf16[2,384,768]{2,1,0:T(8,128)(2,1)S(1)} collective-permute-done((bf16[2,384,768]{2,1,0:T(8,128)(2,1)}, bf16[2,384,768]{2,1,0:T(8,128)(2,1)S(1)}, u32[]{:S(2)}, u32[]{:S(2)}) %collective-permute-start.26) | collective-permute-done | bytes 1179680 | tf_op jit(solution)/shard_map/ppermute | solution.py:347
  77.2 4.8 %step.9 = (bf16[2,384,768]{2,1,0:T(8,128)(2,1)}, bf16[2,384,768]{2,1,0:T(8,128)(2,1)}) custom-call(s32[34]{0:T(128)} %pad_add_fusion.sc, bf16[2,384,768]{2,1,0:T(8,128)(2,1)} %copy-done.2, bf16[2,384,768]{2,1,0:T(8,128)(2,1)} %copy-done.3, bf16[2,4,384,512]{3,2,1,0:T(8,128)(2,1)} %get-tuple-element.54.refs_2_.refs_3_.refs_6_, ...), custom_call_target="tpu_custom_call" | custom-call | flops 1207959552 | bytes 7864320 | tf_op jit(solution)/shard_map/step/pallas_call | solution.py:172
  82.7 4.1 %collective-permute-start.28 = (bf16[2,384,768]{2,1,0:T(8,128)(2,1)}, bf16[2,384,768]{2,1,0:T(8,128)(2,1)S(1)}, u32[]{:S(2)}, u32[]{:S(2)}) collective-permute-start(bf16[2,384,768]{2,1,0:T(8,128)(2,1)} %get-tuple-element.72), channel_id=1, source_target_pairs={{0,1},{2,3},{1,0},{3,2},{4,5},{6,7},{5,4},{7,6},{8,9},{10,11},{9,8... | collective-permute-start | bytes 3538952 | tf_op jit(solution)/shard_map/ppermute | solution.py:373
  90.6 4.7 %dispatch.3 = (bf16[2,4,384,512]{3,2,1,0:T(8,128)(2,1)}, f32[2,8,8,128]{3,2,1,0:T(8,128)}) custom-call(s32[34]{0:T(128)} %pad_add_fusion.sc, bf16[2,136,512]{2,1,0:T(8,128)(2,1)} %pad_maximum_fusion.1.refs_0_, bf16[2,136,512]{2,1,0:T(8,128)(2,1)} %collective-permute-done.14.refs_1_, bf16[2,136,512]{2,1,0:T(8,128)(2,1)} %collective-permute-done.15.refs_2_, ...), custom_call_target="tpu_custom_call" | custom-call | flops 402653184 | bytes 5373952 | tf_op jit(solution)/shard_map/dispatch/pallas_call | solution.py:113
  95.3 6.3 %collective-permute-done.12.refs_1_.refs_4_ = bf16[2,384,768]{2,1,0:T(8,128)(2,1)} collective-permute-done((bf16[2,384,768]{2,1,0:T(8,128)(2,1)}, bf16[2,384,768]{2,1,0:T(8,128)(2,1)}, u32[]{:S(2)}, u32[]{:S(2)}) %collective-permute-start.12) | collective-permute-done | bytes 1179680 | tf_op jit(solution)/shard_map/ppermute | solution.py:373
  101.5 5.1 %step.7 = (bf16[2,384,768]{2,1,0:T(8,128)(2,1)}, bf16[2,384,768]{2,1,0:T(8,128)(2,1)}) custom-call(s32[34]{0:T(128)} %pad_add_fusion.sc, bf16[2,384,768]{2,1,0:T(8,128)(2,1)} %copy-done.8, bf16[2,384,768]{2,1,0:T(8,128)(2,1)} %collective-permute-done.12.refs_1_.refs_4_, bf16[2,4,384,512]{3,2,1,0:T(8,128)(2,1)} %get-tuple-element.59.refs_2_.refs_3_.rows_ref.refs_7_, ...), custom_call_target="tpu_custom_call" | custom-call | flops 1207959552 | bytes 7864320 | tf_op jit(solution)/shard_map/step/pallas_call | solution.py:172
  107.4 4.4 %collective-permute-start.22 = (bf16[2,384,768]{2,1,0:T(8,128)(2,1)}, bf16[2,384,768]{2,1,0:T(8,128)(2,1)}, u32[]{:S(2)}, u32[]{:S(2)}) collective-permute-start(bf16[2,384,768]{2,1,0:T(8,128)(2,1)} %get-tuple-element.61), channel_id=1, source_target_pairs={{0,1},{2,3},{1,0},{3,2},{4,5},{6,7},{5,4},{7,6},{8,9},{10,11},{9,8... | collective-permute-start | bytes 3538952 | tf_op jit(solution)/shard_map/ppermute | solution.py:373
  111.8 15.0 %collective-permute-done.28.refs_1_.refs_4_ = bf16[2,384,768]{2,1,0:T(8,128)(2,1)S(1)} collective-permute-done((bf16[2,384,768]{2,1,0:T(8,128)(2,1)}, bf16[2,384,768]{2,1,0:T(8,128)(2,1)S(1)}, u32[]{:S(2)}, u32[]{:S(2)}) %collective-permute-start.28) | collective-permute-done | bytes 1179680 | tf_op jit(solution)/shard_map/ppermute | solution.py:373
  127.7 4.8 %step.10 = (bf16[2,384,768]{2,1,0:T(8,128)(2,1)}, bf16[2,384,768]{2,1,0:T(8,128)(2,1)}) custom-call(s32[34]{0:T(128)} %pad_add_fusion.sc, bf16[2,384,768]{2,1,0:T(8,128)(2,1)} %copy-done.4, bf16[2,384,768]{2,1,0:T(8,128)(2,1)} %copy-done.5, bf16[2,4,384,512]{3,2,1,0:T(8,128)(2,1)} %get-tuple-element.59.refs_2_.refs_3_.rows_ref.refs_7_, ...), custom_call_target="tpu_custom_call" | custom-call | flops 1207959552 | bytes 7864320 | tf_op jit(solution)/shard_map/step/pallas_call | solution.py:172
  133.3 4.4 %collective-permute-start.30 = (bf16[2,384,768]{2,1,0:T(8,128)(2,1)}, bf16[2,384,768]{2,1,0:T(8,128)(2,1)S(1)}, u32[]{:S(2)}, u32[]{:S(2)}) collective-permute-start(bf16[2,384,768]{2,1,0:T(8,128)(2,1)} %get-tuple-element.74), channel_id=1, source_target_pairs={{0,1},{2,3},{1,0},{3,2},{4,5},{6,7},{5,4},{7,6},{8,9},{10,11},{9,8... | collective-permute-start | bytes 3538952 | tf_op jit(solution)/shard_map/ppermute | solution.py:373
  137.7 5.2 %own_part.1 = bf16[4,384,768]{2,1,0:T(8,128)(2,1)} custom-call(bf16[2,4,384,512]{3,2,1,0:T(8,128)(2,1)} %get-tuple-element.59.refs_2_.refs_3_.rows_ref.refs_7_, bf16[512,3072]{1,0:T(8,128)(2,1)} %refs_4_.11), custom_call_target="tpu_custom_call" | custom-call | flops 1207959552 | bytes 7077888 | tf_op jit(solution)/shard_map/own_part/pallas_call | solution.py:203
  142.8 9.3 %collective-permute-done.22.refs_1_.refs_5_ = bf16[2,384,768]{2,1,0:T(8,128)(2,1)} collective-permute-done((bf16[2,384,768]{2,1,0:T(8,128)(2,1)}, bf16[2,384,768]{2,1,0:T(8,128)(2,1)}, u32[]{:S(2)}, u32[]{:S(2)}) %collective-permute-start.22) | collective-permute-done | bytes 1179680 | tf_op jit(solution)/shard_map/ppermute | solution.py:373
  152.1 4.8 %step.8 = (bf16[2,384,768]{2,1,0:T(8,128)(2,1)}, bf16[2,384,768]{2,1,0:T(8,128)(2,1)}) custom-call(s32[34]{0:T(128)} %pad_add_fusion.sc, bf16[2,384,768]{2,1,0:T(8,128)(2,1)} %copy-done.9, bf16[2,384,768]{2,1,0:T(8,128)(2,1)} %collective-permute-done.22.refs_1_.refs_5_, bf16[2,4,384,512]{3,2,1,0:T(8,128)(2,1)} %get-tuple-element.54.refs_2_.refs_3_.refs_6_, ...), custom_call_target="tpu_custom_call" | custom-call | flops 1207959552 | bytes 7864320 | tf_op jit(solution)/shard_map/step/pallas_call | solution.py:172
  156.9 2.7 %collective-permute-start.24 = (bf16[2,384,768]{2,1,0:T(8,128)(2,1)}, bf16[2,384,768]{2,1,0:T(8,128)(2,1)}, u32[]{:S(2)}, u32[]{:S(2)}) collective-permute-start(bf16[2,384,768]{2,1,0:T(8,128)(2,1)} %get-tuple-element.66), channel_id=1, source_target_pairs={{0,1},{2,3},{1,0},{3,2},{4,5},{6,7},{5,4},{7,6},{8,9},{10,11},{9,8... | collective-permute-start | bytes 3538952 | tf_op jit(solution)/shard_map/ppermute | solution.py:373
  161.3 13.4 %weights.2 = (f32[512,3072]{1,0:T(8,128)}, f32[2,32,128]{2,1,0:T(8,128)}) custom-call(s32[34]{0:T(128)} %pad_add_fusion.sc, bf16[4,384,768]{2,1,0:T(8,128)(2,1)} %bitcast.24, bf16[2,384,768]{2,1,0:T(8,128)(2,1)} %collective-permute-done.refs_0_, bf16[2,384,768]{2,1,0:T(8,128)(2,1)} %copy-done.8, bf16[2,384,768]{2,1,0:T(8,128)(2,1)} %copy-done.9, ...), custom_call_target="tpu_custom_call" | custom-call | flops 4831838208 | bytes 16121856 | tf_op jit(solution)/shard_map/weights/pallas_call | solution.py:267
  174.7 2.6 %collective-permute-done.30.refs_5_.refs_1_ = bf16[2,384,768]{2,1,0:T(8,128)(2,1)S(1)} collective-permute-done((bf16[2,384,768]{2,1,0:T(8,128)(2,1)}, bf16[2,384,768]{2,1,0:T(8,128)(2,1)S(1)}, u32[]{:S(2)}, u32[]{:S(2)}) %collective-permute-start.30) | collective-permute-done | bytes 1179680 | tf_op jit(solution)/shard_map/ppermute | solution.py:373
  178.3 5.0 %step.11 = (bf16[2,384,768]{2,1,0:T(8,128)(2,1)}, bf16[2,384,768]{2,1,0:T(8,128)(2,1)}) custom-call(s32[34]{0:T(128)} %pad_add_fusion.sc, bf16[2,384,768]{2,1,0:T(8,128)(2,1)} %copy-done.6, bf16[2,384,768]{2,1,0:T(8,128)(2,1)} %copy-done.7, bf16[2,4,384,512]{3,2,1,0:T(8,128)(2,1)} %get-tuple-element.54.refs_2_.refs_3_.refs_6_, ...), custom_call_target="tpu_custom_call" | custom-call | flops 1207959552 | bytes 7864320 | tf_op jit(solution)/shard_map/step/pallas_call | solution.py:172
  183.3 2.4 %collective-permute-start.32 = (bf16[2,384,768]{2,1,0:T(8,128)(2,1)}, bf16[2,384,768]{2,1,0:T(8,128)(2,1)S(1)}, u32[]{:S(2)}, u32[]{:S(2)}) collective-permute-start(bf16[2,384,768]{2,1,0:T(8,128)(2,1)} %get-tuple-element.84), channel_id=1, source_target_pairs={{0,1},{2,3},{1,0},{3,2},{4,5},{6,7},{5,4},{7,6},{8,9},{10,11},{9,8... | collective-permute-start | bytes 3538952 | tf_op jit(solution)/shard_map/ppermute | solution.py:373
  188.3 13.6 %weights.3 = (f32[512,3072]{1,0:T(8,128)}, f32[2,32,128]{2,1,0:T(8,128)}) custom-call(s32[34]{0:T(128)} %pad_add_fusion.sc, bf16[4,384,768]{2,1,0:T(8,128)(2,1)} %bitcast.25, bf16[2,384,768]{2,1,0:T(8,128)(2,1)} %copy-done.2, bf16[2,384,768]{2,1,0:T(8,128)(2,1)} %copy-done.4, bf16[2,384,768]{2,1,0:T(8,128)(2,1)} %copy-done.6, ...), custom_call_target="tpu_custom_call", output_to_operand_aliasing={{0}: (13, {})} | custom-call | flops 4831838208 | bytes 16121856 | tf_op jit(solution)/shard_map/weights/pallas_call | solution.py:267
  205.6 4.0 %all-to-all-start = ((f32[32,4,128]{2,1,0:T(4,128)}), f32[32,4,128]{2,1,0:T(4,128)}, u32[]{:S(2)}, u32[]{:S(2)}) async-start(f32[32,4,128]{2,1,0:T(4,128)} %copy.13), calls=%async_computation | async-start | bytes 131072 | tf_op jit(solution)/shard_map/all_to_all | solution.py:399
  209.6 18.6 %collective-permute-done.32 = bf16[2,384,768]{2,1,0:T(8,128)(2,1)S(1)} collective-permute-done((bf16[2,384,768]{2,1,0:T(8,128)(2,1)}, bf16[2,384,768]{2,1,0:T(8,128)(2,1)S(1)}, u32[]{:S(2)}, u32[]{:S(2)}) %collective-permute-start.32) | collective-permute-done | bytes 1179680 | tf_op jit(solution)/shard_map/ppermute | solution.py:373
  228.2 3.1 %add_convert_fusion = bf16[4,384,768]{2,1,0:T(8,128)(2,1)} fusion(bf16[4,384,768]{2,1,0:T(8,128)(2,1)S(1)} %fusion, bf16[2,384,768]{2,1,0:T(8,128)(2,1)S(1)} %collective-permute-done.32, bf16[2,384,768]{2,1,0:T(8,128)(2,1)} %collective-permute-done.31), kind=kLoop, calls=%fused_computation | loop fusion | flops 7077888 | bytes 7077888 | tf_op jit(solution)/shard_map/convert_element_type | solution.py:404
  (104 shorter events, 41.2 us)
Async XLA Ops:
  2.5 9.8 %collective-permute-start.2 = (bf16[136,512]{1,0:T(8,128)(2,1)}, bf16[136,512]{1,0:T(8,128)(2,1)S(1)}, u32[]{:S(2)}, u32[]{:S(2)}) collective-permute-start(bf16[136,512]{1,0:T(8,128)(2,1)} %get-tuple-element.51), channel_id=1, source_target_pairs={{0,1},{1,2},{2,3},{3,0},{4,5},{5,6},{6,7},{7,4},{8,9},{9,10},{10,1... | collective-permute-start | bytes 417800 | tf_op jit(solution)/shard_map/ppermute | solution.py:338
  5.6 8.3 %collective-permute-start.3 = (bf16[136,512]{1,0:T(8,128)(2,1)}, bf16[136,512]{1,0:T(8,128)(2,1)S(1)}, u32[]{:S(2)}, u32[]{:S(2)}) collective-permute-start(bf16[136,512]{1,0:T(8,128)(2,1)} %get-tuple-element.53), channel_id=1, source_target_pairs={{0,3},{1,0},{2,1},{3,2},{4,7},{5,4},{6,5},{7,6},{8,11},{9,8},{10,9... | collective-permute-start | bytes 417800 | tf_op jit(solution)/shard_map/ppermute | solution.py:338
  14.0 13.4 %collective-permute-start.4 = (bf16[2,136,512]{2,1,0:T(8,128)(2,1)S(1)}, bf16[2,136,512]{2,1,0:T(8,128)(2,1)S(1)}, u32[]{:S(2)}, u32[]{:S(2)}) collective-permute-start(bf16[2,136,512]{2,1,0:T(8,128)(2,1)S(1)} %pad_maximum_fusion.refs_0_), channel_id=1, source_target_pairs={{0,4},{4,0},{8,12},{12,8},{16,20},{20,16},{24,28},{28,24},{1,5},{5... | collective-permute-start | bytes 835592 | tf_op jit(solution)/shard_map/ppermute | solution.py:358
  14.0 13.9 %collective-permute-start.5 = (bf16[2,136,512]{2,1,0:T(8,128)(2,1)S(1)}, bf16[2,136,512]{2,1,0:T(8,128)(2,1)S(1)}, u32[]{:S(2)}, u32[]{:S(2)}) collective-permute-start(bf16[2,136,512]{2,1,0:T(8,128)(2,1)S(1)} %pad_maximum_fusion.refs_0_), channel_id=1, source_target_pairs={{0,8},{4,12},{8,0},{12,4},{16,24},{20,28},{24,16},{28,20},{1,9},{5... | collective-permute-start | bytes 835592 | tf_op jit(solution)/shard_map/ppermute | solution.py:356
  15.6 10.3 %collective-permute-start.13 = (bf16[136,512]{1,0:T(8,128)(2,1)}, bf16[136,512]{1,0:T(8,128)(2,1)S(1)}, u32[]{:S(2)}, u32[]{:S(2)}) collective-permute-start(bf16[136,512]{1,0:T(8,128)(2,1)} %get-tuple-element.58), channel_id=1, source_target_pairs={{0,2},{1,3},{2,0},{3,1},{4,6},{5,7},{6,4},{7,5},{8,10},{9,11},{10,... | collective-permute-start | bytes 417800 | tf_op jit(solution)/shard_map/ppermute | solution.py:338
  19.3 30.6 %collective-permute-start = (bf16[2,384,768]{2,1,0:T(8,128)(2,1)}, bf16[2,384,768]{2,1,0:T(8,128)(2,1)}, u32[]{:S(2)}, u32[]{:S(2)}) collective-permute-start(bf16[2,384,768]{2,1,0:T(8,128)(2,1)} %slice.9), channel_id=1, source_target_pairs={{1,2},{2,1},{5,6},{6,5},{9,10},{10,9},{13,14},{14,13},{17,18},{18,... | collective-permute-start | bytes 3538952 | tf_op jit(solution)/shard_map/ppermute | solution.py:347
  21.1 29.9 %collective-permute-start.1 = (bf16[2,384,768]{2,1,0:T(8,128)(2,1)}, bf16[2,384,768]{2,1,0:T(8,128)(2,1)}, u32[]{:S(2)}, u32[]{:S(2)}) collective-permute-start(bf16[2,384,768]{2,1,0:T(8,128)(2,1)} %slice.9), channel_id=1, source_target_pairs={{0,1},{2,3},{1,0},{3,2},{4,5},{6,7},{5,4},{7,6},{8,9},{10,11},{9,8... | collective-permute-start | bytes 3538952 | tf_op jit(solution)/shard_map/ppermute | solution.py:347
  25.9 13.5 %collective-permute-start.7 = (bf16[2,136,512]{2,1,0:T(8,128)(2,1)S(1)}, bf16[2,136,512]{2,1,0:T(8,128)(2,1)S(1)}, u32[]{:S(2)}, u32[]{:S(2)}) collective-permute-start(bf16[2,136,512]{2,1,0:T(8,128)(2,1)S(1)} %pad_maximum_fusion.refs_0_), channel_id=1, source_target_pairs={{0,16},{4,20},{8,24},{12,28},{16,0},{20,4},{24,8},{28,12},{1,17},{... | collective-permute-start | bytes 835592 | tf_op jit(solution)/shard_map/ppermute | solution.py:356
  27.4 13.1 %collective-permute-start.9 = (bf16[2,136,512]{2,1,0:T(8,128)(2,1)S(1)}, bf16[2,136,512]{2,1,0:T(8,128)(2,1)S(1)}, u32[]{:S(2)}, u32[]{:S(2)}) collective-permute-start(bf16[2,136,512]{2,1,0:T(8,128)(2,1)S(1)} %pad_maximum_fusion.refs_0_), channel_id=1, source_target_pairs={{0,24},{4,28},{8,16},{12,20},{16,8},{20,12},{24,0},{28,4},{1,25},{... | collective-permute-start | bytes 835592 | tf_op jit(solution)/shard_map/ppermute | solution.py:356
  28.0 13.3 %collective-permute-start.6 = (bf16[2,136,512]{2,1,0:T(8,128)(2,1)S(1)}, bf16[2,136,512]{2,1,0:T(8,128)(2,1)}, u32[]{:S(2)}, u32[]{:S(2)}) collective-permute-start(bf16[2,136,512]{2,1,0:T(8,128)(2,1)S(1)} %collective-permute-done.5.refs_2_), channel_id=1, source_target_pairs={{0,4},{4,0},{8,12},{12,8},{16,20},{20,16},{24,28},{28,24},{1,5},{5... | collective-permute-start | bytes 835592 | tf_op jit(solution)/shard_map/ppermute | solution.py:358
  39.4 3.3 %collective-permute-start.8 = (bf16[2,136,512]{2,1,0:T(8,128)(2,1)S(1)}, bf16[2,136,512]{2,1,0:T(8,128)(2,1)S(1)}, u32[]{:S(2)}, u32[]{:S(2)}) collective-permute-start(bf16[2,136,512]{2,1,0:T(8,128)(2,1)S(1)} %collective-permute-done.7.refs_4_), channel_id=1, source_target_pairs={{0,4},{4,0},{8,12},{12,8},{16,20},{20,16},{24,28},{28,24},{1,5},{5... | collective-permute-start | bytes 835592 | tf_op jit(solution)/shard_map/ppermute | solution.py:358
  40.5 28.4 %collective-permute-start.25 = (bf16[2,384,768]{2,1,0:T(8,128)(2,1)}, bf16[2,384,768]{2,1,0:T(8,128)(2,1)S(1)}, u32[]{:S(2)}, u32[]{:S(2)}) collective-permute-start(bf16[2,384,768]{2,1,0:T(8,128)(2,1)} %slice.11), channel_id=1, source_target_pairs={{1,2},{2,1},{5,6},{6,5},{9,10},{10,9},{13,14},{14,13},{17,18},{18,... | collective-permute-start | bytes 3538952 | tf_op jit(solution)/shard_map/ppermute | solution.py:347
  41.3 34.9 %collective-permute-start.26 = (bf16[2,384,768]{2,1,0:T(8,128)(2,1)}, bf16[2,384,768]{2,1,0:T(8,128)(2,1)S(1)}, u32[]{:S(2)}, u32[]{:S(2)}) collective-permute-start(bf16[2,384,768]{2,1,0:T(8,128)(2,1)} %slice.11), channel_id=1, source_target_pairs={{0,1},{2,3},{1,0},{3,2},{4,5},{6,7},{5,4},{7,6},{8,9},{10,11},{9,8... | collective-permute-start | bytes 3538952 | tf_op jit(solution)/shard_map/ppermute | solution.py:347
  44.3 16.1 %collective-permute-start.14 = (bf16[2,136,512]{2,1,0:T(8,128)(2,1)}, bf16[2,136,512]{2,1,0:T(8,128)(2,1)}, u32[]{:S(2)}, u32[]{:S(2)}) collective-permute-start(bf16[2,136,512]{2,1,0:T(8,128)(2,1)} %pad_maximum_fusion.1.refs_0_), channel_id=1, source_target_pairs={{0,4},{4,0},{8,12},{12,8},{16,20},{20,16},{24,28},{28,24},{1,5},{5... | collective-permute-start | bytes 835592 | tf_op jit(solution)/shard_map/ppermute | solution.py:358
  55.8 39.5 %collective-permute-start.11 = (bf16[2,384,768]{2,1,0:T(8,128)(2,1)}, bf16[2,384,768]{2,1,0:T(8,128)(2,1)S(1)}, u32[]{:S(2)}, u32[]{:S(2)}) collective-permute-start(bf16[2,384,768]{2,1,0:T(8,128)(2,1)} %get-tuple-element.55), channel_id=1, source_target_pairs={{1,2},{2,1},{5,6},{6,5},{9,10},{10,9},{13,14},{14,13},{17,18},{18,... | collective-permute-start | bytes 3538952 | tf_op jit(solution)/shard_map/ppermute | solution.py:374
  56.5 45.0 %collective-permute-start.12 = (bf16[2,384,768]{2,1,0:T(8,128)(2,1)}, bf16[2,384,768]{2,1,0:T(8,128)(2,1)}, u32[]{:S(2)}, u32[]{:S(2)}) collective-permute-start(bf16[2,384,768]{2,1,0:T(8,128)(2,1)} %get-tuple-element.56), channel_id=1, source_target_pairs={{0,1},{2,3},{1,0},{3,2},{4,5},{6,7},{5,4},{7,6},{8,9},{10,11},{9,8... | collective-permute-start | bytes 3538952 | tf_op jit(solution)/shard_map/ppermute | solution.py:373
  60.5 7.0 %collective-permute-start.15 = (bf16[2,136,512]{2,1,0:T(8,128)(2,1)}, bf16[2,136,512]{2,1,0:T(8,128)(2,1)}, u32[]{:S(2)}, u32[]{:S(2)}) collective-permute-start(bf16[2,136,512]{2,1,0:T(8,128)(2,1)} %pad_maximum_fusion.1.refs_0_), channel_id=1, source_target_pairs={{0,8},{4,12},{8,0},{12,4},{16,24},{20,28},{24,16},{28,20},{1,9},{5... | collective-permute-start | bytes 835592 | tf_op jit(solution)/shard_map/ppermute | solution.py:356
  67.4 14.6 %collective-permute-start.17 = (bf16[2,136,512]{2,1,0:T(8,128)(2,1)}, bf16[2,136,512]{2,1,0:T(8,128)(2,1)}, u32[]{:S(2)}, u32[]{:S(2)}) collective-permute-start(bf16[2,136,512]{2,1,0:T(8,128)(2,1)} %pad_maximum_fusion.1.refs_0_), channel_id=1, source_target_pairs={{0,16},{4,20},{8,24},{12,28},{16,0},{20,4},{24,8},{28,12},{1,17},{... | collective-permute-start | bytes 835592 | tf_op jit(solution)/shard_map/ppermute | solution.py:356
  68.9 13.8 %collective-permute-start.19 = (bf16[2,136,512]{2,1,0:T(8,128)(2,1)}, bf16[2,136,512]{2,1,0:T(8,128)(2,1)}, u32[]{:S(2)}, u32[]{:S(2)}) collective-permute-start(bf16[2,136,512]{2,1,0:T(8,128)(2,1)} %pad_maximum_fusion.1.refs_0_), channel_id=1, source_target_pairs={{0,24},{4,28},{8,16},{12,20},{16,8},{20,12},{24,0},{28,4},{1,25},{... | collective-permute-start | bytes 835592 | tf_op jit(solution)/shard_map/ppermute | solution.py:356
  76.2 10.6 %collective-permute-start.16 = (bf16[2,136,512]{2,1,0:T(8,128)(2,1)}, bf16[2,136,512]{2,1,0:T(8,128)(2,1)}, u32[]{:S(2)}, u32[]{:S(2)}) collective-permute-start(bf16[2,136,512]{2,1,0:T(8,128)(2,1)} %collective-permute-done.15.refs_2_), channel_id=1, source_target_pairs={{0,4},{4,0},{8,12},{12,8},{16,20},{20,16},{24,28},{28,24},{1,5},{5... | collective-permute-start | bytes 835592 | tf_op jit(solution)/shard_map/ppermute | solution.py:358
  82.0 29.8 %collective-permute-start.27 = (bf16[2,384,768]{2,1,0:T(8,128)(2,1)}, bf16[2,384,768]{2,1,0:T(8,128)(2,1)S(1)}, u32[]{:S(2)}, u32[]{:S(2)}) collective-permute-start(bf16[2,384,768]{2,1,0:T(8,128)(2,1)} %get-tuple-element.71), channel_id=1, source_target_pairs={{1,2},{2,1},{5,6},{6,5},{9,10},{10,9},{13,14},{14,13},{17,18},{18,... | collective-permute-start | bytes 3538952 | tf_op jit(solution)/shard_map/ppermute | solution.py:374
  82.7 44.0 %collective-permute-start.28 = (bf16[2,384,768]{2,1,0:T(8,128)(2,1)}, bf16[2,384,768]{2,1,0:T(8,128)(2,1)S(1)}, u32[]{:S(2)}, u32[]{:S(2)}) collective-permute-start(bf16[2,384,768]{2,1,0:T(8,128)(2,1)} %get-tuple-element.72), channel_id=1, source_target_pairs={{0,1},{2,3},{1,0},{3,2},{4,5},{6,7},{5,4},{7,6},{8,9},{10,11},{9,8... | collective-permute-start | bytes 3538952 | tf_op jit(solution)/shard_map/ppermute | solution.py:373
  86.8 1.9 collective-permute-start.18
  106.6 36.2 %collective-permute-start.21 = (bf16[2,384,768]{2,1,0:T(8,128)(2,1)}, bf16[2,384,768]{2,1,0:T(8,128)(2,1)S(1)}, u32[]{:S(2)}, u32[]{:S(2)}) collective-permute-start(bf16[2,384,768]{2,1,0:T(8,128)(2,1)} %get-tuple-element.60), channel_id=1, source_target_pairs={{1,2},{2,1},{5,6},{6,5},{9,10},{10,9},{13,14},{14,13},{17,18},{18,... | collective-permute-start | bytes 3538952 | tf_op jit(solution)/shard_map/ppermute | solution.py:374
  107.4 44.7 %collective-permute-start.22 = (bf16[2,384,768]{2,1,0:T(8,128)(2,1)}, bf16[2,384,768]{2,1,0:T(8,128)(2,1)}, u32[]{:S(2)}, u32[]{:S(2)}) collective-permute-start(bf16[2,384,768]{2,1,0:T(8,128)(2,1)} %get-tuple-element.61), channel_id=1, source_target_pairs={{0,1},{2,3},{1,0},{3,2},{4,5},{6,7},{5,4},{7,6},{8,9},{10,11},{9,8... | collective-permute-start | bytes 3538952 | tf_op jit(solution)/shard_map/ppermute | solution.py:373
  132.6 42.1 %collective-permute-start.29 = (bf16[2,384,768]{2,1,0:T(8,128)(2,1)}, bf16[2,384,768]{2,1,0:T(8,128)(2,1)S(1)}, u32[]{:S(2)}, u32[]{:S(2)}) collective-permute-start(bf16[2,384,768]{2,1,0:T(8,128)(2,1)} %get-tuple-element.73), channel_id=1, source_target_pairs={{1,2},{2,1},{5,6},{6,5},{9,10},{10,9},{13,14},{14,13},{17,18},{18,... | collective-permute-start | bytes 3538952 | tf_op jit(solution)/shard_map/ppermute | solution.py:374
  133.3 44.0 %collective-permute-start.30 = (bf16[2,384,768]{2,1,0:T(8,128)(2,1)}, bf16[2,384,768]{2,1,0:T(8,128)(2,1)S(1)}, u32[]{:S(2)}, u32[]{:S(2)}) collective-permute-start(bf16[2,384,768]{2,1,0:T(8,128)(2,1)} %get-tuple-element.74), channel_id=1, source_target_pairs={{0,1},{2,3},{1,0},{3,2},{4,5},{6,7},{5,4},{7,6},{8,9},{10,11},{9,8... | collective-permute-start | bytes 3538952 | tf_op jit(solution)/shard_map/ppermute | solution.py:373
  156.9 45.8 %collective-permute-start.24 = (bf16[2,384,768]{2,1,0:T(8,128)(2,1)}, bf16[2,384,768]{2,1,0:T(8,128)(2,1)}, u32[]{:S(2)}, u32[]{:S(2)}) collective-permute-start(bf16[2,384,768]{2,1,0:T(8,128)(2,1)} %get-tuple-element.66), channel_id=1, source_target_pairs={{0,1},{2,3},{1,0},{3,2},{4,5},{6,7},{5,4},{7,6},{8,9},{10,11},{9,8... | collective-permute-start | bytes 3538952 | tf_op jit(solution)/shard_map/ppermute | solution.py:373
  159.6 43.1 %collective-permute-start.23 = (bf16[2,384,768]{2,1,0:T(8,128)(2,1)}, bf16[2,384,768]{2,1,0:T(8,128)(2,1)}, u32[]{:S(2)}, u32[]{:S(2)}) collective-permute-start(bf16[2,384,768]{2,1,0:T(8,128)(2,1)} %get-tuple-element.65), channel_id=1, source_target_pairs={{1,2},{2,1},{5,6},{6,5},{9,10},{10,9},{13,14},{14,13},{17,18},{18,... | collective-permute-start | bytes 3538952 | tf_op jit(solution)/shard_map/ppermute | solution.py:374
  183.3 44.9 %collective-permute-start.32 = (bf16[2,384,768]{2,1,0:T(8,128)(2,1)}, bf16[2,384,768]{2,1,0:T(8,128)(2,1)S(1)}, u32[]{:S(2)}, u32[]{:S(2)}) collective-permute-start(bf16[2,384,768]{2,1,0:T(8,128)(2,1)} %get-tuple-element.84), channel_id=1, source_target_pairs={{0,1},{2,3},{1,0},{3,2},{4,5},{6,7},{5,4},{7,6},{8,9},{10,11},{9,8... | collective-permute-start | bytes 3538952 | tf_op jit(solution)/shard_map/ppermute | solution.py:373
  185.7 42.5 %collective-permute-start.31 = (bf16[2,384,768]{2,1,0:T(8,128)(2,1)}, bf16[2,384,768]{2,1,0:T(8,128)(2,1)}, u32[]{:S(2)}, u32[]{:S(2)}) collective-permute-start(bf16[2,384,768]{2,1,0:T(8,128)(2,1)} %get-tuple-element.83), channel_id=1, source_target_pairs={{1,2},{2,1},{5,6},{6,5},{9,10},{10,9},{13,14},{14,13},{17,18},{18,... | collective-permute-start | bytes 3538952 | tf_op jit(solution)/shard_map/ppermute | solution.py:374
  205.6 25.7 %all-to-all-start = ((f32[32,4,128]{2,1,0:T(4,128)}), f32[32,4,128]{2,1,0:T(4,128)}, u32[]{:S(2)}, u32[]{:S(2)}) async-start(f32[32,4,128]{2,1,0:T(4,128)} %copy.13), calls=%async_computation | async-start | bytes 131072 | tf_op jit(solution)/shard_map/all_to_all | solution.py:399
  (23 other events, 201.2 us)

commit v2 on v1

--- a/solution.py
+++ b/solution.py
@@ -217,83 +217,112 @@
     )(rows, w)
 
 
-def weight_kernel(n, places, base, sc, own_ref, *refs):
-    others, refs = refs[: 2 * (n - 1)], refs[2 * (n - 1) :]
+def arrivals(n, d):
+    found = []
+    for i in range(2):
+        for z in range(n):
+            up = 1 - z % 2 if i == 0 else z % 2
+            if (z if up else n - 1 - z) >= d and i not in found:
+                found.append(i)
+    return found
+
+
+def weight_kernel(n, places, base, pairs, mode, sc, *refs):
+    refs = list(refs)
     sets = 1 + max(p for p, _ in places)
-    rows_refs, refs = refs[:sets], refs[sets:]
-    tgt_refs, refs = refs[:sets], refs[sets:]
-    w_ref, o_ref, x_ref = refs[0], refs[-2], refs[-1]
+    own_ref = refs.pop(0) if mode == "begin" else None
+    others = [refs.pop(0) for _ in pairs]
+    rows_refs = [refs.pop(0) for _ in range(sets)]
+    if mode != "end":
+        tgt_refs = [refs.pop(0) for _ in range(sets)]
+        w_ref = refs.pop(0)
+        x_ref = refs[-1]
+        sources, tokens = tgt_refs[0].shape[1], tgt_refs[0].shape[3]
+    o_ref = {"begin": refs[-2], "parts": None, "end": refs[-1]}[mode]
     z, me = sc[0], sc[1]
     l = base + pl.program_id(0)
-    depth = own_ref.shape[1]
-    sources, tokens = tgt_refs[0].shape[1], tgt_refs[0].shape[3]
-    here = lax.broadcasted_iota(jnp.int32, (depth, tokens), 0).astype(F32)
+    depth = rows_refs[0].shape[2]
+    if mode != "begin":
+        refs[-1][...] = refs[0][...]
 
     def take(h_ref, place, g, fresh):
         group, at = place
         rows = rows_refs[group][at, 0]
         h = h_ref[0]
-        grad = lax.dot_general(rows, h, (((0,), (0,)), ((), ())), preferred_element_type=F32)
-        if fresh:
-            o_ref[...] = grad
-        else:
-            o_ref[...] += grad
-        u = dot(rows, w_ref[...])
-        col = jnp.sum(u * h.astype(F32), axis=1, keepdims=True)
-        wide = jnp.broadcast_to(col, (depth, tokens))
-        for m in range(sources):
-            target = tgt_refs[group][at, m, pl.ds(l, 1), :]
-            row = jnp.sum(jnp.where(here == target, wide, 0.0), axis=0, keepdims=True)
-            x_ref[0, pl.ds((me ^ m) * n + g, 1), :] = row
-
-    take(own_ref, places[0], z, True)
-    for d in range(1, n):
-        for i in range(2):
-            up, behind = heading(z, n, i)
-            place = (places[d][0], up * places[d][1] + (1 - up) * places[n - d][1])
-
-            @pl.when(behind >= d)
-            def _():
-                take(others[i * (n - 1) + d - 1], place, z + d * (1 - 2 * up), False)
-
-
-def weights(sc, own, one, two, sets, places, w, base, held):
+        if mode != "parts":
+            grad = lax.dot_general(rows, h, (((0,), (0,)), ((), ())), preferred_element_type=F32)
+            if fresh:
+                o_ref[...] = grad
+            else:
+                o_ref[...] += grad
+        if mode != "end":
+            here = lax.broadcasted_iota(jnp.int32, (depth, tokens), 0).astype(F32)
+            u = dot(rows, w_ref[...])
+            col = jnp.sum(u * h.astype(F32), axis=1, keepdims=True)
+            wide = jnp.broadcast_to(col, (depth, tokens))
+            for m in range(sources):
+                target = tgt_refs[group][at, m, pl.ds(l, 1), :]
+                row = jnp.sum(jnp.where(here == target, wide, 0.0), axis=0, keepdims=True)
+                x_ref[0, pl.ds((me ^ m) * n + g, 1), :] = row
+
+    if mode == "begin":
+        take(own_ref, places[0], z, True)
+    for h_ref, (i, d) in zip(others, pairs):
+        up, behind = heading(z, n, i)
+        place = (places[d][0], up * places[d][1] + (1 - up) * places[n - d][1])
+
+        @pl.when(behind >= d)
+        def _():
+            take(h_ref, place, z + d * (1 - 2 * up), False)
+
+
+def weights(sc, own, got, sets, places, w, base, mode, held):
     n = len(places)
+    distances = range(1, n - 1) if mode == "begin" else [n - 1]
+    pairs = [(i, d) for d in distances for i in arrivals(n, d)]
     _, total, depth, part = sets[0][0].shape
-    count, _, hidden = one[0].shape
+    count, _, hidden = got[0][0].shape
     _, sources, _, tokens = sets[0][1].shape
-    extra = [] if held is None else [held]
     chunk = pl.BlockSpec((1, depth, hidden), lambda l, sc: (l, 0, 0))
+    block = pl.BlockSpec((part, hidden), lambda l, sc: (0, base + l))
+    lines = pl.BlockSpec((1, sources * n, tokens), lambda l, sc: (l, 0, 0))
+    args, specs = [], []
+    if mode == "begin":
+        args.append(own)
+        specs.append(pl.BlockSpec((1, depth, hidden), lambda l, sc: (base + l, 0, 0)))
+    args += [got[i][d - 1] for i, d in pairs]
+    specs += [chunk] * len(pairs)
+    for rows, _ in sets:
+        args.append(rows)
+        specs.append(
+            pl.BlockSpec((rows.shape[0], 1, depth, part), lambda l, sc: (0, base + l, 0, 0))
+        )
+    if mode != "end":
+        for _, tgt in sets:
+            args.append(tgt)
+            specs.append(pl.BlockSpec(tgt.shape, lambda l, sc: (0, 0, 0, 0)))
+        args.append(w)
+        specs.append(block)
+    if held is not None:
+        args.append(held)
+        inner = {"begin": pl.BlockSpec(memory_space=pl.ANY), "parts": lines, "end": block}
+        specs.append(inner[mode])
+    grads = jax.ShapeDtypeStruct((part, total * hidden), F32)
+    rest = jax.ShapeDtypeStruct((count, sources * n, tokens), F32)
+    outs = {"begin": ([grads, rest], [block, lines]), "parts": (rest, lines), "end": (grads, block)}
+    flops = 2 * (len(pairs) + 1) * count * depth * part * hidden
     return pl.pallas_call(
-        functools.partial(weight_kernel, n, places, base),
+        functools.partial(weight_kernel, n, places, base, pairs, mode),
         grid_spec=pltpu.PrefetchScalarGridSpec(
-            num_scalar_prefetch=1,
-            grid=(count,),
-            in_specs=[pl.BlockSpec((1, depth, hidden), lambda l, sc: (base + l, 0, 0))]
-            + [chunk] * (2 * (n - 1))
-            + [
-                pl.BlockSpec((rows.shape[0], 1, depth, part), lambda l, sc: (0, base + l, 0, 0))
-                for rows, _ in sets
-            ]
-            + [pl.BlockSpec(tgt.shape, lambda l, sc: (0, 0, 0, 0)) for _, tgt in sets]
-            + [pl.BlockSpec((part, hidden), lambda l, sc: (0, base + l))]
-            + [pl.BlockSpec(memory_space=pl.ANY)] * len(extra),
-            out_specs=[
-                pl.BlockSpec((part, hidden), lambda l, sc: (0, base + l)),
-                pl.BlockSpec((1, sources * n, tokens), lambda l, sc: (l, 0, 0)),
-            ],
-        ),
-        out_shape=[
-            jax.ShapeDtypeStruct((part, total * hidden), F32),
-            jax.ShapeDtypeStruct((count, sources * n, tokens), F32),
-        ],
-        input_output_aliases={2 * n + 2 * len(sets) + 1: 0} if extra else {},
+            num_scalar_prefetch=1, grid=(count,), in_specs=specs, out_specs=outs[mode][1]
+        ),
+        out_shape=outs[mode][0],
+        input_output_aliases={} if held is None else {len(args): 0},
         cost_estimate=cost(
-            4 * n * count * depth * part * hidden,
-            count * (2 * (2 * n - 1) * depth * hidden + 2 * n * depth * part + 6 * part * hidden),
-        ),
-        name="weights",
-    )(sc, own, *one, *two, *[r for r, _ in sets], *[t for _, t in sets], w, *extra)
+            flops,
+            count * (2 * (len(pairs) + 1) * depth * hidden + 2 * n * depth * part + 6 * part * hidden),
+        ),
+    )(sc, *args)
 
 
 def shares(expert_of, routes, gates, n_ep):
@@ -360,32 +389,32 @@
     rows = [(sets[i][0], at) for i, at in places]
     own = own_part(rows, w_down)
 
-    weight_grad, parts = None, []
+    weight_grad, parts = None, [None] * chunks
     for t in range(2, n + 1):
         for c in range(chunks):
             base = c * count
             a, b = got[c][0][-1], got[c][1][-1]
-            if t == n and c == 0:
-                a, b, own = lax.optimization_barrier((a, b, own))
-            if t == n and c > 0:
+            if (t == n - 1 and c > 0) or (t == n and c == 0):
                 a, b, weight_grad = lax.optimization_barrier((a, b, weight_grad))
+            if t == n and c == chunks - 1:
+                for e in range(chunks):
+                    parts[e] = weights(
+                        sc, saved, got[e], sets, places, w_down, e * count, "parts", parts[e]
+                    )
+                ready = jnp.concatenate(parts, axis=0).transpose(1, 0, 2)
+                a, b, ready, own = lax.optimization_barrier((a, b, ready, own))
+                back = lax.all_to_all(ready, ("ep", "dp"), split_axis=0, concat_axis=0, tiled=True)
             a, b = step(sc, a, b, rows, w_down, n, t, base)
             got[c][1].append(lax.ppermute(a, "dp", swaps[1]))
             got[c][0].append(lax.ppermute(b, "dp", swaps[0]))
-            if t == n:
-                weight_grad, x = weights(
-                    sc,
-                    saved,
-                    got[c][0][: n - 1],
-                    got[c][1][: n - 1],
-                    sets,
-                    places,
-                    w_down,
-                    base,
-                    weight_grad,
+            if t == n - 1:
+                weight_grad, parts[c] = weights(
+                    sc, saved, got[c], sets, places, w_down, base, "begin", weight_grad
                 )
-                parts.append(x)
-    ready = jnp.concatenate(parts, axis=0).transpose(1, 0, 2)
+    for c in range(chunks):
+        weight_grad = weights(
+            sc, saved, got[c], sets, places, w_down, c * count, "end", weight_grad
+        )
     for c in range(chunks):
         base = c * count
         if c < chunks - 1:
@@ -393,16 +422,13 @@
             for part in got[c]:
                 total = total + part[-1].astype(F32)
             own = lax.dynamic_update_slice_in_dim(own, total.astype(BF), base, axis=0)
-            own, ready = lax.optimization_barrier((own, ready))
+            own, weight_grad, got[-1] = lax.optimization_barrier((own, weight_grad, got[-1]))
     inverse = shares(expert_of, routes[0].T, gates[0].T, n_ep)
-    ready, inverse = lax.optimization_barrier((ready, inverse))
-    back = lax.all_to_all(ready, ("ep", "dp"), split_axis=0, concat_axis=0, tiled=True)
     total = own.astype(F32)
     for part in got[-1]:
         wide = ((local_experts - count, 0), (0, 0), (0, 0))
         total = total + jnp.pad(part[-1], wide).astype(F32)
     hidden_grad = total.astype(BF)
-    back, hidden_grad = lax.optimization_barrier((back, hidden_grad))
     back = back.reshape(n_ep, n, local_experts, 1, tokens)
     gate_grad = jnp.sum(back * inverse, axis=(0, 1, 2)).T[None]
     return (hidden_grad.reshape(hidden_saved.shape), gate_grad, weight_grad)

time: 234 us -> 269 us (1.15)
  waiting for transfers between devices: 90.5 us -> 119 us
  Pallas kernels: 72.7 us -> 88.8 us
  starting transfers between devices: 51.6 us -> 38.9 us
  local copies, waits for them, and re-layouts: 7.36 us -> 10.1 us
    ppermute x3, waiting for transfers between devices: 8.62 us -> 36.9 us  [local(): arrived[d] = lax.ppermute(packed[d], 'dp', shift)]
    ppermute x6, waiting for transfers between devices: 51.7 us -> 28.3 us  [local(): got[c][1].append(lax.ppermute(a, 'dp', swaps[1]))]
    all_to_all x1, waiting for transfers between devices: 0.01 us -> 18.9 us  [local(): lax.all_to_all(ready, ('ep', 'dp'), split_axis=0, concat_axis=0, tiled=True)]
    ppermute x4, waiting for transfers between devices: 7.88 us -> 26.3 us  [local(): got[c][i].append(lax.ppermute(part, 'dp', swaps[i]))]
    pallas_call x2 -> x6, Pallas kernels: 27 us -> 43.1 us  [weights(): pl.pallas_call(functools.partial(weight_kernel, n, places, base, pairs, m...]
    ppermute x6, starting transfers between devices: 21.8 us -> 8.63 us  [local(): got[c][1].append(lax.ppermute(a, 'dp', swaps[1]))]
    ppermute x6, waiting for transfers between devices: 17.9 us -> 5.36 us  [local(): pieces[m] = lax.ppermute(pieces[0], 'ep', [(e, e ^ m) for e in range(n_ep)])]
    ppermute x4, starting transfers between devices: 6.48 us -> 3.39 us  [local(): got[c][i].append(lax.ppermute(part, 'dp', swaps[i]))]
  transfers between devices with their start and end apart: 34 -> 34, of which waited for: 15 -> 14; matrix products, arithmetic and copies ran while one was open for 5% -> 4% of each run, Pallas kernels for 30% -> 32%
where the time goes in v2:
time: 269 us; the launch traced here: 268 us
  waiting for transfers between devices  119 us (44%)
  Pallas kernels  88.8 us (33%)
  starting transfers between devices  38.9 us (14%)
  local copies, waits for them, and re-layouts  10.1 us (4%)
  other arithmetic  9.96 us (4%)
    pallas_call x6, Pallas kernels, weights(): pl.pallas_call(functools.partial(weight_kernel, n, places, base, pairs, m...  43.1 us
    ppermute x3, waiting for transfers between devices, local(): arrived[d] = lax.ppermute(packed[d], 'dp', shift)  36.9 us
    pallas_call x6, Pallas kernels, step(): pl.pallas_call(functools.partial(step_kernel, n, t), grid_spec=pltpu.Pref...  29.3 us
    ppermute x6, waiting for transfers between devices, local(): got[c][1].append(lax.ppermute(a, 'dp', swaps[1]))  28.3 us
    ppermute x4, waiting for transfers between devices, local(): got[c][i].append(lax.ppermute(part, 'dp', swaps[i]))  26.3 us
    all_to_all x1, waiting for transfers between devices, local(): lax.all_to_all(ready, ('ep', 'dp'), split_axis=0, concat_axis=0, tiled=True)  18.9 us
    pallas_call x2, Pallas kernels, dispatch(): pl.pallas_call(functools.partial(dispatch_kernel, (sources, local_experts...  9.3 us
    ppermute x3, starting transfers between devices, local(): arrived[d] = lax.ppermute(packed[d], 'dp', shift)  8.91 us
  transfers between devices with their start and end apart: 34, of which 14 were waited for; matrix products, arithmetic and copies ran while one was open for 4% of the time, Pallas kernels for 32%

profile of v2, /device:TPU:0, one launch (start us, length us, event | category | flops | bytes accessed | tf_op | source)
XLA Modules:
  0.0 268.1 jit_solution(18047889420052716073)
XLA Ops:
  2.5 3.1 %collective-permute-start = (bf16[136,512]{1,0:T(8,128)(2,1)}, bf16[136,512]{1,0:T(8,128)(2,1)S(1)}, u32[]{:S(2)}, u32[]{:S(2)}) collective-permute-start(bf16[136,512]{1,0:T(8,128)(2,1)} %get-tuple-element.53), channel_id=1, source_target_pairs={{0,1},{1,2},{2,3},{3,0},{4,5},{5,6},{6,7},{7,4},{8,9},{9,10},{10,1... | collective-permute-start | bytes 417800 | tf_op jit(solution)/shard_map/ppermute | solution.py:367
  7.6 4.8 %collective-permute-done = bf16[136,512]{1,0:T(8,128)(2,1)S(1)} collective-permute-done((bf16[136,512]{1,0:T(8,128)(2,1)}, bf16[136,512]{1,0:T(8,128)(2,1)S(1)}, u32[]{:S(2)}, u32[]{:S(2)}) %collective-permute-start) | collective-permute-done | bytes 139296 | tf_op jit(solution)/shard_map/ppermute | solution.py:367
  15.6 2.4 slice.10
  18.8 3.8 %collective-permute-start.17 = (bf16[136,512]{1,0:T(8,128)(2,1)S(1)}, bf16[136,512]{1,0:T(8,128)(2,1)S(1)}, u32[]{:S(2)}, u32[]{:S(2)}) collective-permute-start(bf16[136,512]{1,0:T(8,128)(2,1)S(1)} %copy-done.24), channel_id=1, source_target_pairs={{0,2},{1,3},{2,0},{3,1},{4,6},{5,7},{6,4},{7,5},{8,10},{9,11},{10,... | collective-permute-start | bytes 417800 | tf_op jit(solution)/shard_map/ppermute | solution.py:367
  24.2 30.6 %collective-permute-done.17 = bf16[136,512]{1,0:T(8,128)(2,1)S(1)} collective-permute-done((bf16[136,512]{1,0:T(8,128)(2,1)S(1)}, bf16[136,512]{1,0:T(8,128)(2,1)S(1)}, u32[]{:S(2)}, u32[]{:S(2)}) %collective-permute-start.17) | collective-permute-done | bytes 139296 | tf_op jit(solution)/shard_map/ppermute | solution.py:367
  58.2 5.3 %collective-permute-done.9.refs_6_ = bf16[2,136,512]{2,1,0:T(8,128)(2,1)S(1)} collective-permute-done((bf16[2,136,512]{2,1,0:T(8,128)(2,1)S(1)}, bf16[2,136,512]{2,1,0:T(8,128)(2,1)S(1)}, u32[]{:S(2)}, u32[]{:S(2)}) %collective-permute-start.9) | collective-permute-done | bytes 278560 | tf_op jit(solution)/shard_map/ppermute | solution.py:385
  69.0 4.6 %dispatch.2 = (bf16[2,4,384,512]{3,2,1,0:T(8,128)(2,1)}, f32[2,8,8,128]{3,2,1,0:T(8,128)}) custom-call(s32[34]{0:T(128)} %pad_add_fusion.sc, bf16[2,136,512]{2,1,0:T(8,128)(2,1)} %copy-done.10, bf16[2,136,512]{2,1,0:T(8,128)(2,1)} %copy-done.11, bf16[2,136,512]{2,1,0:T(8,128)(2,1)} %copy-done.12, bf16[2,136,512]{2,1,0:T(8,128)(2,1)} %copy-done.15, ...), custom_call_target="tpu_custom_call" | custom-call | flops 402653184 | bytes 5373952 | tf_op jit(solution)/shard_map/dispatch/pallas_call | solution.py:113
  73.7 10.3 %collective-permute-done.14.refs_1_.refs_2_ = bf16[2,384,768]{2,1,0:T(8,128)(2,1)} collective-permute-done((bf16[2,384,768]{2,1,0:T(8,128)(2,1)}, bf16[2,384,768]{2,1,0:T(8,128)(2,1)}, u32[]{:S(2)}, u32[]{:S(2)}) %collective-permute-start.14) | collective-permute-done | bytes 1179680 | tf_op jit(solution)/shard_map/ppermute | solution.py:376
  83.9 4.8 %step.7 = (bf16[2,384,768]{2,1,0:T(8,128)(2,1)}, bf16[2,384,768]{2,1,0:T(8,128)(2,1)}) custom-call(s32[34]{0:T(128)} %pad_add_fusion.sc, bf16[2,384,768]{2,1,0:T(8,128)(2,1)} %copy-done.4, bf16[2,384,768]{2,1,0:T(8,128)(2,1)} %collective-permute-done.14.refs_1_.refs_2_, bf16[2,4,384,512]{3,2,1,0:T(8,128)(2,1)} %get-tuple-element.57.refs_2_.refs_3_.refs_5_.refs_1_, ...), custom_call_target="tpu_custom_call" | custom-call | flops 1207959552 | bytes 7864320 | tf_op jit(solution)/shard_map/step/pallas_call | solution.py:172
  93.0 16.1 %collective-permute-done.2.refs_1_.refs_2_ = bf16[2,384,768]{2,1,0:T(8,128)(2,1)S(1)} collective-permute-done((bf16[2,384,768]{2,1,0:T(8,128)(2,1)}, bf16[2,384,768]{2,1,0:T(8,128)(2,1)S(1)}, u32[]{:S(2)}, u32[]{:S(2)}) %collective-permute-start.2) | collective-permute-done | bytes 1179680 | tf_op jit(solution)/shard_map/ppermute | solution.py:376
  110.1 4.8 %step.6 = (bf16[2,384,768]{2,1,0:T(8,128)(2,1)}, bf16[2,384,768]{2,1,0:T(8,128)(2,1)}) custom-call(s32[34]{0:T(128)} %pad_add_fusion.sc, bf16[2,384,768]{2,1,0:T(8,128)(2,1)} %copy-done.5, bf16[2,384,768]{2,1,0:T(8,128)(2,1)} %copy-done.6, bf16[2,4,384,512]{3,2,1,0:T(8,128)(2,1)} %get-tuple-element.57.refs_2_.refs_3_.refs_5_.refs_1_, ...), custom_call_target="tpu_custom_call" | custom-call | flops 1207959552 | bytes 7864320 | tf_op jit(solution)/shard_map/step/pallas_call | solution.py:172
  121.5 4.7 %dispatch.3 = (bf16[2,4,384,512]{3,2,1,0:T(8,128)(2,1)}, f32[2,8,8,128]{3,2,1,0:T(8,128)}) custom-call(s32[34]{0:T(128)} %pad_add_fusion.sc, bf16[2,136,512]{2,1,0:T(8,128)(2,1)} %pad_maximum_fusion.1.refs_0_, bf16[2,136,512]{2,1,0:T(8,128)(2,1)} %collective-permute-done.18.refs_1_, bf16[2,136,512]{2,1,0:T(8,128)(2,1)} %collective-permute-done.19.refs_2_, ...), custom_call_target="tpu_custom_call" | custom-call | flops 402653184 | bytes 5373952 | tf_op jit(solution)/shard_map/dispatch/pallas_call | solution.py:113
  126.2 8.3 %collective-permute-done.16.refs_4_.refs_1_ = bf16[2,384,768]{2,1,0:T(8,128)(2,1)} collective-permute-done((bf16[2,384,768]{2,1,0:T(8,128)(2,1)}, bf16[2,384,768]{2,1,0:T(8,128)(2,1)}, u32[]{:S(2)}, u32[]{:S(2)}) %collective-permute-start.16) | collective-permute-done | bytes 1179680 | tf_op jit(solution)/shard_map/ppermute | solution.py:408
  134.5 5.1 %step.9 = (bf16[2,384,768]{2,1,0:T(8,128)(2,1)}, bf16[2,384,768]{2,1,0:T(8,128)(2,1)}) custom-call(s32[34]{0:T(128)} %pad_add_fusion.sc, bf16[2,384,768]{2,1,0:T(8,128)(2,1)} %copy-done.7, bf16[2,384,768]{2,1,0:T(8,128)(2,1)} %collective-permute-done.16.refs_4_.refs_1_, bf16[2,4,384,512]{3,2,1,0:T(8,128)(2,1)} %get-tuple-element.64.refs_6_.refs_2_.refs_3_.rows_ref, ...), custom_call_target="tpu_custom_call" | custom-call | flops 1207959552 | bytes 7864320 | tf_op jit(solution)/shard_map/step/pallas_call | solution.py:172
  141.3 11.0 %shard_map.85 = (f32[512,3072]{1,0:T(8,128)}, f32[2,32,128]{2,1,0:T(8,128)}) custom-call(s32[34]{0:T(128)} %pad_add_fusion.sc, bf16[4,384,768]{2,1,0:T(8,128)(2,1)} %bitcast.23, bf16[2,384,768]{2,1,0:T(8,128)(2,1)} %copy-done.4, bf16[2,384,768]{2,1,0:T(8,128)(2,1)} %collective-permute-done.14.refs_1_.refs_2_, bf16[2,384,768]{2,1,0:T(8,128)(2,1)} %copy-done.7, ...), custom_call_target="tpu_custom_call" | custom-call | flops 3019898880 | bytes 13762560 | tf_op jit(solution)/shard_map/pallas_call | solution.py:314
  152.3 7.5 %collective-permute-done.12.refs_1_.refs_4_ = bf16[2,384,768]{2,1,0:T(8,128)(2,1)} collective-permute-done((bf16[2,384,768]{2,1,0:T(8,128)(2,1)}, bf16[2,384,768]{2,1,0:T(8,128)(2,1)}, u32[]{:S(2)}, u32[]{:S(2)}) %collective-permute-start.12) | collective-permute-done | bytes 1179680 | tf_op jit(solution)/shard_map/ppermute | solution.py:408
  159.7 4.9 %step.8 = (bf16[2,384,768]{2,1,0:T(8,128)(2,1)}, bf16[2,384,768]{2,1,0:T(8,128)(2,1)}) custom-call(s32[34]{0:T(128)} %pad_add_fusion.sc, bf16[2,384,768]{2,1,0:T(8,128)(2,1)} %copy-done.8, bf16[2,384,768]{2,1,0:T(8,128)(2,1)} %collective-permute-done.12.refs_1_.refs_4_, bf16[2,4,384,512]{3,2,1,0:T(8,128)(2,1)} %get-tuple-element.64.refs_6_.refs_2_.refs_3_.rows_ref, ...), custom_call_target="tpu_custom_call" | custom-call | flops 1207959552 | bytes 7864320 | tf_op jit(solution)/shard_map/step/pallas_call | solution.py:172
  165.6 5.2 %own_part.1 = bf16[4,384,768]{2,1,0:T(8,128)(2,1)} custom-call(bf16[2,4,384,512]{3,2,1,0:T(8,128)(2,1)} %get-tuple-element.64.refs_6_.refs_2_.refs_3_.rows_ref, bf16[512,3072]{1,0:T(8,128)(2,1)} %refs_4_.11), custom_call_target="tpu_custom_call" | custom-call | flops 1207959552 | bytes 7077888 | tf_op jit(solution)/shard_map/own_part/pallas_call | solution.py:203
  170.8 11.0 %shard_map.87 = (f32[512,3072]{1,0:T(8,128)}, f32[2,32,128]{2,1,0:T(8,128)}) custom-call(s32[34]{0:T(128)} %pad_add_fusion.sc, bf16[4,384,768]{2,1,0:T(8,128)(2,1)} %bitcast.24, bf16[2,384,768]{2,1,0:T(8,128)(2,1)} %copy-done.5, bf16[2,384,768]{2,1,0:T(8,128)(2,1)} %copy-done.6, bf16[2,384,768]{2,1,0:T(8,128)(2,1)} %copy-done.8, ...), custom_call_target="tpu_custom_call", output_to_operand_aliasing={{0}: (11, {})} | custom-call | flops 3019898880 | bytes 13762560 | tf_op jit(solution)/shard_map/pallas_call | solution.py:314
  181.8 3.1 %collective-permute-done.27.refs_0_.refs_1_ = bf16[2,384,768]{2,1,0:T(8,128)(2,1)S(1)} collective-permute-done((bf16[2,384,768]{2,1,0:T(8,128)(2,1)}, bf16[2,384,768]{2,1,0:T(8,128)(2,1)S(1)}, u32[]{:S(2)}, u32[]{:S(2)}) %collective-permute-start.27) | collective-permute-done | bytes 1179680 | tf_op jit(solution)/shard_map/ppermute | solution.py:408
  186.0 4.9 %step.10 = (bf16[2,384,768]{2,1,0:T(8,128)(2,1)}, bf16[2,384,768]{2,1,0:T(8,128)(2,1)}) custom-call(s32[34]{0:T(128)} %pad_add_fusion.sc, bf16[2,384,768]{2,1,0:T(8,128)(2,1)} %collective-permute-done.28.refs_0_, bf16[2,384,768]{2,1,0:T(8,128)(2,1)} %copy-done.2, bf16[2,4,384,512]{3,2,1,0:T(8,128)(2,1)} %get-tuple-element.57.refs_2_.refs_3_.refs_5_.refs_1_, ...), custom_call_target="tpu_custom_call" | custom-call | flops 1207959552 | bytes 7864320 | tf_op jit(solution)/shard_map/step/pallas_call | solution.py:172
  190.8 3.6 %collective-permute-start.30 = (bf16[2,384,768]{2,1,0:T(8,128)(2,1)}, bf16[2,384,768]{2,1,0:T(8,128)(2,1)}, u32[]{:S(2)}, u32[]{:S(2)}) collective-permute-start(bf16[2,384,768]{2,1,0:T(8,128)(2,1)} %get-tuple-element.82), channel_id=1, source_target_pairs={{0,1},{2,3},{1,0},{3,2},{4,5},{6,7},{5,4},{7,6},{8,9},{10,11},{9,8... | collective-permute-start | bytes 3538952 | tf_op jit(solution)/shard_map/ppermute | solution.py:408
  196.1 4.7 %shard_map.86 = f32[2,32,128]{2,1,0:T(8,128)} custom-call(s32[34]{0:T(128)} %pad_add_fusion.sc, bf16[2,384,768]{2,1,0:T(8,128)(2,1)} %copy-done.2, bf16[2,4,384,512]{3,2,1,0:T(8,128)(2,1)} %get-tuple-element.57.refs_2_.refs_3_.refs_5_.refs_1_, ...), custom_call_target="tpu_custom_call", output_to_operand_aliasing={{}: (7, {})} | custom-call | flops 1207959552 | bytes 10223616 | tf_op jit(solution)/shard_map/pallas_call | solution.py:314
  200.8 9.4 %collective-permute-done.26.refs_0_.refs_1_ = bf16[2,384,768]{2,1,0:T(8,128)(2,1)S(1)} collective-permute-done((bf16[2,384,768]{2,1,0:T(8,128)(2,1)}, bf16[2,384,768]{2,1,0:T(8,128)(2,1)S(1)}, u32[]{:S(2)}, u32[]{:S(2)}) %collective-permute-start.26) | collective-permute-done | bytes 1179680 | tf_op jit(solution)/shard_map/ppermute | solution.py:408
  211.2 4.8 %shard_map.88 = f32[2,32,128]{2,1,0:T(8,128)} custom-call(s32[34]{0:T(128)} %pad_add_fusion.sc, bf16[2,384,768]{2,1,0:T(8,128)(2,1)} %copy-done.3, bf16[2,4,384,512]{3,2,1,0:T(8,128)(2,1)} %get-tuple-element.57.refs_2_.refs_3_.refs_5_.refs_1_, ...), custom_call_target="tpu_custom_call", output_to_operand_aliasing={{}: (7, {})} | custom-call | flops 1207959552 | bytes 10223616 | tf_op jit(solution)/shard_map/pallas_call | solution.py:314
  217.8 4.8 %step.11 = (bf16[2,384,768]{2,1,0:T(8,128)(2,1)}, bf16[2,384,768]{2,1,0:T(8,128)(2,1)}) custom-call(s32[34]{0:T(128)} %pad_add_fusion.sc, bf16[2,384,768]{2,1,0:T(8,128)(2,1)} %copy-done.9, bf16[2,384,768]{2,1,0:T(8,128)(2,1)} %copy-done.3, bf16[2,4,384,512]{3,2,1,0:T(8,128)(2,1)} %get-tuple-element.57.refs_2_.refs_3_.refs_5_.refs_1_, ...), custom_call_target="tpu_custom_call" | custom-call | flops 1207959552 | bytes 7864320 | tf_op jit(solution)/shard_map/step/pallas_call | solution.py:172
  226.9 3.6 %all-to-all-start = ((f32[32,4,128]{2,1,0:T(4,128)}), f32[32,4,128]{2,1,0:T(4,128)}, u32[]{:S(2)}, u32[]{:S(2)}) async-start(f32[32,4,128]{2,1,0:T(4,128)} %copy.17), calls=%async_computation | async-start | bytes 131072 | tf_op jit(solution)/shard_map/all_to_all | solution.py:406
  230.6 5.7 %shard_map.89.refs_3_ = f32[512,3072]{1,0:T(8,128)} custom-call(s32[34]{0:T(128)} %pad_add_fusion.sc, bf16[2,384,768]{2,1,0:T(8,128)(2,1)} %copy-done.2, bf16[2,4,384,512]{3,2,1,0:T(8,128)(2,1)} %get-tuple-element.57.refs_2_.refs_3_.refs_5_.refs_1_, ...), custom_call_target="tpu_custom_call", output_to_operand_aliasing={{}: (4, {})} | custom-call | flops 1207959552 | bytes 10223616 | tf_op jit(solution)/shard_map/pallas_call | solution.py:314
  236.3 5.9 %shard_map.90 = f32[512,3072]{1,0:T(8,128)} custom-call(s32[34]{0:T(128)} %pad_add_fusion.sc, bf16[2,384,768]{2,1,0:T(8,128)(2,1)} %copy-done.3, bf16[2,4,384,512]{3,2,1,0:T(8,128)(2,1)} %get-tuple-element.57.refs_2_.refs_3_.refs_5_.refs_1_, ...), custom_call_target="tpu_custom_call", output_to_operand_aliasing={{}: (4, {})} | custom-call | flops 1207959552 | bytes 10223616 | tf_op jit(solution)/shard_map/pallas_call | solution.py:314
  242.2 18.9 %all-to-all-done = f32[32,4,128]{2,1,0:T(4,128)} async-done(((f32[32,4,128]{2,1,0:T(4,128)}), f32[32,4,128]{2,1,0:T(4,128)}, u32[]{:S(2)}, u32[]{:S(2)}) %all-to-all-start) | async-done | bytes 65568 | tf_op jit(solution)/shard_map/all_to_all | solution.py:406
  262.8 2.2 fusion
  265.0 3.2 %add_convert_fusion = bf16[4,384,768]{2,1,0:T(8,128)(2,1)} fusion(bf16[4,384,768]{2,1,0:T(8,128)(2,1)S(1)} %fusion, bf16[2,384,768]{2,1,0:T(8,128)(2,1)} %collective-permute-done.32, bf16[2,384,768]{2,1,0:T(8,128)(2,1)S(1)} %collective-permute-done.31), kind=kLoop, calls=%fused_computation | loop fusion | flops 7077888 | bytes 7077888 | tf_op jit(solution)/shard_map/convert_element_type | solution.py:431
  (118 shorter events, 44.3 us)
Async XLA Ops:
  2.5 9.8 %collective-permute-start = (bf16[136,512]{1,0:T(8,128)(2,1)}, bf16[136,512]{1,0:T(8,128)(2,1)S(1)}, u32[]{:S(2)}, u32[]{:S(2)}) collective-permute-start(bf16[136,512]{1,0:T(8,128)(2,1)} %get-tuple-element.53), channel_id=1, source_target_pairs={{0,1},{1,2},{2,3},{3,0},{4,5},{5,6},{6,7},{7,4},{8,9},{9,10},{10,1... | collective-permute-start | bytes 417800 | tf_op jit(solution)/shard_map/ppermute | solution.py:367
  5.6 8.3 %collective-permute-start.3 = (bf16[136,512]{1,0:T(8,128)(2,1)}, bf16[136,512]{1,0:T(8,128)(2,1)S(1)}, u32[]{:S(2)}, u32[]{:S(2)}) collective-permute-start(bf16[136,512]{1,0:T(8,128)(2,1)} %get-tuple-element.56), channel_id=1, source_target_pairs={{0,3},{1,0},{2,1},{3,2},{4,7},{5,4},{6,5},{7,6},{8,11},{9,8},{10,9... | collective-permute-start | bytes 417800 | tf_op jit(solution)/shard_map/ppermute | solution.py:367
  14.0 40.8 %collective-permute-start.4 = (bf16[2,136,512]{2,1,0:T(8,128)(2,1)S(1)}, bf16[2,136,512]{2,1,0:T(8,128)(2,1)S(1)}, u32[]{:S(2)}, u32[]{:S(2)}) collective-permute-start(bf16[2,136,512]{2,1,0:T(8,128)(2,1)S(1)} %pad_maximum_fusion.refs_0_), channel_id=1, source_target_pairs={{0,4},{4,0},{8,12},{12,8},{16,20},{20,16},{24,28},{28,24},{1,5},{5... | collective-permute-start | bytes 835592 | tf_op jit(solution)/shard_map/ppermute | solution.py:387
  14.0 42.3 %collective-permute-start.5 = (bf16[2,136,512]{2,1,0:T(8,128)(2,1)S(1)}, bf16[2,136,512]{2,1,0:T(8,128)(2,1)S(1)}, u32[]{:S(2)}, u32[]{:S(2)}) collective-permute-start(bf16[2,136,512]{2,1,0:T(8,128)(2,1)S(1)} %pad_maximum_fusion.refs_0_), channel_id=1, source_target_pairs={{0,8},{4,12},{8,0},{12,4},{16,24},{20,28},{24,16},{28,20},{1,9},{5... | collective-permute-start | bytes 835592 | tf_op jit(solution)/shard_map/ppermute | solution.py:385
  18.0 49.9 %collective-permute-start.13 = (bf16[2,384,768]{2,1,0:T(8,128)(2,1)}, bf16[2,384,768]{2,1,0:T(8,128)(2,1)S(1)}, u32[]{:S(2)}, u32[]{:S(2)}) collective-permute-start(bf16[2,384,768]{2,1,0:T(8,128)(2,1)} %slice.10), channel_id=1, source_target_pairs={{1,2},{2,1},{5,6},{6,5},{9,10},{10,9},{13,14},{14,13},{17,18},{18,... | collective-permute-start | bytes 3538952 | tf_op jit(solution)/shard_map/ppermute | solution.py:376
  18.8 35.9 %collective-permute-start.17 = (bf16[136,512]{1,0:T(8,128)(2,1)S(1)}, bf16[136,512]{1,0:T(8,128)(2,1)S(1)}, u32[]{:S(2)}, u32[]{:S(2)}) collective-permute-start(bf16[136,512]{1,0:T(8,128)(2,1)S(1)} %copy-done.24), channel_id=1, source_target_pairs={{0,2},{1,3},{2,0},{3,1},{4,6},{5,7},{6,4},{7,5},{8,10},{9,11},{10,... | collective-permute-start | bytes 417800 | tf_op jit(solution)/shard_map/ppermute | solution.py:367
  22.7 34.8 %collective-permute-start.7 = (bf16[2,136,512]{2,1,0:T(8,128)(2,1)S(1)}, bf16[2,136,512]{2,1,0:T(8,128)(2,1)S(1)}, u32[]{:S(2)}, u32[]{:S(2)}) collective-permute-start(bf16[2,136,512]{2,1,0:T(8,128)(2,1)S(1)} %pad_maximum_fusion.refs_0_), channel_id=1, source_target_pairs={{0,16},{4,20},{8,24},{12,28},{16,0},{20,4},{24,8},{28,12},{1,17},{... | collective-permute-start | bytes 835592 | tf_op jit(solution)/shard_map/ppermute | solution.py:385
  54.7 29.2 %collective-permute-start.14 = (bf16[2,384,768]{2,1,0:T(8,128)(2,1)}, bf16[2,384,768]{2,1,0:T(8,128)(2,1)}, u32[]{:S(2)}, u32[]{:S(2)}) collective-permute-start(bf16[2,384,768]{2,1,0:T(8,128)(2,1)} %slice.10), channel_id=1, source_target_pairs={{0,1},{2,3},{1,0},{3,2},{4,5},{6,7},{5,4},{7,6},{8,9},{10,11},{9,8... | collective-permute-start | bytes 3538952 | tf_op jit(solution)/shard_map/ppermute | solution.py:376
  54.8 8.8 %collective-permute-start.9 = (bf16[2,136,512]{2,1,0:T(8,128)(2,1)S(1)}, bf16[2,136,512]{2,1,0:T(8,128)(2,1)S(1)}, u32[]{:S(2)}, u32[]{:S(2)}) collective-permute-start(bf16[2,136,512]{2,1,0:T(8,128)(2,1)S(1)} %pad_maximum_fusion.refs_0_), channel_id=1, source_target_pairs={{0,24},{4,28},{8,16},{12,20},{16,8},{20,12},{24,0},{28,4},{1,25},{... | collective-permute-start | bytes 835592 | tf_op jit(solution)/shard_map/ppermute | solution.py:385
  56.4 7.2 %collective-permute-start.6 = (bf16[2,136,512]{2,1,0:T(8,128)(2,1)S(1)}, bf16[2,136,512]{2,1,0:T(8,128)(2,1)S(1)}, u32[]{:S(2)}, u32[]{:S(2)}) collective-permute-start(bf16[2,136,512]{2,1,0:T(8,128)(2,1)S(1)} %collective-permute-done.5.refs_2_), channel_id=1, source_target_pairs={{0,4},{4,0},{8,12},{12,8},{16,20},{20,16},{24,28},{28,24},{1,5},{5... | collective-permute-start | bytes 835592 | tf_op jit(solution)/shard_map/ppermute | solution.py:387
  57.5 35.0 %collective-permute-start.1 = (bf16[2,384,768]{2,1,0:T(8,128)(2,1)}, bf16[2,384,768]{2,1,0:T(8,128)(2,1)S(1)}, u32[]{:S(2)}, u32[]{:S(2)}) collective-permute-start(bf16[2,384,768]{2,1,0:T(8,128)(2,1)} %slice.9), channel_id=1, source_target_pairs={{1,2},{2,1},{5,6},{6,5},{9,10},{10,9},{13,14},{14,13},{17,18},{18,... | collective-permute-start | bytes 3538952 | tf_op jit(solution)/shard_map/ppermute | solution.py:376
  63.6 1.8 collective-permute-start.8
  63.6 45.5 %collective-permute-start.2 = (bf16[2,384,768]{2,1,0:T(8,128)(2,1)}, bf16[2,384,768]{2,1,0:T(8,128)(2,1)S(1)}, u32[]{:S(2)}, u32[]{:S(2)}) collective-permute-start(bf16[2,384,768]{2,1,0:T(8,128)(2,1)} %slice.9), channel_id=1, source_target_pairs={{0,1},{2,3},{1,0},{3,2},{4,5},{6,7},{5,4},{7,6},{8,9},{10,11},{9,8... | collective-permute-start | bytes 3538952 | tf_op jit(solution)/shard_map/ppermute | solution.py:376
  67.0 22.4 %collective-permute-start.18 = (bf16[2,136,512]{2,1,0:T(8,128)(2,1)}, bf16[2,136,512]{2,1,0:T(8,128)(2,1)}, u32[]{:S(2)}, u32[]{:S(2)}) collective-permute-start(bf16[2,136,512]{2,1,0:T(8,128)(2,1)} %pad_maximum_fusion.1.refs_0_), channel_id=1, source_target_pairs={{0,4},{4,0},{8,12},{12,8},{16,20},{20,16},{24,28},{28,24},{1,5},{5... | collective-permute-start | bytes 835592 | tf_op jit(solution)/shard_map/ppermute | solution.py:387
  67.9 23.1 %collective-permute-start.19 = (bf16[2,136,512]{2,1,0:T(8,128)(2,1)}, bf16[2,136,512]{2,1,0:T(8,128)(2,1)}, u32[]{:S(2)}, u32[]{:S(2)}) collective-permute-start(bf16[2,136,512]{2,1,0:T(8,128)(2,1)} %pad_maximum_fusion.1.refs_0_), channel_id=1, source_target_pairs={{0,8},{4,12},{8,0},{12,4},{16,24},{20,28},{24,16},{28,20},{1,9},{5... | collective-permute-start | bytes 835592 | tf_op jit(solution)/shard_map/ppermute | solution.py:385
  88.7 37.4 %collective-permute-start.15 = (bf16[2,384,768]{2,1,0:T(8,128)(2,1)}, bf16[2,384,768]{2,1,0:T(8,128)(2,1)S(1)}, u32[]{:S(2)}, u32[]{:S(2)}) collective-permute-start(bf16[2,384,768]{2,1,0:T(8,128)(2,1)} %get-tuple-element.60), channel_id=1, source_target_pairs={{1,2},{2,1},{5,6},{6,5},{9,10},{10,9},{13,14},{14,13},{17,18},{18,... | collective-permute-start | bytes 3538952 | tf_op jit(solution)/shard_map/ppermute | solution.py:409
  89.4 45.0 %collective-permute-start.16 = (bf16[2,384,768]{2,1,0:T(8,128)(2,1)}, bf16[2,384,768]{2,1,0:T(8,128)(2,1)}, u32[]{:S(2)}, u32[]{:S(2)}) collective-permute-start(bf16[2,384,768]{2,1,0:T(8,128)(2,1)} %get-tuple-element.61), channel_id=1, source_target_pairs={{0,1},{2,3},{1,0},{3,2},{4,5},{6,7},{5,4},{7,6},{8,9},{10,11},{9,8... | collective-permute-start | bytes 3538952 | tf_op jit(solution)/shard_map/ppermute | solution.py:408
  91.0 23.9 %collective-permute-start.21 = (bf16[2,136,512]{2,1,0:T(8,128)(2,1)}, bf16[2,136,512]{2,1,0:T(8,128)(2,1)}, u32[]{:S(2)}, u32[]{:S(2)}) collective-permute-start(bf16[2,136,512]{2,1,0:T(8,128)(2,1)} %pad_maximum_fusion.1.refs_0_), channel_id=1, source_target_pairs={{0,16},{4,20},{8,24},{12,28},{16,0},{20,4},{24,8},{28,12},{1,17},{... | collective-permute-start | bytes 835592 | tf_op jit(solution)/shard_map/ppermute | solution.py:385
  92.5 23.2 %collective-permute-start.23 = (bf16[2,136,512]{2,1,0:T(8,128)(2,1)}, bf16[2,136,512]{2,1,0:T(8,128)(2,1)}, u32[]{:S(2)}, u32[]{:S(2)}) collective-permute-start(bf16[2,136,512]{2,1,0:T(8,128)(2,1)} %pad_maximum_fusion.1.refs_0_), channel_id=1, source_target_pairs={{0,24},{4,28},{8,16},{12,20},{16,8},{20,12},{24,0},{28,4},{1,25},{... | collective-permute-start | bytes 835592 | tf_op jit(solution)/shard_map/ppermute | solution.py:385
  109.1 8.1 %collective-permute-start.20 = (bf16[2,136,512]{2,1,0:T(8,128)(2,1)}, bf16[2,136,512]{2,1,0:T(8,128)(2,1)}, u32[]{:S(2)}, u32[]{:S(2)}) collective-permute-start(bf16[2,136,512]{2,1,0:T(8,128)(2,1)} %collective-permute-done.19.refs_2_), channel_id=1, source_target_pairs={{0,4},{4,0},{8,12},{12,8},{16,20},{20,16},{24,28},{28,24},{1,5},{5... | collective-permute-start | bytes 835592 | tf_op jit(solution)/shard_map/ppermute | solution.py:387
  114.9 37.3 %collective-permute-start.11 = (bf16[2,384,768]{2,1,0:T(8,128)(2,1)}, bf16[2,384,768]{2,1,0:T(8,128)(2,1)S(1)}, u32[]{:S(2)}, u32[]{:S(2)}) collective-permute-start(bf16[2,384,768]{2,1,0:T(8,128)(2,1)} %get-tuple-element.58), channel_id=1, source_target_pairs={{1,2},{2,1},{5,6},{6,5},{9,10},{10,9},{13,14},{14,13},{17,18},{18,... | collective-permute-start | bytes 3538952 | tf_op jit(solution)/shard_map/ppermute | solution.py:409
  115.7 44.1 %collective-permute-start.12 = (bf16[2,384,768]{2,1,0:T(8,128)(2,1)}, bf16[2,384,768]{2,1,0:T(8,128)(2,1)}, u32[]{:S(2)}, u32[]{:S(2)}) collective-permute-start(bf16[2,384,768]{2,1,0:T(8,128)(2,1)} %get-tuple-element.59), channel_id=1, source_target_pairs={{0,1},{2,3},{1,0},{3,2},{4,5},{6,7},{5,4},{7,6},{8,9},{10,11},{9,8... | collective-permute-start | bytes 3538952 | tf_op jit(solution)/shard_map/ppermute | solution.py:408
  117.2 1.8 collective-permute-start.22
  139.6 45.3 %collective-permute-start.27 = (bf16[2,384,768]{2,1,0:T(8,128)(2,1)}, bf16[2,384,768]{2,1,0:T(8,128)(2,1)S(1)}, u32[]{:S(2)}, u32[]{:S(2)}) collective-permute-start(bf16[2,384,768]{2,1,0:T(8,128)(2,1)} %get-tuple-element.72), channel_id=1, source_target_pairs={{0,1},{2,3},{1,0},{3,2},{4,5},{6,7},{5,4},{7,6},{8,9},{10,11},{9,8... | collective-permute-start | bytes 3538952 | tf_op jit(solution)/shard_map/ppermute | solution.py:408
  139.6 45.3 %collective-permute-start.28 = (bf16[2,384,768]{2,1,0:T(8,128)(2,1)}, bf16[2,384,768]{2,1,0:T(8,128)(2,1)}, u32[]{:S(2)}, u32[]{:S(2)}) collective-permute-start(bf16[2,384,768]{2,1,0:T(8,128)(2,1)} %get-tuple-element.77), channel_id=1, source_target_pairs={{1,2},{2,1},{5,6},{6,5},{9,10},{10,9},{13,14},{14,13},{17,18},{18,... | collective-permute-start | bytes 3538952 | tf_op jit(solution)/shard_map/ppermute | solution.py:409
  164.6 45.6 %collective-permute-start.26 = (bf16[2,384,768]{2,1,0:T(8,128)(2,1)}, bf16[2,384,768]{2,1,0:T(8,128)(2,1)S(1)}, u32[]{:S(2)}, u32[]{:S(2)}) collective-permute-start(bf16[2,384,768]{2,1,0:T(8,128)(2,1)} %get-tuple-element.71), channel_id=1, source_target_pairs={{0,1},{2,3},{1,0},{3,2},{4,5},{6,7},{5,4},{7,6},{8,9},{10,11},{9,8... | collective-permute-start | bytes 3538952 | tf_op jit(solution)/shard_map/ppermute | solution.py:408
  164.6 52.2 %collective-permute-start.25 = (bf16[2,384,768]{2,1,0:T(8,128)(2,1)}, bf16[2,384,768]{2,1,0:T(8,128)(2,1)S(1)}, u32[]{:S(2)}, u32[]{:S(2)}) collective-permute-start(bf16[2,384,768]{2,1,0:T(8,128)(2,1)} %get-tuple-element.70), channel_id=1, source_target_pairs={{1,2},{2,1},{5,6},{6,5},{9,10},{10,9},{13,14},{14,13},{17,18},{18,... | collective-permute-start | bytes 3538952 | tf_op jit(solution)/shard_map/ppermute | solution.py:409
  190.8 71.9 %collective-permute-start.30 = (bf16[2,384,768]{2,1,0:T(8,128)(2,1)}, bf16[2,384,768]{2,1,0:T(8,128)(2,1)}, u32[]{:S(2)}, u32[]{:S(2)}) collective-permute-start(bf16[2,384,768]{2,1,0:T(8,128)(2,1)} %get-tuple-element.82), channel_id=1, source_target_pairs={{0,1},{2,3},{1,0},{3,2},{4,5},{6,7},{5,4},{7,6},{8,9},{10,11},{9,8... | collective-permute-start | bytes 3538952 | tf_op jit(solution)/shard_map/ppermute | solution.py:408
  194.4 68.3 %collective-permute-start.29 = (bf16[2,384,768]{2,1,0:T(8,128)(2,1)}, bf16[2,384,768]{2,1,0:T(8,128)(2,1)}, u32[]{:S(2)}, u32[]{:S(2)}) collective-permute-start(bf16[2,384,768]{2,1,0:T(8,128)(2,1)} %get-tuple-element.81), channel_id=1, source_target_pairs={{1,2},{2,1},{5,6},{6,5},{9,10},{10,9},{13,14},{14,13},{17,18},{18,... | collective-permute-start | bytes 3538952 | tf_op jit(solution)/shard_map/ppermute | solution.py:409
  222.7 42.3 %collective-permute-start.31 = (bf16[2,384,768]{2,1,0:T(8,128)(2,1)}, bf16[2,384,768]{2,1,0:T(8,128)(2,1)S(1)}, u32[]{:S(2)}, u32[]{:S(2)}) collective-permute-start(bf16[2,384,768]{2,1,0:T(8,128)(2,1)} %get-tuple-element.86), channel_id=1, source_target_pairs={{1,2},{2,1},{5,6},{6,5},{9,10},{10,9},{13,14},{14,13},{17,18},{18,... | collective-permute-start | bytes 3538952 | tf_op jit(solution)/shard_map/ppermute | solution.py:409
  223.4 41.6 %collective-permute-start.32 = (bf16[2,384,768]{2,1,0:T(8,128)(2,1)}, bf16[2,384,768]{2,1,0:T(8,128)(2,1)}, u32[]{:S(2)}, u32[]{:S(2)}) collective-permute-start(bf16[2,384,768]{2,1,0:T(8,128)(2,1)} %get-tuple-element.87), channel_id=1, source_target_pairs={{0,1},{2,3},{1,0},{3,2},{4,5},{6,7},{5,4},{7,6},{8,9},{10,11},{9,8... | collective-permute-start | bytes 3538952 | tf_op jit(solution)/shard_map/ppermute | solution.py:408
  226.9 34.2 %all-to-all-start = ((f32[32,4,128]{2,1,0:T(4,128)}), f32[32,4,128]{2,1,0:T(4,128)}, u32[]{:S(2)}, u32[]{:S(2)}) async-start(f32[32,4,128]{2,1,0:T(4,128)} %copy.17), calls=%async_computation | async-start | bytes 131072 | tf_op jit(solution)/shard_map/all_to_all | solution.py:406
  (28 other events, 309.8 us)

commit v3 on v2

--- a/solution.py
+++ b/solution.py
@@ -11,6 +11,7 @@
 BF = jnp.bfloat16
 F32 = jnp.float32
 CHUNKS = 2
+ROOM = 32 << 20
 
 
 def cost(flops, nbytes):
@@ -188,8 +189,56 @@
             4 * count * depth * part * hidden,
             2 * count * (4 * depth * hidden + 2 * depth * part + part * hidden),
         ),
+        compiler_params=pltpu.CompilerParams(vmem_limit_bytes=ROOM),
         name="step",
     )(sc, a, b, source, source, w)
+
+
+def last_kernel(base, a_ref, b_ref, own_ref, *rest):
+    o_ref, a_in, b_in, total, sem = rest[-5:]
+    count, depth, _ = own_ref.shape
+    cut = 2 if depth % 32 == 0 else 1
+    high = depth // cut
+    spots = [(l, pl.ds(h * high, high)) for l in range(count) for h in range(cut)]
+    inward = []
+    for k, spot in enumerate(spots):
+        pair = [
+            pltpu.make_async_copy(a_ref.at[spot], a_in.at[spot], sem.at[0, k]),
+            pltpu.make_async_copy(b_ref.at[spot], b_in.at[spot], sem.at[1, k]),
+        ]
+        for copy in pair:
+            copy.start()
+        inward.append(pair)
+    outward = []
+    for k, spot in enumerate(spots):
+        for copy in inward[k]:
+            copy.wait()
+        value = a_in[spot].astype(F32) + b_in[spot].astype(F32)
+        total[spot] = (value + own_ref[spot].astype(F32)).astype(BF)
+        l, rows = spot
+        copy = pltpu.make_async_copy(total.at[spot], o_ref.at[base + l, rows], sem.at[2, k])
+        copy.start()
+        outward.append(copy)
+    for copy in outward:
+        copy.wait()
+
+
+def last(a, b, own, base, held, total):
+    inner = pl.BlockSpec(memory_space=pltpu.VMEM)
+    outer = pl.BlockSpec(memory_space=pl.ANY)
+    extra = [] if held is None else [held]
+    return pl.pallas_call(
+        functools.partial(last_kernel, base),
+        in_specs=[outer, outer, inner] + [outer] * len(extra),
+        out_specs=outer,
+        out_shape=jax.ShapeDtypeStruct((total,) + a.shape[1:], BF),
+        scratch_shapes=[pltpu.VMEM(a.shape, BF)] * 3
+        + [pltpu.SemaphoreType.DMA((3, 2 * a.shape[0]))],
+        input_output_aliases={3: 0} if extra else {},
+        compiler_params=pltpu.CompilerParams(vmem_limit_bytes=16 * a.size),
+        cost_estimate=cost(2 * a.size, 8 * a.size),
+        name="last",
+    )(a, b, own, *extra)
 
 
 def own_kernel(rows_ref, w_ref, o_ref):
@@ -322,6 +371,7 @@
             flops,
             count * (2 * (len(pairs) + 1) * depth * hidden + 2 * n * depth * part + 6 * part * hidden),
         ),
+        compiler_params=pltpu.CompilerParams(vmem_limit_bytes=ROOM),
     )(sc, *args)
 
 
@@ -415,20 +465,15 @@
         weight_grad = weights(
             sc, saved, got[c], sets, places, w_down, c * count, "end", weight_grad
         )
+    hidden_grad = None
     for c in range(chunks):
         base = c * count
-        if c < chunks - 1:
-            total = lax.slice_in_dim(own, base, base + count, axis=0).astype(F32)
-            for part in got[c]:
-                total = total + part[-1].astype(F32)
-            own = lax.dynamic_update_slice_in_dim(own, total.astype(BF), base, axis=0)
-            own, weight_grad, got[-1] = lax.optimization_barrier((own, weight_grad, got[-1]))
+        a, b = got[c][0][-1], got[c][1][-1]
+        mine = lax.slice_in_dim(own, base, base + count, axis=0)
+        if c == 0:
+            mine, weight_grad = lax.optimization_barrier((mine, weight_grad))
+        hidden_grad = last(a, b, mine, base, hidden_grad, local_experts)
     inverse = shares(expert_of, routes[0].T, gates[0].T, n_ep)
-    total = own.astype(F32)
-    for part in got[-1]:
-        wide = ((local_experts - count, 0), (0, 0), (0, 0))
-        total = total + jnp.pad(part[-1], wide).astype(F32)
-    hidden_grad = total.astype(BF)
     back = back.reshape(n_ep, n, local_experts, 1, tokens)
     gate_grad = jnp.sum(back * inverse, axis=(0, 1, 2)).T[None]
     return (hidden_grad.reshape(hidden_saved.shape), gate_grad, weight_grad)

time: 269 us -> 270 us (level)
  local copies, waits for them, and re-layouts: 10.1 us -> 23.3 us
  other arithmetic: 9.96 us -> 1.65 us
  Pallas kernels: 88.8 us -> 80.8 us
  starting transfers between devices: 38.9 us -> 45.3 us
    unnamed x52 -> x78, local copies, waits for them, and re-layouts: 5.85 us -> 15.8 us
    pallas_call x6, Pallas kernels: 43.1 us -> 35.1 us  [weights(): pl.pallas_call(functools.partial(weight_kernel, n, places, base, pairs, m...]
    ppermute x6, waiting for transfers between devices: 5.36 us -> 0.02 us  [local(): pieces[m] = lax.ppermute(pieces[0], 'ep', [(e, e ^ m) for e in range(n_ep)])]
    pallas_call x6, Pallas kernels: 29.3 us -> 24.2 us  [step(): pl.pallas_call(functools.partial(step_kernel, n, t), grid_spec=pltpu.Pref...]
    pallas_call x0 -> x2, Pallas kernels: none -> 5.02 us  [last(): pl.pallas_call(functools.partial(last_kernel, base), in_specs=[outer, out...]
    ppermute x6, waiting for transfers between devices: 28.3 us -> 24.1 us  [local(): got[c][1].append(lax.ppermute(a, 'dp', swaps[1]))]
    ppermute x6, starting transfers between devices: 6.51 us -> 10.4 us  [local(): got[c][0].append(lax.ppermute(b, 'dp', swaps[0]))]
    ppermute x4, waiting for transfers between devices: 26.3 us -> 29.9 us  [local(): got[c][i].append(lax.ppermute(part, 'dp', swaps[i]))]
  transfers between devices with their start and end apart: 34 -> 34, of which waited for: 14 -> 12; matrix products, arithmetic and copies ran while one was open for 4% -> 3% of each run, Pallas kernels for 32% -> 28%
where the time goes in v3:
time: 270 us; the launch traced here: 269 us
  waiting for transfers between devices  117 us (43%)
  Pallas kernels  80.8 us (30%)
  starting transfers between devices  45.3 us (17%)
  local copies, waits for them, and re-layouts  23.3 us (9%)
    ppermute x3, waiting for transfers between devices, local(): arrived[d] = lax.ppermute(packed[d], 'dp', shift)  37.2 us
    pallas_call x6, Pallas kernels, weights(): pl.pallas_call(functools.partial(weight_kernel, n, places, base, pairs, m...  35.1 us
    ppermute x4, waiting for transfers between devices, local(): got[c][i].append(lax.ppermute(part, 'dp', swaps[i]))  29.9 us
    pallas_call x6, Pallas kernels, step(): pl.pallas_call(functools.partial(step_kernel, n, t), grid_spec=pltpu.Pref...  24.2 us
    ppermute x6, waiting for transfers between devices, local(): got[c][1].append(lax.ppermute(a, 'dp', swaps[1]))  24.1 us
    all_to_all x1, waiting for transfers between devices, local(): lax.all_to_all(ready, ('ep', 'dp'), split_axis=0, concat_axis=0, tiled=True)  22.1 us
    unnamed x78, local copies, waits for them, and re-layouts  15.8 us
    ppermute x6, starting transfers between devices, local(): got[c][0].append(lax.ppermute(b, 'dp', swaps[0]))  10.4 us
  transfers between devices with their start and end apart: 34, of which 12 were waited for; matrix products, arithmetic and copies ran while one was open for 3% of the time, Pallas kernels for 28%

profile of v3, /device:TPU:0, one launch (start us, length us, event | category | flops | bytes accessed | tf_op | source)
XLA Modules:
  0.0 269.0 jit_solution(7307084198437066857)
XLA Ops:
  2.5 3.1 %collective-permute-start = (bf16[136,512]{1,0:T(8,128)(2,1)}, bf16[136,512]{1,0:T(8,128)(2,1)S(1)}, u32[]{:S(2)}, u32[]{:S(2)}) collective-permute-start(bf16[136,512]{1,0:T(8,128)(2,1)} %get-tuple-element.51), channel_id=1, source_target_pairs={{0,1},{1,2},{2,3},{3,0},{4,5},{5,6},{6,7},{7,4},{8,9},{9,10},{10,1... | collective-permute-start | bytes 417800 | tf_op jit(solution)/shard_map/ppermute | solution.py:417
  7.6 4.8 %collective-permute-done = bf16[136,512]{1,0:T(8,128)(2,1)S(1)} collective-permute-done((bf16[136,512]{1,0:T(8,128)(2,1)}, bf16[136,512]{1,0:T(8,128)(2,1)S(1)}, u32[]{:S(2)}, u32[]{:S(2)}) %collective-permute-start) | collective-permute-done | bytes 139296 | tf_op jit(solution)/shard_map/ppermute | solution.py:417
  14.0 2.5 collective-permute-start.9
  21.2 2.9 %collective-permute-start.17 = (bf16[136,512]{1,0:T(8,128)(2,1)S(1)}, bf16[136,512]{1,0:T(8,128)(2,1)S(1)}, u32[]{:S(2)}, u32[]{:S(2)}) collective-permute-start(bf16[136,512]{1,0:T(8,128)(2,1)S(1)} %copy-done.37), channel_id=1, source_target_pairs={{0,2},{1,3},{2,0},{3,1},{4,6},{5,7},{6,4},{7,5},{8,10},{9,11},{10,... | collective-permute-start | bytes 417800 | tf_op jit(solution)/shard_map/ppermute | solution.py:417
  24.6 30.9 %collective-permute-done.17 = bf16[136,512]{1,0:T(8,128)(2,1)S(1)} collective-permute-done((bf16[136,512]{1,0:T(8,128)(2,1)S(1)}, bf16[136,512]{1,0:T(8,128)(2,1)S(1)}, u32[]{:S(2)}, u32[]{:S(2)}) %collective-permute-start.17) | collective-permute-done | bytes 139296 | tf_op jit(solution)/shard_map/ppermute | solution.py:417
  59.2 2.6 collective-permute-start.2
  66.2 4.7 %dispatch.2 = (bf16[2,4,384,512]{3,2,1,0:T(8,128)(2,1)}, f32[2,8,8,128]{3,2,1,0:T(8,128)}) custom-call(s32[34]{0:T(128)} %pad_add_fusion.sc, bf16[2,136,512]{2,1,0:T(8,128)(2,1)} %copy-done.21, bf16[2,136,512]{2,1,0:T(8,128)(2,1)} %copy-done.25, bf16[2,136,512]{2,1,0:T(8,128)(2,1)} %copy-done.23, bf16[2,136,512]{2,1,0:T(8,128)(2,1)} %copy-done.27, ...), custom_call_target="tpu_custom_call" | custom-call | flops 402653184 | bytes 5373952 | tf_op jit(solution)/shard_map/dispatch/pallas_call | solution.py:114
  70.9 13.7 %collective-permute-done.14.refs_1_.refs_2_ = bf16[2,384,768]{2,1,0:T(8,128)(2,1)} collective-permute-done((bf16[2,384,768]{2,1,0:T(8,128)(2,1)}, bf16[2,384,768]{2,1,0:T(8,128)(2,1)}, u32[]{:S(2)}, u32[]{:S(2)}) %collective-permute-start.14) | collective-permute-done | bytes 1179680 | tf_op jit(solution)/shard_map/ppermute | solution.py:426
  86.5 3.9 %step.7 = (bf16[2,384,768]{2,1,0:T(8,128)(2,1)}, bf16[2,384,768]{2,1,0:T(8,128)(2,1)}) custom-call(s32[34]{0:T(128)S(1)} %copy-done.18, bf16[2,384,768]{2,1,0:T(8,128)(2,1)} %collective-permute-done.13.refs_0_.refs_1_, bf16[2,384,768]{2,1,0:T(8,128)(2,1)} %collective-permute-done.14.refs_1_.refs_2_, bf16[2,4,384,512]{3,2,1,0:T(8,128)(2,1)S(1)} %copy-done, ...), custom_call_target="tpu_custom_call" | custom-call | flops 1207959552 | bytes 7864320 | tf_op jit(solution)/shard_map/step/pallas_call | solution.py:173
  93.7 16.2 %collective-permute-done.2.refs_1_.refs_2_ = bf16[2,384,768]{2,1,0:T(8,128)(2,1)} collective-permute-done((bf16[2,384,768]{2,1,0:T(8,128)(2,1)}, bf16[2,384,768]{2,1,0:T(8,128)(2,1)}, u32[]{:S(2)}, u32[]{:S(2)}) %collective-permute-start.2) | collective-permute-done | bytes 1179680 | tf_op jit(solution)/shard_map/ppermute | solution.py:426
  109.9 3.9 %step.6 = (bf16[2,384,768]{2,1,0:T(8,128)(2,1)}, bf16[2,384,768]{2,1,0:T(8,128)(2,1)}) custom-call(s32[34]{0:T(128)S(1)} %copy-done.18, bf16[2,384,768]{2,1,0:T(8,128)(2,1)} %collective-permute-done.1.refs_0_.refs_1_, bf16[2,384,768]{2,1,0:T(8,128)(2,1)} %collective-permute-done.2.refs_1_.refs_2_, bf16[2,4,384,512]{3,2,1,0:T(8,128)(2,1)S(1)} %copy-done, ...), custom_call_target="tpu_custom_call" | custom-call | flops 1207959552 | bytes 7864320 | tf_op jit(solution)/shard_map/step/pallas_call | solution.py:173
  119.8 4.6 %dispatch.3 = (bf16[2,4,384,512]{3,2,1,0:T(8,128)(2,1)}, f32[2,8,8,128]{3,2,1,0:T(8,128)}) custom-call(s32[34]{0:T(128)} %pad_add_fusion.sc, bf16[2,136,512]{2,1,0:T(8,128)(2,1)} %copy-done.20, bf16[2,136,512]{2,1,0:T(8,128)(2,1)} %copy-done.29, bf16[2,136,512]{2,1,0:T(8,128)(2,1)} %collective-permute-done.19.refs_2_, bf16[2,136,512]{2,1,0:T(8,128)(2,1)} %copy-done.31, ...), custom_call_target="tpu_custom_call" | custom-call | flops 402653184 | bytes 5373952 | tf_op jit(solution)/shard_map/dispatch/pallas_call | solution.py:114
  124.5 10.7 %collective-permute-done.16.refs_4_.refs_1_ = bf16[2,384,768]{2,1,0:T(8,128)(2,1)} collective-permute-done((bf16[2,384,768]{2,1,0:T(8,128)(2,1)}, bf16[2,384,768]{2,1,0:T(8,128)(2,1)}, u32[]{:S(2)}, u32[]{:S(2)}) %collective-permute-start.16) | collective-permute-done | bytes 1179680 | tf_op jit(solution)/shard_map/ppermute | solution.py:458
  139.0 4.2 %step.9 = (bf16[2,384,768]{2,1,0:T(8,128)(2,1)}, bf16[2,384,768]{2,1,0:T(8,128)(2,1)}) custom-call(s32[34]{0:T(128)S(1)} %copy-done.19, bf16[2,384,768]{2,1,0:T(8,128)(2,1)} %collective-permute-done.15.refs_3_.refs_0_, bf16[2,384,768]{2,1,0:T(8,128)(2,1)} %collective-permute-done.16.refs_4_.refs_1_, bf16[2,4,384,512]{3,2,1,0:T(8,128)(2,1)S(1)} %copy-done.5, ...), custom_call_target="tpu_custom_call" | custom-call | flops 1207959552 | bytes 7864320 | tf_op jit(solution)/shard_map/step/pallas_call | solution.py:173
  144.9 9.9 %shard_map.85 = (f32[512,3072]{1,0:T(8,128)}, f32[2,32,128]{2,1,0:T(8,128)S(1)}) custom-call(s32[34]{0:T(128)S(1)} %copy-done.19, bf16[4,384,768]{2,1,0:T(8,128)(2,1)S(1)} %bitcast.24, bf16[2,384,768]{2,1,0:T(8,128)(2,1)} %collective-permute-done.13.refs_0_.refs_1_, bf16[2,384,768]{2,1,0:T(8,128)(2,1)} %collective-permute-done.14.refs_1_.refs_2_, ...), custom_call_target="tpu_custom_call" | custom-call | flops 3019898880 | bytes 13762560 | tf_op jit(solution)/shard_map/pallas_call | solution.py:363
  154.8 5.7 %collective-permute-done.12.refs_1_.refs_4_ = bf16[2,384,768]{2,1,0:T(8,128)(2,1)} collective-permute-done((bf16[2,384,768]{2,1,0:T(8,128)(2,1)}, bf16[2,384,768]{2,1,0:T(8,128)(2,1)}, u32[]{:S(2)}, u32[]{:S(2)}) %collective-permute-start.12) | collective-permute-done | bytes 1179680 | tf_op jit(solution)/shard_map/ppermute | solution.py:458
  160.5 3.9 %step.8 = (bf16[2,384,768]{2,1,0:T(8,128)(2,1)}, bf16[2,384,768]{2,1,0:T(8,128)(2,1)}) custom-call(s32[34]{0:T(128)S(1)} %copy-done.19, bf16[2,384,768]{2,1,0:T(8,128)(2,1)} %collective-permute-done.11.refs_0_.refs_3_, bf16[2,384,768]{2,1,0:T(8,128)(2,1)} %collective-permute-done.12.refs_1_.refs_4_, bf16[2,4,384,512]{3,2,1,0:T(8,128)(2,1)S(1)} %copy-done.6, ...), custom_call_target="tpu_custom_call" | custom-call | flops 1207959552 | bytes 7864320 | tf_op jit(solution)/shard_map/step/pallas_call | solution.py:173
  166.2 5.2 %own_part.1 = bf16[4,384,768]{2,1,0:T(8,128)(2,1)} custom-call(bf16[2,4,384,512]{3,2,1,0:T(8,128)(2,1)} %get-tuple-element.62.refs_6_.refs_2_.refs_3_.rows_ref, bf16[512,3072]{1,0:T(8,128)(2,1)} %refs_4_.11), custom_call_target="tpu_custom_call" | custom-call | flops 1207959552 | bytes 7077888 | tf_op jit(solution)/shard_map/own_part/pallas_call | solution.py:252
  176.8 9.9 %shard_map.87 = (f32[512,3072]{1,0:T(8,128)}, f32[2,32,128]{2,1,0:T(8,128)S(1)}) custom-call(s32[34]{0:T(128)S(1)} %copy-done.19, bf16[4,384,768]{2,1,0:T(8,128)(2,1)S(1)} %bitcast.25, bf16[2,384,768]{2,1,0:T(8,128)(2,1)} %collective-permute-done.1.refs_0_.refs_1_, ...), custom_call_target="tpu_custom_call", output_to_operand_aliasing={{0}: (11, {})} | custom-call | flops 3019898880 | bytes 13762560 | tf_op jit(solution)/shard_map/pallas_call | solution.py:363
  186.7 4.2 %step.11 = (bf16[2,384,768]{2,1,0:T(8,128)(2,1)}, bf16[2,384,768]{2,1,0:T(8,128)(2,1)}) custom-call(s32[34]{0:T(128)S(1)} %copy-done.19, bf16[2,384,768]{2,1,0:T(8,128)(2,1)} %collective-permute-done.30.refs_0_, bf16[2,384,768]{2,1,0:T(8,128)(2,1)} %collective-permute-done.27.refs_0_.refs_1_, bf16[2,4,384,512]{3,2,1,0:T(8,128)(2,1)S(1)} %copy-done.1, ...), custom_call_target="tpu_custom_call" | custom-call | flops 1207959552 | bytes 7864320 | tf_op jit(solution)/shard_map/step/pallas_call | solution.py:173
  192.7 7.7 %collective-permute-start.32 = (bf16[2,384,768]{2,1,0:T(8,128)(2,1)}, bf16[2,384,768]{2,1,0:T(8,128)(2,1)}, u32[]{:S(2)}, u32[]{:S(2)}) collective-permute-start(bf16[2,384,768]{2,1,0:T(8,128)(2,1)} %get-tuple-element.84), channel_id=1, source_target_pairs={{0,1},{2,3},{1,0},{3,2},{4,5},{6,7},{5,4},{7,6},{8,9},{10,11},{9,8... | collective-permute-start | bytes 3538952 | tf_op jit(solution)/shard_map/ppermute | solution.py:458
  200.4 2.9 %shard_map.86 = f32[2,32,128]{2,1,0:T(8,128)S(1)} custom-call(s32[34]{0:T(128)S(1)} %copy-done.19, bf16[2,384,768]{2,1,0:T(8,128)(2,1)} %collective-permute-done.27.refs_0_.refs_1_, bf16[2,4,384,512]{3,2,1,0:T(8,128)(2,1)S(1)} %copy-done.1, bf16[2,4,384,512]{3,2,1,0:T(8,128)(2,1)S(1)} %copy-done.8, ...), custom_call_target="tpu_custom_call", output_to_operand_aliasing={{}: (7, {})} | custom-call | flops 1207959552 | bytes 10223616 | tf_op jit(solution)/shard_map/pallas_call | solution.py:363
  203.3 7.7 %collective-permute-done.26.refs_0_.refs_1_ = bf16[2,384,768]{2,1,0:T(8,128)(2,1)} collective-permute-done((bf16[2,384,768]{2,1,0:T(8,128)(2,1)}, bf16[2,384,768]{2,1,0:T(8,128)(2,1)}, u32[]{:S(2)}, u32[]{:S(2)}) %collective-permute-start.26) | collective-permute-done | bytes 1179680 | tf_op jit(solution)/shard_map/ppermute | solution.py:458
  211.0 2.9 %shard_map.88 = f32[2,32,128]{2,1,0:T(8,128)S(1)} custom-call(s32[34]{0:T(128)S(1)} %copy-done.19, bf16[2,384,768]{2,1,0:T(8,128)(2,1)} %collective-permute-done.26.refs_0_.refs_1_, bf16[2,4,384,512]{3,2,1,0:T(8,128)(2,1)S(1)} %copy-done.1, bf16[2,4,384,512]{3,2,1,0:T(8,128)(2,1)S(1)} %copy-done.8, ...), custom_call_target="tpu_custom_call", output_to_operand_aliasing={{}: (7, {})} | custom-call | flops 1207959552 | bytes 10223616 | tf_op jit(solution)/shard_map/pallas_call | solution.py:363
  214.0 3.9 %step.10 = (bf16[2,384,768]{2,1,0:T(8,128)(2,1)}, bf16[2,384,768]{2,1,0:T(8,128)(2,1)}) custom-call(s32[34]{0:T(128)S(1)} %copy-done.19, bf16[2,384,768]{2,1,0:T(8,128)(2,1)} %collective-permute-done.25.refs_0_, bf16[2,384,768]{2,1,0:T(8,128)(2,1)} %collective-permute-done.26.refs_0_.refs_1_, bf16[2,4,384,512]{3,2,1,0:T(8,128)(2,1)S(1)} %copy-done.1, ...), custom_call_target="tpu_custom_call" | custom-call | flops 1207959552 | bytes 7864320 | tf_op jit(solution)/shard_map/step/pallas_call | solution.py:173
  222.1 4.8 %shard_map.89.refs_3_ = f32[512,3072]{1,0:T(8,128)} custom-call(s32[34]{0:T(128)S(1)} %copy-done.19, bf16[2,384,768]{2,1,0:T(8,128)(2,1)} %collective-permute-done.27.refs_0_.refs_1_, bf16[2,4,384,512]{3,2,1,0:T(8,128)(2,1)S(1)} %copy-done.1, bf16[2,4,384,512]{3,2,1,0:T(8,128)(2,1)S(1)} %copy-done.9, ...), custom_call_target="tpu_custom_call", output_to_operand_aliasing={{}: (4, {})} | custom-call | flops 1207959552 | bytes 10223616 | tf_op jit(solution)/shard_map/pallas_call | solution.py:363
  227.5 3.9 %all-to-all-start = ((f32[32,4,128]{2,1,0:T(4,128)}), f32[32,4,128]{2,1,0:T(4,128)S(1)}, u32[]{:S(2)}, u32[]{:S(2)}) async-start(f32[32,4,128]{2,1,0:T(4,128)} %copy.18), calls=%async_computation | async-start | bytes 131072 | tf_op jit(solution)/shard_map/all_to_all | solution.py:456
  231.5 3.3 %fusion = (bf16[2,384,768]{2,1,0:T(8,128)(2,1)}, bf16[2,384,768]{2,1,0:T(8,128)(2,1)}) fusion(bf16[4,384,768]{2,1,0:T(8,128)(2,1)} %own_part.1), kind=kLoop, calls=%fused_computation.9 | loop fusion | bytes 4718592 | tf_op jit(solution)/shard_map/slice | solution.py:472
  234.8 4.8 %shard_map.90 = f32[512,3072]{1,0:T(8,128)} custom-call(s32[34]{0:T(128)S(1)} %copy-done.19, bf16[2,384,768]{2,1,0:T(8,128)(2,1)} %collective-permute-done.26.refs_0_.refs_1_, bf16[2,4,384,512]{3,2,1,0:T(8,128)(2,1)S(1)} %copy-done.1, bf16[2,4,384,512]{3,2,1,0:T(8,128)(2,1)S(1)} %copy-done.10, ...), custom_call_target="tpu_custom_call", output_to_operand_aliasing={{}: (4, {})} | custom-call | flops 1207959552 | bytes 10223616 | tf_op jit(solution)/shard_map/pallas_call | solution.py:363
  239.6 22.1 %all-to-all-done = f32[32,4,128]{2,1,0:T(4,128)S(1)} async-done(((f32[32,4,128]{2,1,0:T(4,128)}), f32[32,4,128]{2,1,0:T(4,128)S(1)}, u32[]{:S(2)}, u32[]{:S(2)}) %all-to-all-start) | async-done | bytes 65568 | tf_op jit(solution)/shard_map/all_to_all | solution.py:456
  263.8 2.5 last.2.rest_0_
  266.3 2.5 last.3
  (145 shorter events, 51.2 us)
Async XLA Ops:
  2.5 9.8 %collective-permute-start = (bf16[136,512]{1,0:T(8,128)(2,1)}, bf16[136,512]{1,0:T(8,128)(2,1)S(1)}, u32[]{:S(2)}, u32[]{:S(2)}) collective-permute-start(bf16[136,512]{1,0:T(8,128)(2,1)} %get-tuple-element.51), channel_id=1, source_target_pairs={{0,1},{1,2},{2,3},{3,0},{4,5},{5,6},{6,7},{7,4},{8,9},{9,10},{10,1... | collective-permute-start | bytes 417800 | tf_op jit(solution)/shard_map/ppermute | solution.py:417
  5.6 8.3 %collective-permute-start.3 = (bf16[136,512]{1,0:T(8,128)(2,1)}, bf16[136,512]{1,0:T(8,128)(2,1)S(1)}, u32[]{:S(2)}, u32[]{:S(2)}) collective-permute-start(bf16[136,512]{1,0:T(8,128)(2,1)} %get-tuple-element.54), channel_id=1, source_target_pairs={{0,3},{1,0},{2,1},{3,2},{4,7},{5,4},{6,5},{7,6},{8,11},{9,8},{10,9... | collective-permute-start | bytes 417800 | tf_op jit(solution)/shard_map/ppermute | solution.py:417
  14.0 41.5 %collective-permute-start.9 = (bf16[2,136,512]{2,1,0:T(8,128)(2,1)S(1)}, bf16[2,136,512]{2,1,0:T(8,128)(2,1)S(1)}, u32[]{:S(2)}, u32[]{:S(2)}) collective-permute-start(bf16[2,136,512]{2,1,0:T(8,128)(2,1)S(1)} %pad_maximum_fusion.refs_0_), channel_id=1, source_target_pairs={{0,24},{4,28},{8,16},{12,20},{16,8},{20,12},{24,0},{28,4},{1,25},{... | collective-permute-start | bytes 835592 | tf_op jit(solution)/shard_map/ppermute | solution.py:435
  16.5 39.1 %collective-permute-start.5 = (bf16[2,136,512]{2,1,0:T(8,128)(2,1)S(1)}, bf16[2,136,512]{2,1,0:T(8,128)(2,1)S(1)}, u32[]{:S(2)}, u32[]{:S(2)}) collective-permute-start(bf16[2,136,512]{2,1,0:T(8,128)(2,1)S(1)} %pad_maximum_fusion.refs_0_), channel_id=1, source_target_pairs={{0,8},{4,12},{8,0},{12,4},{16,24},{20,28},{24,16},{28,20},{1,9},{5... | collective-permute-start | bytes 835592 | tf_op jit(solution)/shard_map/ppermute | solution.py:435
  19.4 45.5 %collective-permute-start.13 = (bf16[2,384,768]{2,1,0:T(8,128)(2,1)}, bf16[2,384,768]{2,1,0:T(8,128)(2,1)}, u32[]{:S(2)}, u32[]{:S(2)}) collective-permute-start(bf16[2,384,768]{2,1,0:T(8,128)(2,1)} %slice.13), channel_id=1, source_target_pairs={{1,2},{2,1},{5,6},{6,5},{9,10},{10,9},{13,14},{14,13},{17,18},{18,... | collective-permute-start | bytes 3538952 | tf_op jit(solution)/shard_map/ppermute | solution.py:426
  21.2 34.3 %collective-permute-start.17 = (bf16[136,512]{1,0:T(8,128)(2,1)S(1)}, bf16[136,512]{1,0:T(8,128)(2,1)S(1)}, u32[]{:S(2)}, u32[]{:S(2)}) collective-permute-start(bf16[136,512]{1,0:T(8,128)(2,1)S(1)} %copy-done.37), channel_id=1, source_target_pairs={{0,2},{1,3},{2,0},{3,1},{4,6},{5,7},{6,4},{7,5},{8,10},{9,11},{10,... | collective-permute-start | bytes 417800 | tf_op jit(solution)/shard_map/ppermute | solution.py:417
  24.1 33.1 %collective-permute-start.7 = (bf16[2,136,512]{2,1,0:T(8,128)(2,1)S(1)}, bf16[2,136,512]{2,1,0:T(8,128)(2,1)S(1)}, u32[]{:S(2)}, u32[]{:S(2)}) collective-permute-start(bf16[2,136,512]{2,1,0:T(8,128)(2,1)S(1)} %pad_maximum_fusion.refs_0_), channel_id=1, source_target_pairs={{0,16},{4,20},{8,24},{12,28},{16,0},{20,4},{24,8},{28,12},{1,17},{... | collective-permute-start | bytes 835592 | tf_op jit(solution)/shard_map/ppermute | solution.py:435
  55.5 29.2 %collective-permute-start.14 = (bf16[2,384,768]{2,1,0:T(8,128)(2,1)}, bf16[2,384,768]{2,1,0:T(8,128)(2,1)}, u32[]{:S(2)}, u32[]{:S(2)}) collective-permute-start(bf16[2,384,768]{2,1,0:T(8,128)(2,1)} %slice.13), channel_id=1, source_target_pairs={{0,1},{2,3},{1,0},{3,2},{4,5},{6,7},{5,4},{7,6},{8,9},{10,11},{9,8... | collective-permute-start | bytes 3538952 | tf_op jit(solution)/shard_map/ppermute | solution.py:426
  55.5 3.5 %collective-permute-start.4 = (bf16[2,136,512]{2,1,0:T(8,128)(2,1)S(1)}, bf16[2,136,512]{2,1,0:T(8,128)(2,1)S(1)}, u32[]{:S(2)}, u32[]{:S(2)}) collective-permute-start(bf16[2,136,512]{2,1,0:T(8,128)(2,1)S(1)} %pad_maximum_fusion.refs_0_), channel_id=1, source_target_pairs={{0,4},{4,0},{8,12},{12,8},{16,20},{20,16},{24,28},{28,24},{1,5},{5... | collective-permute-start | bytes 835592 | tf_op jit(solution)/shard_map/ppermute | solution.py:437
  55.6 3.5 %collective-permute-start.10 = (bf16[2,136,512]{2,1,0:T(8,128)(2,1)S(1)}, bf16[2,136,512]{2,1,0:T(8,128)(2,1)S(1)}, u32[]{:S(2)}, u32[]{:S(2)}) collective-permute-start(bf16[2,136,512]{2,1,0:T(8,128)(2,1)S(1)} %collective-permute-done.9.refs_6_), channel_id=1, source_target_pairs={{0,4},{4,0},{8,12},{12,8},{16,20},{20,16},{24,28},{28,24},{1,5},{5... | collective-permute-start | bytes 835592 | tf_op jit(solution)/shard_map/ppermute | solution.py:437
  57.2 36.5 %collective-permute-start.1 = (bf16[2,384,768]{2,1,0:T(8,128)(2,1)}, bf16[2,384,768]{2,1,0:T(8,128)(2,1)}, u32[]{:S(2)}, u32[]{:S(2)}) collective-permute-start(bf16[2,384,768]{2,1,0:T(8,128)(2,1)} %slice.12), channel_id=1, source_target_pairs={{1,2},{2,1},{5,6},{6,5},{9,10},{10,9},{13,14},{14,13},{17,18},{18,... | collective-permute-start | bytes 3538952 | tf_op jit(solution)/shard_map/ppermute | solution.py:426
  59.1 2.7 collective-permute-start.6
  59.2 50.8 %collective-permute-start.2 = (bf16[2,384,768]{2,1,0:T(8,128)(2,1)}, bf16[2,384,768]{2,1,0:T(8,128)(2,1)}, u32[]{:S(2)}, u32[]{:S(2)}) collective-permute-start(bf16[2,384,768]{2,1,0:T(8,128)(2,1)} %slice.12), channel_id=1, source_target_pairs={{0,1},{2,3},{1,0},{3,2},{4,5},{6,7},{5,4},{7,6},{8,9},{10,11},{9,8... | collective-permute-start | bytes 3538952 | tf_op jit(solution)/shard_map/ppermute | solution.py:426
  63.3 28.9 %collective-permute-start.19 = (bf16[2,136,512]{2,1,0:T(8,128)(2,1)S(1)}, bf16[2,136,512]{2,1,0:T(8,128)(2,1)}, u32[]{:S(2)}, u32[]{:S(2)}) collective-permute-start(bf16[2,136,512]{2,1,0:T(8,128)(2,1)S(1)} %pad_maximum_fusion.1.refs_0_), channel_id=1, source_target_pairs={{0,8},{4,12},{8,0},{12,4},{16,24},{20,28},{24,16},{28,20},{1,9},{5... | collective-permute-start | bytes 835592 | tf_op jit(solution)/shard_map/ppermute | solution.py:435
  64.9 27.3 %collective-permute-start.21 = (bf16[2,136,512]{2,1,0:T(8,128)(2,1)S(1)}, bf16[2,136,512]{2,1,0:T(8,128)(2,1)}, u32[]{:S(2)}, u32[]{:S(2)}) collective-permute-start(bf16[2,136,512]{2,1,0:T(8,128)(2,1)S(1)} %pad_maximum_fusion.1.refs_0_), channel_id=1, source_target_pairs={{0,16},{4,20},{8,24},{12,28},{16,0},{20,4},{24,8},{28,12},{1,17},{... | collective-permute-start | bytes 835592 | tf_op jit(solution)/shard_map/ppermute | solution.py:435
  90.5 34.0 %collective-permute-start.15 = (bf16[2,384,768]{2,1,0:T(8,128)(2,1)}, bf16[2,384,768]{2,1,0:T(8,128)(2,1)}, u32[]{:S(2)}, u32[]{:S(2)}) collective-permute-start(bf16[2,384,768]{2,1,0:T(8,128)(2,1)} %get-tuple-element.58), channel_id=1, source_target_pairs={{1,2},{2,1},{5,6},{6,5},{9,10},{10,9},{13,14},{14,13},{17,18},{18,... | collective-permute-start | bytes 3538952 | tf_op jit(solution)/shard_map/ppermute | solution.py:459
  92.2 43.0 %collective-permute-start.16 = (bf16[2,384,768]{2,1,0:T(8,128)(2,1)}, bf16[2,384,768]{2,1,0:T(8,128)(2,1)}, u32[]{:S(2)}, u32[]{:S(2)}) collective-permute-start(bf16[2,384,768]{2,1,0:T(8,128)(2,1)} %get-tuple-element.59), channel_id=1, source_target_pairs={{0,1},{2,3},{1,0},{3,2},{4,5},{6,7},{5,4},{7,6},{8,9},{10,11},{9,8... | collective-permute-start | bytes 3538952 | tf_op jit(solution)/shard_map/ppermute | solution.py:458
  92.2 21.6 %collective-permute-start.23 = (bf16[2,136,512]{2,1,0:T(8,128)(2,1)S(1)}, bf16[2,136,512]{2,1,0:T(8,128)(2,1)S(1)}, u32[]{:S(2)}, u32[]{:S(2)}) collective-permute-start(bf16[2,136,512]{2,1,0:T(8,128)(2,1)S(1)} %pad_maximum_fusion.1.refs_0_), channel_id=1, source_target_pairs={{0,24},{4,28},{8,16},{12,20},{16,8},{20,12},{24,0},{28,4},{1,25},{... | collective-permute-start | bytes 835592 | tf_op jit(solution)/shard_map/ppermute | solution.py:435
  93.7 21.8 %collective-permute-start.18 = (bf16[2,136,512]{2,1,0:T(8,128)(2,1)S(1)}, bf16[2,136,512]{2,1,0:T(8,128)(2,1)S(1)}, u32[]{:S(2)}, u32[]{:S(2)}) collective-permute-start(bf16[2,136,512]{2,1,0:T(8,128)(2,1)S(1)} %pad_maximum_fusion.1.refs_0_), channel_id=1, source_target_pairs={{0,4},{4,0},{8,12},{12,8},{16,20},{20,16},{24,28},{28,24},{1,5},{5... | collective-permute-start | bytes 835592 | tf_op jit(solution)/shard_map/ppermute | solution.py:437
  109.9 5.6 %collective-permute-start.20 = (bf16[2,136,512]{2,1,0:T(8,128)(2,1)}, bf16[2,136,512]{2,1,0:T(8,128)(2,1)S(1)}, u32[]{:S(2)}, u32[]{:S(2)}) collective-permute-start(bf16[2,136,512]{2,1,0:T(8,128)(2,1)} %collective-permute-done.19.refs_2_), channel_id=1, source_target_pairs={{0,4},{4,0},{8,12},{12,8},{16,20},{20,16},{24,28},{28,24},{1,5},{5... | collective-permute-start | bytes 835592 | tf_op jit(solution)/shard_map/ppermute | solution.py:437
  113.9 40.9 %collective-permute-start.11 = (bf16[2,384,768]{2,1,0:T(8,128)(2,1)}, bf16[2,384,768]{2,1,0:T(8,128)(2,1)}, u32[]{:S(2)}, u32[]{:S(2)}) collective-permute-start(bf16[2,384,768]{2,1,0:T(8,128)(2,1)} %get-tuple-element.56), channel_id=1, source_target_pairs={{1,2},{2,1},{5,6},{6,5},{9,10},{10,9},{13,14},{14,13},{17,18},{18,... | collective-permute-start | bytes 3538952 | tf_op jit(solution)/shard_map/ppermute | solution.py:459
  115.6 44.9 %collective-permute-start.12 = (bf16[2,384,768]{2,1,0:T(8,128)(2,1)}, bf16[2,384,768]{2,1,0:T(8,128)(2,1)}, u32[]{:S(2)}, u32[]{:S(2)}) collective-permute-start(bf16[2,384,768]{2,1,0:T(8,128)(2,1)} %get-tuple-element.57), channel_id=1, source_target_pairs={{0,1},{2,3},{1,0},{3,2},{4,5},{6,7},{5,4},{7,6},{8,9},{10,11},{9,8... | collective-permute-start | bytes 3538952 | tf_op jit(solution)/shard_map/ppermute | solution.py:458
  115.6 2.0 collective-permute-start.22
  143.2 43.4 %collective-permute-start.27 = (bf16[2,384,768]{2,1,0:T(8,128)(2,1)}, bf16[2,384,768]{2,1,0:T(8,128)(2,1)}, u32[]{:S(2)}, u32[]{:S(2)}) collective-permute-start(bf16[2,384,768]{2,1,0:T(8,128)(2,1)} %get-tuple-element.70), channel_id=1, source_target_pairs={{0,1},{2,3},{1,0},{3,2},{4,5},{6,7},{5,4},{7,6},{8,9},{10,11},{9,8... | collective-permute-start | bytes 3538952 | tf_op jit(solution)/shard_map/ppermute | solution.py:458
  143.2 43.4 %collective-permute-start.30 = (bf16[2,384,768]{2,1,0:T(8,128)(2,1)}, bf16[2,384,768]{2,1,0:T(8,128)(2,1)}, u32[]{:S(2)}, u32[]{:S(2)}) collective-permute-start(bf16[2,384,768]{2,1,0:T(8,128)(2,1)} %get-tuple-element.79), channel_id=1, source_target_pairs={{1,2},{2,1},{5,6},{6,5},{9,10},{10,9},{13,14},{14,13},{17,18},{18,... | collective-permute-start | bytes 3538952 | tf_op jit(solution)/shard_map/ppermute | solution.py:459
  164.4 46.6 %collective-permute-start.26 = (bf16[2,384,768]{2,1,0:T(8,128)(2,1)}, bf16[2,384,768]{2,1,0:T(8,128)(2,1)}, u32[]{:S(2)}, u32[]{:S(2)}) collective-permute-start(bf16[2,384,768]{2,1,0:T(8,128)(2,1)} %get-tuple-element.69), channel_id=1, source_target_pairs={{0,1},{2,3},{1,0},{3,2},{4,5},{6,7},{5,4},{7,6},{8,9},{10,11},{9,8... | collective-permute-start | bytes 3538952 | tf_op jit(solution)/shard_map/ppermute | solution.py:458
  164.4 49.6 %collective-permute-start.25 = (bf16[2,384,768]{2,1,0:T(8,128)(2,1)}, bf16[2,384,768]{2,1,0:T(8,128)(2,1)}, u32[]{:S(2)}, u32[]{:S(2)}) collective-permute-start(bf16[2,384,768]{2,1,0:T(8,128)(2,1)} %get-tuple-element.68), channel_id=1, source_target_pairs={{1,2},{2,1},{5,6},{6,5},{9,10},{10,9},{13,14},{14,13},{17,18},{18,... | collective-permute-start | bytes 3538952 | tf_op jit(solution)/shard_map/ppermute | solution.py:459
  190.9 71.5 %collective-permute-start.31 = (bf16[2,384,768]{2,1,0:T(8,128)(2,1)}, bf16[2,384,768]{2,1,0:T(8,128)(2,1)}, u32[]{:S(2)}, u32[]{:S(2)}) collective-permute-start(bf16[2,384,768]{2,1,0:T(8,128)(2,1)} %get-tuple-element.83), channel_id=1, source_target_pairs={{1,2},{2,1},{5,6},{6,5},{9,10},{10,9},{13,14},{14,13},{17,18},{18,... | collective-permute-start | bytes 3538952 | tf_op jit(solution)/shard_map/ppermute | solution.py:459
  192.7 69.7 %collective-permute-start.32 = (bf16[2,384,768]{2,1,0:T(8,128)(2,1)}, bf16[2,384,768]{2,1,0:T(8,128)(2,1)}, u32[]{:S(2)}, u32[]{:S(2)}) collective-permute-start(bf16[2,384,768]{2,1,0:T(8,128)(2,1)} %get-tuple-element.84), channel_id=1, source_target_pairs={{0,1},{2,3},{1,0},{3,2},{4,5},{6,7},{5,4},{7,6},{8,9},{10,11},{9,8... | collective-permute-start | bytes 3538952 | tf_op jit(solution)/shard_map/ppermute | solution.py:458
  218.0 48.3 %collective-permute-start.28 = (bf16[2,384,768]{2,1,0:T(8,128)(2,1)}, bf16[2,384,768]{2,1,0:T(8,128)(2,1)}, u32[]{:S(2)}, u32[]{:S(2)}) collective-permute-start(bf16[2,384,768]{2,1,0:T(8,128)(2,1)} %get-tuple-element.76), channel_id=1, source_target_pairs={{1,2},{2,1},{5,6},{6,5},{9,10},{10,9},{13,14},{14,13},{17,18},{18,... | collective-permute-start | bytes 3538952 | tf_op jit(solution)/shard_map/ppermute | solution.py:459
  219.7 46.6 %collective-permute-start.29 = (bf16[2,384,768]{2,1,0:T(8,128)(2,1)}, bf16[2,384,768]{2,1,0:T(8,128)(2,1)}, u32[]{:S(2)}, u32[]{:S(2)}) collective-permute-start(bf16[2,384,768]{2,1,0:T(8,128)(2,1)} %get-tuple-element.77), channel_id=1, source_target_pairs={{0,1},{2,3},{1,0},{3,2},{4,5},{6,7},{5,4},{7,6},{8,9},{10,11},{9,8... | collective-permute-start | bytes 3538952 | tf_op jit(solution)/shard_map/ppermute | solution.py:458
  227.5 34.2 %all-to-all-start = ((f32[32,4,128]{2,1,0:T(4,128)}), f32[32,4,128]{2,1,0:T(4,128)S(1)}, u32[]{:S(2)}, u32[]{:S(2)}) async-start(f32[32,4,128]{2,1,0:T(4,128)} %copy.18), calls=%async_computation | async-start | bytes 131072 | tf_op jit(solution)/shard_map/all_to_all | solution.py:456
  (41 other events, 392.6 us)

commit v4 on v3

--- a/solution.py
+++ b/solution.py
@@ -11,6 +11,7 @@
 BF = jnp.bfloat16
 F32 = jnp.float32
 CHUNKS = 2
+PIECES = 4
 ROOM = 32 << 20
 
 
@@ -197,7 +198,7 @@
 def last_kernel(base, a_ref, b_ref, own_ref, *rest):
     o_ref, a_in, b_in, total, sem = rest[-5:]
     count, depth, _ = own_ref.shape
-    cut = 2 if depth % 32 == 0 else 1
+    cut = PIECES if depth % (16 * PIECES) == 0 else 1
     high = depth // cut
     spots = [(l, pl.ds(h * high, high)) for l in range(count) for h in range(cut)]
     inward = []
@@ -233,7 +234,7 @@
         out_specs=outer,
         out_shape=jax.ShapeDtypeStruct((total,) + a.shape[1:], BF),
         scratch_shapes=[pltpu.VMEM(a.shape, BF)] * 3
-        + [pltpu.SemaphoreType.DMA((3, 2 * a.shape[0]))],
+        + [pltpu.SemaphoreType.DMA((3, PIECES * a.shape[0]))],
         input_output_aliases={3: 0} if extra else {},
         compiler_params=pltpu.CompilerParams(vmem_limit_bytes=16 * a.size),
         cost_estimate=cost(2 * a.size, 8 * a.size),

time: 270 us -> 270 us (level)
  no operation moved by 1% of the time
where the time goes in v4:
time: 270 us; the launch traced here: 269 us
  waiting for transfers between devices  117 us (43%)
  Pallas kernels  81 us (30%)
  starting transfers between devices  45.3 us (17%)
  local copies, waits for them, and re-layouts  23.3 us (9%)
    ppermute x3, waiting for transfers between devices, local(): arrived[d] = lax.ppermute(packed[d], 'dp', shift)  37.2 us
    pallas_call x6, Pallas kernels, weights(): pl.pallas_call(functools.partial(weight_kernel, n, places, base, pairs, m...  35.1 us
    ppermute x4, waiting for transfers between devices, local(): got[c][i].append(lax.ppermute(part, 'dp', swaps[i]))  29.9 us
    pallas_call x6, Pallas kernels, step(): pl.pallas_call(functools.partial(step_kernel, n, t), grid_spec=pltpu.Pref...  24.2 us
    ppermute x6, waiting for transfers between devices, local(): got[c][1].append(lax.ppermute(a, 'dp', swaps[1]))  24.1 us
    all_to_all x1, waiting for transfers between devices, local(): lax.all_to_all(ready, ('ep', 'dp'), split_axis=0, concat_axis=0, tiled=True)  22.1 us
    unnamed x78, local copies, waits for them, and re-layouts  15.8 us
    ppermute x6, starting transfers between devices, local(): got[c][0].append(lax.ppermute(b, 'dp', swaps[0]))  10.4 us
  transfers between devices with their start and end apart: 34, of which 12 were waited for; matrix products, arithmetic and copies ran while one was open for 3% of the time, Pallas kernels for 28%

profile of v4, /device:TPU:0, one launch (start us, length us, event | category | flops | bytes accessed | tf_op | source)
XLA Modules:
  0.0 269.3 jit_solution(13856135213532830202)
XLA Ops:
  2.5 3.1 %collective-permute-start = (bf16[136,512]{1,0:T(8,128)(2,1)}, bf16[136,512]{1,0:T(8,128)(2,1)S(1)}, u32[]{:S(2)}, u32[]{:S(2)}) collective-permute-start(bf16[136,512]{1,0:T(8,128)(2,1)} %get-tuple-element.51), channel_id=1, source_target_pairs={{0,1},{1,2},{2,3},{3,0},{4,5},{5,6},{6,7},{7,4},{8,9},{9,10},{10,1... | collective-permute-start | bytes 417800 | tf_op jit(solution)/shard_map/ppermute | solution.py:418
  7.6 4.8 %collective-permute-done = bf16[136,512]{1,0:T(8,128)(2,1)S(1)} collective-permute-done((bf16[136,512]{1,0:T(8,128)(2,1)}, bf16[136,512]{1,0:T(8,128)(2,1)S(1)}, u32[]{:S(2)}, u32[]{:S(2)}) %collective-permute-start) | collective-permute-done | bytes 139296 | tf_op jit(solution)/shard_map/ppermute | solution.py:418
  14.0 2.5 collective-permute-start.9
  21.2 2.9 %collective-permute-start.17 = (bf16[136,512]{1,0:T(8,128)(2,1)S(1)}, bf16[136,512]{1,0:T(8,128)(2,1)S(1)}, u32[]{:S(2)}, u32[]{:S(2)}) collective-permute-start(bf16[136,512]{1,0:T(8,128)(2,1)S(1)} %copy-done.37), channel_id=1, source_target_pairs={{0,2},{1,3},{2,0},{3,1},{4,6},{5,7},{6,4},{7,5},{8,10},{9,11},{10,... | collective-permute-start | bytes 417800 | tf_op jit(solution)/shard_map/ppermute | solution.py:418
  24.6 30.9 %collective-permute-done.17 = bf16[136,512]{1,0:T(8,128)(2,1)S(1)} collective-permute-done((bf16[136,512]{1,0:T(8,128)(2,1)S(1)}, bf16[136,512]{1,0:T(8,128)(2,1)S(1)}, u32[]{:S(2)}, u32[]{:S(2)}) %collective-permute-start.17) | collective-permute-done | bytes 139296 | tf_op jit(solution)/shard_map/ppermute | solution.py:418
  59.2 2.6 collective-permute-start.2
  66.2 4.7 %dispatch.2 = (bf16[2,4,384,512]{3,2,1,0:T(8,128)(2,1)}, f32[2,8,8,128]{3,2,1,0:T(8,128)}) custom-call(s32[34]{0:T(128)} %pad_add_fusion.sc, bf16[2,136,512]{2,1,0:T(8,128)(2,1)} %copy-done.21, bf16[2,136,512]{2,1,0:T(8,128)(2,1)} %copy-done.25, bf16[2,136,512]{2,1,0:T(8,128)(2,1)} %copy-done.23, bf16[2,136,512]{2,1,0:T(8,128)(2,1)} %copy-done.27, ...), custom_call_target="tpu_custom_call" | custom-call | flops 402653184 | bytes 5373952 | tf_op jit(solution)/shard_map/dispatch/pallas_call | solution.py:115
  70.9 13.7 %collective-permute-done.14.refs_1_.refs_2_ = bf16[2,384,768]{2,1,0:T(8,128)(2,1)} collective-permute-done((bf16[2,384,768]{2,1,0:T(8,128)(2,1)}, bf16[2,384,768]{2,1,0:T(8,128)(2,1)}, u32[]{:S(2)}, u32[]{:S(2)}) %collective-permute-start.14) | collective-permute-done | bytes 1179680 | tf_op jit(solution)/shard_map/ppermute | solution.py:427
  86.5 3.9 %step.7 = (bf16[2,384,768]{2,1,0:T(8,128)(2,1)}, bf16[2,384,768]{2,1,0:T(8,128)(2,1)}) custom-call(s32[34]{0:T(128)S(1)} %copy-done.18, bf16[2,384,768]{2,1,0:T(8,128)(2,1)} %collective-permute-done.13.refs_0_.refs_1_, bf16[2,384,768]{2,1,0:T(8,128)(2,1)} %collective-permute-done.14.refs_1_.refs_2_, bf16[2,4,384,512]{3,2,1,0:T(8,128)(2,1)S(1)} %copy-done, ...), custom_call_target="tpu_custom_call" | custom-call | flops 1207959552 | bytes 7864320 | tf_op jit(solution)/shard_map/step/pallas_call | solution.py:174
  93.7 16.2 %collective-permute-done.2.refs_1_.refs_2_ = bf16[2,384,768]{2,1,0:T(8,128)(2,1)} collective-permute-done((bf16[2,384,768]{2,1,0:T(8,128)(2,1)}, bf16[2,384,768]{2,1,0:T(8,128)(2,1)}, u32[]{:S(2)}, u32[]{:S(2)}) %collective-permute-start.2) | collective-permute-done | bytes 1179680 | tf_op jit(solution)/shard_map/ppermute | solution.py:427
  109.9 3.9 %step.6 = (bf16[2,384,768]{2,1,0:T(8,128)(2,1)}, bf16[2,384,768]{2,1,0:T(8,128)(2,1)}) custom-call(s32[34]{0:T(128)S(1)} %copy-done.18, bf16[2,384,768]{2,1,0:T(8,128)(2,1)} %collective-permute-done.1.refs_0_.refs_1_, bf16[2,384,768]{2,1,0:T(8,128)(2,1)} %collective-permute-done.2.refs_1_.refs_2_, bf16[2,4,384,512]{3,2,1,0:T(8,128)(2,1)S(1)} %copy-done, ...), custom_call_target="tpu_custom_call" | custom-call | flops 1207959552 | bytes 7864320 | tf_op jit(solution)/shard_map/step/pallas_call | solution.py:174
  119.8 4.6 %dispatch.3 = (bf16[2,4,384,512]{3,2,1,0:T(8,128)(2,1)}, f32[2,8,8,128]{3,2,1,0:T(8,128)}) custom-call(s32[34]{0:T(128)} %pad_add_fusion.sc, bf16[2,136,512]{2,1,0:T(8,128)(2,1)} %copy-done.20, bf16[2,136,512]{2,1,0:T(8,128)(2,1)} %copy-done.29, bf16[2,136,512]{2,1,0:T(8,128)(2,1)} %collective-permute-done.19.refs_2_, bf16[2,136,512]{2,1,0:T(8,128)(2,1)} %copy-done.31, ...), custom_call_target="tpu_custom_call" | custom-call | flops 402653184 | bytes 5373952 | tf_op jit(solution)/shard_map/dispatch/pallas_call | solution.py:115
  124.5 10.7 %collective-permute-done.16.refs_4_.refs_1_ = bf16[2,384,768]{2,1,0:T(8,128)(2,1)} collective-permute-done((bf16[2,384,768]{2,1,0:T(8,128)(2,1)}, bf16[2,384,768]{2,1,0:T(8,128)(2,1)}, u32[]{:S(2)}, u32[]{:S(2)}) %collective-permute-start.16) | collective-permute-done | bytes 1179680 | tf_op jit(solution)/shard_map/ppermute | solution.py:459
  139.0 4.2 %step.9 = (bf16[2,384,768]{2,1,0:T(8,128)(2,1)}, bf16[2,384,768]{2,1,0:T(8,128)(2,1)}) custom-call(s32[34]{0:T(128)S(1)} %copy-done.19, bf16[2,384,768]{2,1,0:T(8,128)(2,1)} %collective-permute-done.15.refs_3_.refs_0_, bf16[2,384,768]{2,1,0:T(8,128)(2,1)} %collective-permute-done.16.refs_4_.refs_1_, bf16[2,4,384,512]{3,2,1,0:T(8,128)(2,1)S(1)} %copy-done.5, ...), custom_call_target="tpu_custom_call" | custom-call | flops 1207959552 | bytes 7864320 | tf_op jit(solution)/shard_map/step/pallas_call | solution.py:174
  144.9 9.9 %shard_map.85 = (f32[512,3072]{1,0:T(8,128)}, f32[2,32,128]{2,1,0:T(8,128)S(1)}) custom-call(s32[34]{0:T(128)S(1)} %copy-done.19, bf16[4,384,768]{2,1,0:T(8,128)(2,1)S(1)} %bitcast.24, bf16[2,384,768]{2,1,0:T(8,128)(2,1)} %collective-permute-done.13.refs_0_.refs_1_, bf16[2,384,768]{2,1,0:T(8,128)(2,1)} %collective-permute-done.14.refs_1_.refs_2_, ...), custom_call_target="tpu_custom_call" | custom-call | flops 3019898880 | bytes 13762560 | tf_op jit(solution)/shard_map/pallas_call | solution.py:364
  154.8 5.7 %collective-permute-done.12.refs_1_.refs_4_ = bf16[2,384,768]{2,1,0:T(8,128)(2,1)} collective-permute-done((bf16[2,384,768]{2,1,0:T(8,128)(2,1)}, bf16[2,384,768]{2,1,0:T(8,128)(2,1)}, u32[]{:S(2)}, u32[]{:S(2)}) %collective-permute-start.12) | collective-permute-done | bytes 1179680 | tf_op jit(solution)/shard_map/ppermute | solution.py:459
  160.5 3.9 %step.8 = (bf16[2,384,768]{2,1,0:T(8,128)(2,1)}, bf16[2,384,768]{2,1,0:T(8,128)(2,1)}) custom-call(s32[34]{0:T(128)S(1)} %copy-done.19, bf16[2,384,768]{2,1,0:T(8,128)(2,1)} %collective-permute-done.11.refs_0_.refs_3_, bf16[2,384,768]{2,1,0:T(8,128)(2,1)} %collective-permute-done.12.refs_1_.refs_4_, bf16[2,4,384,512]{3,2,1,0:T(8,128)(2,1)S(1)} %copy-done.6, ...), custom_call_target="tpu_custom_call" | custom-call | flops 1207959552 | bytes 7864320 | tf_op jit(solution)/shard_map/step/pallas_call | solution.py:174
  166.2 5.2 %own_part.1 = bf16[4,384,768]{2,1,0:T(8,128)(2,1)} custom-call(bf16[2,4,384,512]{3,2,1,0:T(8,128)(2,1)} %get-tuple-element.62.refs_6_.refs_2_.refs_3_.rows_ref, bf16[512,3072]{1,0:T(8,128)(2,1)} %refs_4_.11), custom_call_target="tpu_custom_call" | custom-call | flops 1207959552 | bytes 7077888 | tf_op jit(solution)/shard_map/own_part/pallas_call | solution.py:253
  176.8 9.9 %shard_map.87 = (f32[512,3072]{1,0:T(8,128)}, f32[2,32,128]{2,1,0:T(8,128)S(1)}) custom-call(s32[34]{0:T(128)S(1)} %copy-done.19, bf16[4,384,768]{2,1,0:T(8,128)(2,1)S(1)} %bitcast.25, bf16[2,384,768]{2,1,0:T(8,128)(2,1)} %collective-permute-done.1.refs_0_.refs_1_, ...), custom_call_target="tpu_custom_call", output_to_operand_aliasing={{0}: (11, {})} | custom-call | flops 3019898880 | bytes 13762560 | tf_op jit(solution)/shard_map/pallas_call | solution.py:364
  186.7 4.2 %step.11 = (bf16[2,384,768]{2,1,0:T(8,128)(2,1)}, bf16[2,384,768]{2,1,0:T(8,128)(2,1)}) custom-call(s32[34]{0:T(128)S(1)} %copy-done.19, bf16[2,384,768]{2,1,0:T(8,128)(2,1)} %collective-permute-done.30.refs_0_, bf16[2,384,768]{2,1,0:T(8,128)(2,1)} %collective-permute-done.27.refs_0_.refs_1_, bf16[2,4,384,512]{3,2,1,0:T(8,128)(2,1)S(1)} %copy-done.1, ...), custom_call_target="tpu_custom_call" | custom-call | flops 1207959552 | bytes 7864320 | tf_op jit(solution)/shard_map/step/pallas_call | solution.py:174
  192.7 7.7 %collective-permute-start.32 = (bf16[2,384,768]{2,1,0:T(8,128)(2,1)}, bf16[2,384,768]{2,1,0:T(8,128)(2,1)}, u32[]{:S(2)}, u32[]{:S(2)}) collective-permute-start(bf16[2,384,768]{2,1,0:T(8,128)(2,1)} %get-tuple-element.84), channel_id=1, source_target_pairs={{0,1},{2,3},{1,0},{3,2},{4,5},{6,7},{5,4},{7,6},{8,9},{10,11},{9,8... | collective-permute-start | bytes 3538952 | tf_op jit(solution)/shard_map/ppermute | solution.py:459
  200.4 2.9 %shard_map.86 = f32[2,32,128]{2,1,0:T(8,128)S(1)} custom-call(s32[34]{0:T(128)S(1)} %copy-done.19, bf16[2,384,768]{2,1,0:T(8,128)(2,1)} %collective-permute-done.27.refs_0_.refs_1_, bf16[2,4,384,512]{3,2,1,0:T(8,128)(2,1)S(1)} %copy-done.1, bf16[2,4,384,512]{3,2,1,0:T(8,128)(2,1)S(1)} %copy-done.8, ...), custom_call_target="tpu_custom_call", output_to_operand_aliasing={{}: (7, {})} | custom-call | flops 1207959552 | bytes 10223616 | tf_op jit(solution)/shard_map/pallas_call | solution.py:364
  203.3 7.7 %collective-permute-done.26.refs_0_.refs_1_ = bf16[2,384,768]{2,1,0:T(8,128)(2,1)} collective-permute-done((bf16[2,384,768]{2,1,0:T(8,128)(2,1)}, bf16[2,384,768]{2,1,0:T(8,128)(2,1)}, u32[]{:S(2)}, u32[]{:S(2)}) %collective-permute-start.26) | collective-permute-done | bytes 1179680 | tf_op jit(solution)/shard_map/ppermute | solution.py:459
  211.0 2.9 %shard_map.88 = f32[2,32,128]{2,1,0:T(8,128)S(1)} custom-call(s32[34]{0:T(128)S(1)} %copy-done.19, bf16[2,384,768]{2,1,0:T(8,128)(2,1)} %collective-permute-done.26.refs_0_.refs_1_, bf16[2,4,384,512]{3,2,1,0:T(8,128)(2,1)S(1)} %copy-done.1, bf16[2,4,384,512]{3,2,1,0:T(8,128)(2,1)S(1)} %copy-done.8, ...), custom_call_target="tpu_custom_call", output_to_operand_aliasing={{}: (7, {})} | custom-call | flops 1207959552 | bytes 10223616 | tf_op jit(solution)/shard_map/pallas_call | solution.py:364
  214.0 3.9 %step.10 = (bf16[2,384,768]{2,1,0:T(8,128)(2,1)}, bf16[2,384,768]{2,1,0:T(8,128)(2,1)}) custom-call(s32[34]{0:T(128)S(1)} %copy-done.19, bf16[2,384,768]{2,1,0:T(8,128)(2,1)} %collective-permute-done.25.refs_0_, bf16[2,384,768]{2,1,0:T(8,128)(2,1)} %collective-permute-done.26.refs_0_.refs_1_, bf16[2,4,384,512]{3,2,1,0:T(8,128)(2,1)S(1)} %copy-done.1, ...), custom_call_target="tpu_custom_call" | custom-call | flops 1207959552 | bytes 7864320 | tf_op jit(solution)/shard_map/step/pallas_call | solution.py:174
  222.1 4.8 %shard_map.89.refs_3_ = f32[512,3072]{1,0:T(8,128)} custom-call(s32[34]{0:T(128)S(1)} %copy-done.19, bf16[2,384,768]{2,1,0:T(8,128)(2,1)} %collective-permute-done.27.refs_0_.refs_1_, bf16[2,4,384,512]{3,2,1,0:T(8,128)(2,1)S(1)} %copy-done.1, bf16[2,4,384,512]{3,2,1,0:T(8,128)(2,1)S(1)} %copy-done.9, ...), custom_call_target="tpu_custom_call", output_to_operand_aliasing={{}: (4, {})} | custom-call | flops 1207959552 | bytes 10223616 | tf_op jit(solution)/shard_map/pallas_call | solution.py:364
  227.5 3.9 %all-to-all-start = ((f32[32,4,128]{2,1,0:T(4,128)}), f32[32,4,128]{2,1,0:T(4,128)S(1)}, u32[]{:S(2)}, u32[]{:S(2)}) async-start(f32[32,4,128]{2,1,0:T(4,128)} %copy.18), calls=%async_computation | async-start | bytes 131072 | tf_op jit(solution)/shard_map/all_to_all | solution.py:457
  231.5 3.3 %fusion = (bf16[2,384,768]{2,1,0:T(8,128)(2,1)}, bf16[2,384,768]{2,1,0:T(8,128)(2,1)}) fusion(bf16[4,384,768]{2,1,0:T(8,128)(2,1)} %own_part.1), kind=kLoop, calls=%fused_computation.9 | loop fusion | bytes 4718592 | tf_op jit(solution)/shard_map/slice | solution.py:473
  234.8 4.8 %shard_map.90 = f32[512,3072]{1,0:T(8,128)} custom-call(s32[34]{0:T(128)S(1)} %copy-done.19, bf16[2,384,768]{2,1,0:T(8,128)(2,1)} %collective-permute-done.26.refs_0_.refs_1_, bf16[2,4,384,512]{3,2,1,0:T(8,128)(2,1)S(1)} %copy-done.1, bf16[2,4,384,512]{3,2,1,0:T(8,128)(2,1)S(1)} %copy-done.10, ...), custom_call_target="tpu_custom_call", output_to_operand_aliasing={{}: (4, {})} | custom-call | flops 1207959552 | bytes 10223616 | tf_op jit(solution)/shard_map/pallas_call | solution.py:364
  239.6 22.1 %all-to-all-done = f32[32,4,128]{2,1,0:T(4,128)S(1)} async-done(((f32[32,4,128]{2,1,0:T(4,128)}), f32[32,4,128]{2,1,0:T(4,128)S(1)}, u32[]{:S(2)}, u32[]{:S(2)}) %all-to-all-start) | async-done | bytes 65568 | tf_op jit(solution)/shard_map/all_to_all | solution.py:457
  263.8 2.6 last.2.rest_0_
  266.4 2.6 last.3
  (145 shorter events, 51.2 us)
Async XLA Ops:
  2.5 9.8 %collective-permute-start = (bf16[136,512]{1,0:T(8,128)(2,1)}, bf16[136,512]{1,0:T(8,128)(2,1)S(1)}, u32[]{:S(2)}, u32[]{:S(2)}) collective-permute-start(bf16[136,512]{1,0:T(8,128)(2,1)} %get-tuple-element.51), channel_id=1, source_target_pairs={{0,1},{1,2},{2,3},{3,0},{4,5},{5,6},{6,7},{7,4},{8,9},{9,10},{10,1... | collective-permute-start | bytes 417800 | tf_op jit(solution)/shard_map/ppermute | solution.py:418
  5.6 8.3 %collective-permute-start.3 = (bf16[136,512]{1,0:T(8,128)(2,1)}, bf16[136,512]{1,0:T(8,128)(2,1)S(1)}, u32[]{:S(2)}, u32[]{:S(2)}) collective-permute-start(bf16[136,512]{1,0:T(8,128)(2,1)} %get-tuple-element.54), channel_id=1, source_target_pairs={{0,3},{1,0},{2,1},{3,2},{4,7},{5,4},{6,5},{7,6},{8,11},{9,8},{10,9... | collective-permute-start | bytes 417800 | tf_op jit(solution)/shard_map/ppermute | solution.py:418
  14.0 41.5 %collective-permute-start.9 = (bf16[2,136,512]{2,1,0:T(8,128)(2,1)S(1)}, bf16[2,136,512]{2,1,0:T(8,128)(2,1)S(1)}, u32[]{:S(2)}, u32[]{:S(2)}) collective-permute-start(bf16[2,136,512]{2,1,0:T(8,128)(2,1)S(1)} %pad_maximum_fusion.refs_0_), channel_id=1, source_target_pairs={{0,24},{4,28},{8,16},{12,20},{16,8},{20,12},{24,0},{28,4},{1,25},{... | collective-permute-start | bytes 835592 | tf_op jit(solution)/shard_map/ppermute | solution.py:436
  16.5 39.1 %collective-permute-start.5 = (bf16[2,136,512]{2,1,0:T(8,128)(2,1)S(1)}, bf16[2,136,512]{2,1,0:T(8,128)(2,1)S(1)}, u32[]{:S(2)}, u32[]{:S(2)}) collective-permute-start(bf16[2,136,512]{2,1,0:T(8,128)(2,1)S(1)} %pad_maximum_fusion.refs_0_), channel_id=1, source_target_pairs={{0,8},{4,12},{8,0},{12,4},{16,24},{20,28},{24,16},{28,20},{1,9},{5... | collective-permute-start | bytes 835592 | tf_op jit(solution)/shard_map/ppermute | solution.py:436
  19.4 45.5 %collective-permute-start.13 = (bf16[2,384,768]{2,1,0:T(8,128)(2,1)}, bf16[2,384,768]{2,1,0:T(8,128)(2,1)}, u32[]{:S(2)}, u32[]{:S(2)}) collective-permute-start(bf16[2,384,768]{2,1,0:T(8,128)(2,1)} %slice.13), channel_id=1, source_target_pairs={{1,2},{2,1},{5,6},{6,5},{9,10},{10,9},{13,14},{14,13},{17,18},{18,... | collective-permute-start | bytes 3538952 | tf_op jit(solution)/shard_map/ppermute | solution.py:427
  21.2 34.3 %collective-permute-start.17 = (bf16[136,512]{1,0:T(8,128)(2,1)S(1)}, bf16[136,512]{1,0:T(8,128)(2,1)S(1)}, u32[]{:S(2)}, u32[]{:S(2)}) collective-permute-start(bf16[136,512]{1,0:T(8,128)(2,1)S(1)} %copy-done.37), channel_id=1, source_target_pairs={{0,2},{1,3},{2,0},{3,1},{4,6},{5,7},{6,4},{7,5},{8,10},{9,11},{10,... | collective-permute-start | bytes 417800 | tf_op jit(solution)/shard_map/ppermute | solution.py:418
  24.1 33.1 %collective-permute-start.7 = (bf16[2,136,512]{2,1,0:T(8,128)(2,1)S(1)}, bf16[2,136,512]{2,1,0:T(8,128)(2,1)S(1)}, u32[]{:S(2)}, u32[]{:S(2)}) collective-permute-start(bf16[2,136,512]{2,1,0:T(8,128)(2,1)S(1)} %pad_maximum_fusion.refs_0_), channel_id=1, source_target_pairs={{0,16},{4,20},{8,24},{12,28},{16,0},{20,4},{24,8},{28,12},{1,17},{... | collective-permute-start | bytes 835592 | tf_op jit(solution)/shard_map/ppermute | solution.py:436
  55.5 29.2 %collective-permute-start.14 = (bf16[2,384,768]{2,1,0:T(8,128)(2,1)}, bf16[2,384,768]{2,1,0:T(8,128)(2,1)}, u32[]{:S(2)}, u32[]{:S(2)}) collective-permute-start(bf16[2,384,768]{2,1,0:T(8,128)(2,1)} %slice.13), channel_id=1, source_target_pairs={{0,1},{2,3},{1,0},{3,2},{4,5},{6,7},{5,4},{7,6},{8,9},{10,11},{9,8... | collective-permute-start | bytes 3538952 | tf_op jit(solution)/shard_map/ppermute | solution.py:427
  55.5 3.5 %collective-permute-start.4 = (bf16[2,136,512]{2,1,0:T(8,128)(2,1)S(1)}, bf16[2,136,512]{2,1,0:T(8,128)(2,1)S(1)}, u32[]{:S(2)}, u32[]{:S(2)}) collective-permute-start(bf16[2,136,512]{2,1,0:T(8,128)(2,1)S(1)} %pad_maximum_fusion.refs_0_), channel_id=1, source_target_pairs={{0,4},{4,0},{8,12},{12,8},{16,20},{20,16},{24,28},{28,24},{1,5},{5... | collective-permute-start | bytes 835592 | tf_op jit(solution)/shard_map/ppermute | solution.py:438
  55.6 3.5 %collective-permute-start.10 = (bf16[2,136,512]{2,1,0:T(8,128)(2,1)S(1)}, bf16[2,136,512]{2,1,0:T(8,128)(2,1)S(1)}, u32[]{:S(2)}, u32[]{:S(2)}) collective-permute-start(bf16[2,136,512]{2,1,0:T(8,128)(2,1)S(1)} %collective-permute-done.9.refs_6_), channel_id=1, source_target_pairs={{0,4},{4,0},{8,12},{12,8},{16,20},{20,16},{24,28},{28,24},{1,5},{5... | collective-permute-start | bytes 835592 | tf_op jit(solution)/shard_map/ppermute | solution.py:438
  57.2 36.5 %collective-permute-start.1 = (bf16[2,384,768]{2,1,0:T(8,128)(2,1)}, bf16[2,384,768]{2,1,0:T(8,128)(2,1)}, u32[]{:S(2)}, u32[]{:S(2)}) collective-permute-start(bf16[2,384,768]{2,1,0:T(8,128)(2,1)} %slice.12), channel_id=1, source_target_pairs={{1,2},{2,1},{5,6},{6,5},{9,10},{10,9},{13,14},{14,13},{17,18},{18,... | collective-permute-start | bytes 3538952 | tf_op jit(solution)/shard_map/ppermute | solution.py:427
  59.1 2.7 collective-permute-start.6
  59.2 50.8 %collective-permute-start.2 = (bf16[2,384,768]{2,1,0:T(8,128)(2,1)}, bf16[2,384,768]{2,1,0:T(8,128)(2,1)}, u32[]{:S(2)}, u32[]{:S(2)}) collective-permute-start(bf16[2,384,768]{2,1,0:T(8,128)(2,1)} %slice.12), channel_id=1, source_target_pairs={{0,1},{2,3},{1,0},{3,2},{4,5},{6,7},{5,4},{7,6},{8,9},{10,11},{9,8... | collective-permute-start | bytes 3538952 | tf_op jit(solution)/shard_map/ppermute | solution.py:427
  63.3 28.9 %collective-permute-start.19 = (bf16[2,136,512]{2,1,0:T(8,128)(2,1)S(1)}, bf16[2,136,512]{2,1,0:T(8,128)(2,1)}, u32[]{:S(2)}, u32[]{:S(2)}) collective-permute-start(bf16[2,136,512]{2,1,0:T(8,128)(2,1)S(1)} %pad_maximum_fusion.1.refs_0_), channel_id=1, source_target_pairs={{0,8},{4,12},{8,0},{12,4},{16,24},{20,28},{24,16},{28,20},{1,9},{5... | collective-permute-start | bytes 835592 | tf_op jit(solution)/shard_map/ppermute | solution.py:436
  64.9 27.3 %collective-permute-start.21 = (bf16[2,136,512]{2,1,0:T(8,128)(2,1)S(1)}, bf16[2,136,512]{2,1,0:T(8,128)(2,1)}, u32[]{:S(2)}, u32[]{:S(2)}) collective-permute-start(bf16[2,136,512]{2,1,0:T(8,128)(2,1)S(1)} %pad_maximum_fusion.1.refs_0_), channel_id=1, source_target_pairs={{0,16},{4,20},{8,24},{12,28},{16,0},{20,4},{24,8},{28,12},{1,17},{... | collective-permute-start | bytes 835592 | tf_op jit(solution)/shard_map/ppermute | solution.py:436
  90.5 34.0 %collective-permute-start.15 = (bf16[2,384,768]{2,1,0:T(8,128)(2,1)}, bf16[2,384,768]{2,1,0:T(8,128)(2,1)}, u32[]{:S(2)}, u32[]{:S(2)}) collective-permute-start(bf16[2,384,768]{2,1,0:T(8,128)(2,1)} %get-tuple-element.58), channel_id=1, source_target_pairs={{1,2},{2,1},{5,6},{6,5},{9,10},{10,9},{13,14},{14,13},{17,18},{18,... | collective-permute-start | bytes 3538952 | tf_op jit(solution)/shard_map/ppermute | solution.py:460
  92.2 43.0 %collective-permute-start.16 = (bf16[2,384,768]{2,1,0:T(8,128)(2,1)}, bf16[2,384,768]{2,1,0:T(8,128)(2,1)}, u32[]{:S(2)}, u32[]{:S(2)}) collective-permute-start(bf16[2,384,768]{2,1,0:T(8,128)(2,1)} %get-tuple-element.59), channel_id=1, source_target_pairs={{0,1},{2,3},{1,0},{3,2},{4,5},{6,7},{5,4},{7,6},{8,9},{10,11},{9,8... | collective-permute-start | bytes 3538952 | tf_op jit(solution)/shard_map/ppermute | solution.py:459
  92.2 21.6 %collective-permute-start.23 = (bf16[2,136,512]{2,1,0:T(8,128)(2,1)S(1)}, bf16[2,136,512]{2,1,0:T(8,128)(2,1)S(1)}, u32[]{:S(2)}, u32[]{:S(2)}) collective-permute-start(bf16[2,136,512]{2,1,0:T(8,128)(2,1)S(1)} %pad_maximum_fusion.1.refs_0_), channel_id=1, source_target_pairs={{0,24},{4,28},{8,16},{12,20},{16,8},{20,12},{24,0},{28,4},{1,25},{... | collective-permute-start | bytes 835592 | tf_op jit(solution)/shard_map/ppermute | solution.py:436
  93.7 21.8 %collective-permute-start.18 = (bf16[2,136,512]{2,1,0:T(8,128)(2,1)S(1)}, bf16[2,136,512]{2,1,0:T(8,128)(2,1)S(1)}, u32[]{:S(2)}, u32[]{:S(2)}) collective-permute-start(bf16[2,136,512]{2,1,0:T(8,128)(2,1)S(1)} %pad_maximum_fusion.1.refs_0_), channel_id=1, source_target_pairs={{0,4},{4,0},{8,12},{12,8},{16,20},{20,16},{24,28},{28,24},{1,5},{5... | collective-permute-start | bytes 835592 | tf_op jit(solution)/shard_map/ppermute | solution.py:438
  109.9 5.6 %collective-permute-start.20 = (bf16[2,136,512]{2,1,0:T(8,128)(2,1)}, bf16[2,136,512]{2,1,0:T(8,128)(2,1)S(1)}, u32[]{:S(2)}, u32[]{:S(2)}) collective-permute-start(bf16[2,136,512]{2,1,0:T(8,128)(2,1)} %collective-permute-done.19.refs_2_), channel_id=1, source_target_pairs={{0,4},{4,0},{8,12},{12,8},{16,20},{20,16},{24,28},{28,24},{1,5},{5... | collective-permute-start | bytes 835592 | tf_op jit(solution)/shard_map/ppermute | solution.py:438
  113.9 40.9 %collective-permute-start.11 = (bf16[2,384,768]{2,1,0:T(8,128)(2,1)}, bf16[2,384,768]{2,1,0:T(8,128)(2,1)}, u32[]{:S(2)}, u32[]{:S(2)}) collective-permute-start(bf16[2,384,768]{2,1,0:T(8,128)(2,1)} %get-tuple-element.56), channel_id=1, source_target_pairs={{1,2},{2,1},{5,6},{6,5},{9,10},{10,9},{13,14},{14,13},{17,18},{18,... | collective-permute-start | bytes 3538952 | tf_op jit(solution)/shard_map/ppermute | solution.py:460
  115.6 44.9 %collective-permute-start.12 = (bf16[2,384,768]{2,1,0:T(8,128)(2,1)}, bf16[2,384,768]{2,1,0:T(8,128)(2,1)}, u32[]{:S(2)}, u32[]{:S(2)}) collective-permute-start(bf16[2,384,768]{2,1,0:T(8,128)(2,1)} %get-tuple-element.57), channel_id=1, source_target_pairs={{0,1},{2,3},{1,0},{3,2},{4,5},{6,7},{5,4},{7,6},{8,9},{10,11},{9,8... | collective-permute-start | bytes 3538952 | tf_op jit(solution)/shard_map/ppermute | solution.py:459
  115.6 2.0 collective-permute-start.22
  143.2 43.4 %collective-permute-start.27 = (bf16[2,384,768]{2,1,0:T(8,128)(2,1)}, bf16[2,384,768]{2,1,0:T(8,128)(2,1)}, u32[]{:S(2)}, u32[]{:S(2)}) collective-permute-start(bf16[2,384,768]{2,1,0:T(8,128)(2,1)} %get-tuple-element.70), channel_id=1, source_target_pairs={{0,1},{2,3},{1,0},{3,2},{4,5},{6,7},{5,4},{7,6},{8,9},{10,11},{9,8... | collective-permute-start | bytes 3538952 | tf_op jit(solution)/shard_map/ppermute | solution.py:459
  143.2 43.4 %collective-permute-start.30 = (bf16[2,384,768]{2,1,0:T(8,128)(2,1)}, bf16[2,384,768]{2,1,0:T(8,128)(2,1)}, u32[]{:S(2)}, u32[]{:S(2)}) collective-permute-start(bf16[2,384,768]{2,1,0:T(8,128)(2,1)} %get-tuple-element.79), channel_id=1, source_target_pairs={{1,2},{2,1},{5,6},{6,5},{9,10},{10,9},{13,14},{14,13},{17,18},{18,... | collective-permute-start | bytes 3538952 | tf_op jit(solution)/shard_map/ppermute | solution.py:460
  164.4 46.6 %collective-permute-start.26 = (bf16[2,384,768]{2,1,0:T(8,128)(2,1)}, bf16[2,384,768]{2,1,0:T(8,128)(2,1)}, u32[]{:S(2)}, u32[]{:S(2)}) collective-permute-start(bf16[2,384,768]{2,1,0:T(8,128)(2,1)} %get-tuple-element.69), channel_id=1, source_target_pairs={{0,1},{2,3},{1,0},{3,2},{4,5},{6,7},{5,4},{7,6},{8,9},{10,11},{9,8... | collective-permute-start | bytes 3538952 | tf_op jit(solution)/shard_map/ppermute | solution.py:459
  164.4 49.6 %collective-permute-start.25 = (bf16[2,384,768]{2,1,0:T(8,128)(2,1)}, bf16[2,384,768]{2,1,0:T(8,128)(2,1)}, u32[]{:S(2)}, u32[]{:S(2)}) collective-permute-start(bf16[2,384,768]{2,1,0:T(8,128)(2,1)} %get-tuple-element.68), channel_id=1, source_target_pairs={{1,2},{2,1},{5,6},{6,5},{9,10},{10,9},{13,14},{14,13},{17,18},{18,... | collective-permute-start | bytes 3538952 | tf_op jit(solution)/shard_map/ppermute | solution.py:460
  190.9 71.5 %collective-permute-start.31 = (bf16[2,384,768]{2,1,0:T(8,128)(2,1)}, bf16[2,384,768]{2,1,0:T(8,128)(2,1)}, u32[]{:S(2)}, u32[]{:S(2)}) collective-permute-start(bf16[2,384,768]{2,1,0:T(8,128)(2,1)} %get-tuple-element.83), channel_id=1, source_target_pairs={{1,2},{2,1},{5,6},{6,5},{9,10},{10,9},{13,14},{14,13},{17,18},{18,... | collective-permute-start | bytes 3538952 | tf_op jit(solution)/shard_map/ppermute | solution.py:460
  192.7 69.7 %collective-permute-start.32 = (bf16[2,384,768]{2,1,0:T(8,128)(2,1)}, bf16[2,384,768]{2,1,0:T(8,128)(2,1)}, u32[]{:S(2)}, u32[]{:S(2)}) collective-permute-start(bf16[2,384,768]{2,1,0:T(8,128)(2,1)} %get-tuple-element.84), channel_id=1, source_target_pairs={{0,1},{2,3},{1,0},{3,2},{4,5},{6,7},{5,4},{7,6},{8,9},{10,11},{9,8... | collective-permute-start | bytes 3538952 | tf_op jit(solution)/shard_map/ppermute | solution.py:459
  218.0 48.4 %collective-permute-start.28 = (bf16[2,384,768]{2,1,0:T(8,128)(2,1)}, bf16[2,384,768]{2,1,0:T(8,128)(2,1)}, u32[]{:S(2)}, u32[]{:S(2)}) collective-permute-start(bf16[2,384,768]{2,1,0:T(8,128)(2,1)} %get-tuple-element.76), channel_id=1, source_target_pairs={{1,2},{2,1},{5,6},{6,5},{9,10},{10,9},{13,14},{14,13},{17,18},{18,... | collective-permute-start | bytes 3538952 | tf_op jit(solution)/shard_map/ppermute | solution.py:460
  219.7 46.7 %collective-permute-start.29 = (bf16[2,384,768]{2,1,0:T(8,128)(2,1)}, bf16[2,384,768]{2,1,0:T(8,128)(2,1)}, u32[]{:S(2)}, u32[]{:S(2)}) collective-permute-start(bf16[2,384,768]{2,1,0:T(8,128)(2,1)} %get-tuple-element.77), channel_id=1, source_target_pairs={{0,1},{2,3},{1,0},{3,2},{4,5},{6,7},{5,4},{7,6},{8,9},{10,11},{9,8... | collective-permute-start | bytes 3538952 | tf_op jit(solution)/shard_map/ppermute | solution.py:459
  227.5 34.2 %all-to-all-start = ((f32[32,4,128]{2,1,0:T(4,128)}), f32[32,4,128]{2,1,0:T(4,128)S(1)}, u32[]{:S(2)}, u32[]{:S(2)}) async-start(f32[32,4,128]{2,1,0:T(4,128)} %copy.18), calls=%async_computation | async-start | bytes 131072 | tf_op jit(solution)/shard_map/all_to_all | solution.py:457
  (41 other events, 392.8 us)
